TPU v7x, 128 devices: a whole 4x4x4 slice. The times are simulated.
128 devices in a mesh: lon: 32 (over z, y, x_lo), lat: 4 (over x_hi, core).
Axes of the slice: x: 4 (x_hi: 2, x_lo: 2; x = x_hi * 2 + x_lo), y: 4, z: 4, core: 2. Of those that a mesh axis runs over, the one named last changes fastest.
Arguments:
- points: bfloat16 [256, 69, 5216], P('lat', None, 'lon'), may hold values from -6 to 6
- row_len: int32 [256], P('lat'), may hold values from 20 to 5136, as said below
- w_embed: bfloat16 [69, 256], replicated, may hold values from -0.75 to 0.75
- kernel1: bfloat16 [25, 256], replicated, may hold values from -1.1953125 to 1.1953125
- gain1: float32 [256], replicated, may hold values from 0.5 to 1.5
- point1: bfloat16 [256, 256], replicated, may hold values from -0.375 to 0.375
- kernel2: bfloat16 [25, 256], replicated, may hold values from -1.1953125 to 1.1953125
- gain2: float32 [256], replicated, may hold values from 0.5 to 1.5
- point2: bfloat16 [256, 256], replicated, may hold values from -0.375 to 0.375
- cotangent: bfloat16 [256, 768, 256], P('lat', 'lon'), may hold values from -6 to 6
Outputs:
- out: bfloat16 [256, 768, 256], P('lat', 'lon')
- grad_embed: float32 [69, 256], replicated
- grad_kernel1: float32 [25, 256], replicated
- grad_kernel2: float32 [25, 256], replicated
- grad_point1: float32 [256, 256], replicated
- grad_point2: float32 [256, 256], replicated
- grad_gain1: float32 [256], replicated
- grad_gain2: float32 [256], replicated
Inputs may be any that keep to these rules, and one draw needn't show every extreme that they name: `row_len`: every row holds 20 plus a multiple of 4 points; some row holds exactly 5136.
All inputs are finite; a program needn't handle non-finite values.
Results may differ from a plain program's by a relative error of at most 0.012.
Values may be sent and summed in bfloat16 or wider, within the bound.
No kernel may reach another device: no remote copies, remote signals or barrier semaphores. Data moves between devices by JAX's collectives and lax.ppermute only.
A program may use at most 128 MiB of HBM per device.

v0:
```python
import jax
import jax.numpy as jnp
from jax import lax
from jax.sharding import PartitionSpec as P


def with_halo(array, sides, width, wrap):
    for axis, dim in sides:
        devices, length = (lax.axis_size(axis), array.shape[dim])
        up = [(i, (i + 1) % devices) for i in range(devices if wrap else devices - 1)]
        down = [(j, i) for i, j in up]
        last = lax.slice_in_dim(array, length - width, length, axis=dim)
        initial = lax.slice_in_dim(array, 0, width, axis=dim)
        before = lax.ppermute(last, axis, up)
        after = lax.ppermute(initial, axis, down)
        array = jnp.concatenate([before, array, after], axis=dim)
    return array


def together(arrays, axis):
    ends = [0]
    for a in arrays:
        ends.append(ends[-1] + a.size)
    total = lax.psum(jnp.concatenate([a.ravel() for a in arrays]), axis)
    return tuple((total[b:e].reshape(a.shape) for a, b, e in zip(arrays, ends, ends[1:])))


def regrid(points, lengths, first_sector, lon_dev, lon_total):
    nrows, nvars, nsec, slots = points.shape
    sector = jnp.arange(nsec, dtype=jnp.int32) + first_sector
    cell = sector[:, None] * lon_dev + jnp.arange(lon_dev, dtype=jnp.int32)[None, :]
    count = lengths[:, None, None]
    product = cell[None] * count
    lower = product // lon_total
    start = sector[None, :, None] * lon_dev * count // lon_total
    frac = (product - lower * lon_total).astype(jnp.float32) / lon_total
    offset = (lower - start)[..., None]
    marks = jnp.arange(slots, dtype=jnp.int32)
    weights = jnp.where(marks == offset, 1.0 - frac[..., None], 0.0) + jnp.where(
        marks == offset + 1, frac[..., None], 0.0
    )
    result = jnp.einsum(
        "rvsm,rsjm->rvsj", points.astype(jnp.float32), weights, precision=lax.Precision.HIGHEST
    )
    return result.reshape(nrows, nvars, nsec * lon_dev)


def embed(regridded, w_embed):
    return jnp.einsum(
        "rvj,vc->rjc", regridded, w_embed.astype(jnp.float32), precision=lax.Precision.HIGHEST
    ).astype(jnp.bfloat16)


def depthwise(padded, kernel):
    nrows = padded.shape[0] - 4
    ncols = padded.shape[1] - 4
    taps = kernel.astype(jnp.float32)
    wide = padded.astype(jnp.float32)
    total = jnp.zeros((nrows, ncols, padded.shape[2]), jnp.float32)
    for first in range(5):
        for second in range(5):
            total = (
                total
                + wide[first : first + nrows, second : second + ncols] * taps[5 * first + second]
            )
    return total


def mix_forward(conv, gain, point):
    scale = lax.rsqrt(jnp.mean(conv * conv, -1, keepdims=True) + 1e-06)
    normed = (conv * scale * gain).astype(jnp.bfloat16)
    mixed = jnp.dot(normed, point, preferred_element_type=jnp.float32)
    return (normed, scale, mixed)


def residual(inputs, mixed):
    return (inputs.astype(jnp.float32) + jax.nn.silu(mixed)).astype(jnp.bfloat16)


def mix_backward(upstream, conv, scale, normed, mixed, gain, point):
    chans = normed.shape[-1]
    sig = jax.nn.sigmoid(mixed)
    dmixed = (upstream * sig * (1.0 + mixed * (1.0 - sig))).astype(jnp.bfloat16)
    dpoint = jnp.dot(
        normed.reshape(-1, chans).T, dmixed.reshape(-1, chans), preferred_element_type=jnp.float32
    )
    dnormed = jnp.dot(dmixed, point.T, preferred_element_type=jnp.float32)
    dgain = jnp.sum((dnormed * conv * scale).reshape(-1, chans), 0)
    gained = gain * dnormed
    dconv = scale * gained - conv * scale**3 * jnp.mean(gained * conv, -1, keepdims=True)
    return (dpoint, dgain, dconv.astype(jnp.bfloat16))


def kernel_grad(padded, dconv):
    nrows, ncols, chans = dconv.shape
    wide = padded.astype(jnp.float32)
    back = dconv.astype(jnp.float32)
    pieces = []
    for first in range(5):
        for second in range(5):
            pieces.append(
                jnp.sum(
                    (wide[first : first + nrows, second : second + ncols] * back).reshape(
                        -1, chans
                    ),
                    0,
                )
            )
    return jnp.stack(pieces)


def extend(field):
    beside_all = with_halo(field, (("lon", 1),), 2, True)
    return with_halo(beside_all, (("lat", 0),), 2, False)


def on_device(points, row_len, w_embed, kernel1, gain1, point1, kernel2, gain2, point2, cotangent):
    nrows, nvars, slots = points.shape
    lon_dev = cotangent.shape[1]
    lon_total = lon_dev * lax.axis_size("lon")
    rows_total = nrows * lax.axis_size("lat")
    regridded = regrid(
        points.reshape(nrows, nvars, 1, slots), row_len, lax.axis_index("lon"), lon_dev, lon_total
    )
    h0 = embed(regridded, w_embed)
    wide = with_halo(h0, (("lon", 1),), 4, True)
    wide = with_halo(wide, (("lat", 0),), 4, False)
    conv_wide = depthwise(wide, kernel1)
    normed_wide, scale_wide, mixed_wide = mix_forward(conv_wide, gain1, point1)
    h1_wide = residual(wide[2:-2, 2:-2], mixed_wide)
    row_ids = lax.axis_index("lat") * nrows - 2 + jnp.arange(nrows + 4, dtype=jnp.int32)
    inside = (row_ids >= 0) & (row_ids < rows_total)
    h1_wide = jnp.where(inside[:, None, None], h1_wide, jnp.zeros_like(h1_wide))
    pad1 = wide[2:-2, 2:-2]
    conv1 = conv_wide[2:-2, 2:-2]
    normed1 = normed_wide[2:-2, 2:-2]
    scale1 = scale_wide[2:-2, 2:-2]
    mixed1 = mixed_wide[2:-2, 2:-2]
    h1 = h1_wide[2:-2, 2:-2]
    conv2 = depthwise(h1_wide, kernel2)
    normed2, scale2, mixed2 = mix_forward(conv2, gain2, point2)
    out = residual(h1, mixed2)
    upstream = cotangent.astype(jnp.float32)
    dpoint2, dgain2, dconv2 = mix_backward(upstream, conv2, scale2, normed2, mixed2, gain2, point2)
    dkernel2 = kernel_grad(h1_wide, dconv2)
    grad1 = upstream + depthwise(extend(dconv2), kernel2[::-1])
    dpoint1, dgain1, dconv1 = mix_backward(grad1, conv1, scale1, normed1, mixed1, gain1, point1)
    dkernel1 = kernel_grad(pad1, dconv1)
    grad0 = grad1 + depthwise(extend(dconv1), kernel1[::-1])
    dembed = jnp.einsum("rvj,rjc->vc", regridded, grad0, precision=lax.Precision.HIGHEST)
    dembed, dkernel1, dkernel2, dpoint1, dpoint2, dgain1, dgain2 = together(
        (dembed, dkernel1, dkernel2, dpoint1, dpoint2, dgain1, dgain2), ("lon", "lat")
    )
    factor = float(rows_total * lon_total) ** (-0.5)
    return (
        out,
        dembed * factor,
        dkernel1 * factor,
        dkernel2 * factor,
        dpoint1 * factor,
        dpoint2 * factor,
        dgain1 * factor,
        dgain2 * factor,
    )


def solution(mesh):
    in_specs = (
        P("lat", None, "lon"),
        P("lat"),
        P(),
        P(),
        P(),
        P(),
        P(),
        P(),
        P(),
        P("lat", "lon", None),
    )
    out_specs = (P("lat", "lon", None), P(), P(), P(), P(), P(), P(), P())
    return jax.shard_map(
        on_device, mesh=mesh, in_specs=in_specs, out_specs=out_specs, check_vma=False
    )
```

profile of v0, /device:TPU:1, one launch (start us, length us, event | category | flops | bytes accessed | tf_op | source)
XLA Modules:
  0.0 351.4 jit_solution(10926215966860628693)
XLA Ops:
  7.2 0.8 and_select_fusion
  8.1 0.8 broadcast_subtract_fusion
  8.8 0.8 broadcast_subtract_fusion.1
  9.6 4.7 %fusion.155 = f32[64,69,24]{1,2,0:T(8,128)S(1)} fusion(bf16[64,69,163]{2,0,1:T(8,128)(2,1)S(1)} %copy-done, f32[64,24]{1,0:T(8,128)S(1)} %get-tuple-element.204, s32[64,24]{1,0:T(8,128)S(1)} %get-tuple-element.202, f32[64,24]{1,0:T(8,128)S(1)} %get-tuple-element.203, s32[64,24]{1,0:T(8,128)S(1)} %get-tuple-element.201), kind=kOutput, calls=%fused_computation.276 | convolution fusion | flops 208556544 | bytes 1888128 | tf_op jit(solution)/shard_map/rvsm,rsjm->rvsj/dot_general | solution.py:42
  14.3 0.9 copy-done.12
  15.2 0.8 convolution_convert_fusion
  15.9 0.8 fusion.217
  16.7 2.0 collective-permute-start
  18.7 5.9 %collective-permute-start.1 = (bf16[64,4,256]{2,1,0:T(4,128)(2,1)S(1)}, bf16[64,4,256]{2,1,0:T(4,128)(2,1)S(1)}, u32[]{:S(2)}, u32[]{:S(2)}) collective-permute-start(bf16[64,4,256]{2,1,0:T(4,128)(2,1)S(1)} %get-tuple-element.88), channel_id=1, source_target_pairs={{4,0},{8,4},{12,8},{16,12},{20,16},{24,20},{28,24},{32,28},{36,32}... | collective-permute-start | bytes 393224 | tf_op jit(solution)/shard_map/ppermute | solution.py:15
  25.4 0.7 fusion.218
  26.2 0.7 fusion.224
  26.8 0.7 fusion.222
  27.5 0.6 fusion.220
  28.8 5.7 %collective-permute-start.2 = (bf16[4,32,256]{2,1,0:T(8,128)(2,1)S(1)}, bf16[4,32,256]{2,1,0:T(8,128)(2,1)S(1)}, u32[]{:S(2)}, u32[]{:S(2)}) collective-permute-start(bf16[4,32,256]{2,1,0:T(8,128)(2,1)S(1)} %get-tuple-element.77), channel_id=1, source_target_pairs={{0,1},{1,2},{2,3},{4,5},{5,6},{6,7},{8,9},{9,10},{10,11},{12,13},{... | collective-permute-start | bytes 196616 | tf_op jit(solution)/shard_map/ppermute | solution.py:14
  34.5 2.1 collective-permute-start.3
  36.8 4.7 %collective-permute-done.3 = bf16[4,32,256]{2,1,0:T(8,128)(2,1)S(1)} collective-permute-done((bf16[4,32,256]{2,1,0:T(8,128)(2,1)S(1)}, bf16[4,32,256]{2,1,0:T(8,128)(2,1)S(1)}, u32[]{:S(2)}, u32[]{:S(2)}) %collective-permute-start.3) | collective-permute-done | bytes 65568 | tf_op jit(solution)/shard_map/ppermute | solution.py:15
  42.3 7.0 %multiply_reduce_fusion = (f32[68,28]{1,0:T(8,128)S(1)}, f32[68,28,256]{2,1,0:T(8,128)S(1)}) fusion(f32[256]{0:T(256)S(1)} %bitcast.285, f32[72,32,256]{2,1,0:T(8,128)S(1)} %get-tuple-element.76, f32[256]{0:T(256)S(1)} %bitcast.284, f32[256]{0:T(256)S(1)} %bitcast.283, f32[256]{0:T(256)S(1)} %bitcast.282, f32[256]{0:T(256)S(1)} %bitcast.281, ...), kind=kLoop, calls=%fused_computation.103 | loop fusion | flops 24856720 | bytes 50725312 | tf_op jit(solution)/shard_map/reduce_sum | solution.py:70
  49.8 1.0 copy-done.4
  50.7 1.2 fusion.163
  52.1 3.2 fusion.213
  55.5 6.1 %multiply_reduce_fusion.5 = (f32[64,24]{1,0:T(8,128)S(1)}, f32[64,24,256]{2,1,0:T(8,128)}) fusion(f32[256]{0:T(256)S(1)} %bitcast.279, f32[68,28,256]{2,1,0:T(8,128)S(1)} %get-tuple-element.68, f32[256]{0:T(256)S(1)} %bitcast.278, f32[256]{0:T(256)S(1)} %bitcast.277, f32[256]{0:T(256)S(1)} %bitcast.276, f32[256]{0:T(256)S(1)} %bitcast.275, ...), kind=kLoop, calls=%fused_computation.268 | loop fusion | flops 20052480 | bytes 40926208 | tf_op jit(solution)/shard_map/reduce_sum | solution.py:70
  61.7 4.1 %fusion.27 = (bf16[64,24,256]{2,1,0:T(8,128)(2,1)S(1)}, bf16[64,24,256]{2,1,0:T(8,128)(2,1)}) fusion(bf16[64,24,256]{2,1,0:T(8,128)(2,1)} %param.19, bf16[68,28,256]{2,1,0:T(8,128)(2,1)} %get-tuple-element.69, bf16[256,256]{1,0:T(8,128)(2,1)S(1)} %copy-done.15, f32[64,24,256]{2,1,0:T(8,128)} %get-tuple-element.67, f32[256]{0:T(256)S(1)} %copy-done.30, ...), kind=kOutput, calls=%fused_computation.107 | convolution fusion | flops 208011264 | bytes 4856832 | tf_op jit(solution)/shard_map/dot_general | solution.py:72
  65.7 1.3 multiply_reduce_fusion.1
  67.0 4.8 %fusion.77 = (f32[256]{0:T(256)}, f32[256]{0:T(256)}, f32[256]{0:T(256)}, f32[256]{0:T(256)}, f32[256]{0:T(256)}, /*index=5*/f32[256]{0:T(256)}, f32[256]{0:T(25...) fusion(f32[68,28,256]{2,1,0:T(8,128)S(1)} %get-tuple-element.68, ...), kind=kLoop, calls=%fused_computation.157 | loop fusion | flops 16903680 | bytes 32281600 | tf_op jit(solution)/shard_map/reduce_sum | solution.py:102
  71.8 1.8 fusion.76
  74.0 5.7 %collective-permute-start.5 = (bf16[64,2,256]{2,1,0:T(2,128)(2,1)S(1)}, bf16[64,2,256]{2,1,0:T(2,128)(2,1)S(1)}, u32[]{:S(2)}, u32[]{:S(2)}) collective-permute-start(bf16[64,2,256]{2,1,0:T(2,128)(2,1)S(1)} %get-tuple-element.86), channel_id=1, source_target_pairs={{4,0},{8,4},{12,8},{16,12},{20,16},{24,20},{28,24},{32,28},{36,32}... | collective-permute-start | bytes 196616 | tf_op jit(solution)/shard_map/ppermute | solution.py:15
  79.7 0.7 convolution_bitcast_fusion
  80.4 1.0 collective-permute-done.4
  81.3 0.7 pad_maximum_fusion.9
  82.0 3.0 collective-permute-start.6
  85.0 1.9 collective-permute-start.7
  87.0 2.0 copy.21
  89.2 2.9 stack.207
  92.1 0.6 reshape.504
  92.8 2.7 maximum_convert_fusion
  95.5 26.1 %multiply_convert_fusion.1 = (bf16[64,24,256]{2,1,0:T(8,128)(2,1)S(1)}, f32[64,24,256]{2,1,0:T(8,128)}) fusion(f32[68,28,256]{2,1,0:T(8,128)} %copy.21, f32[256]{0:T(256)} %bitcast.223, f32[68,28,256]{2,1,0:T(8,128)} %maximum_convert_fusion, f32[256]{0:T(256)} %bitcast.222, f32[256]{0:T(256)} %bitcast.221, f32[256]{0:T(256)} %bitcast.220, f32[256]{0:T(256)} %bitcast.219, ...), kind=kLoop, calls=%fused_computation.262 | loop fusion | flops 23592960 | bytes 44065792 | tf_op jit(solution)/shard_map/convert_element_type | solution.py:83
  121.6 3.3 multiply_reduce_fusion.2
  124.9 4.9 %fusion.52 = (f32[256]{0:T(256)S(1)}, f32[256]{0:T(256)S(1)}, f32[256]{0:T(256)S(1)}, f32[256]{0:T(256)S(1)}, f32[256]{0:T(256)}, /*index=5*/f32[256]{0:T(256)},...) fusion(f32[68,28,256]{2,1,0:T(8,128)S(1)} %copy-done.1, ...), kind=kLoop, calls=%fused_computation.132 | loop fusion | flops 16903680 | bytes 32281600 | tf_op jit(solution)/shard_map/reduce_sum | solution.py:102
  130.0 5.7 %collective-permute-start.9 = (bf16[64,2,256]{2,1,0:T(2,128)(2,1)S(1)}, bf16[64,2,256]{2,1,0:T(2,128)(2,1)S(1)}, u32[]{:S(2)}, u32[]{:S(2)}) collective-permute-start(bf16[64,2,256]{2,1,0:T(2,128)(2,1)S(1)} %get-tuple-element.84), channel_id=1, source_target_pairs={{4,0},{8,4},{12,8},{16,12},{20,16},{24,20},{28,24},{32,28},{36,32}... | collective-permute-start | bytes 196616 | tf_op jit(solution)/shard_map/ppermute | solution.py:15
  135.8 1.8 fusion.51
  137.9 0.7 pad_maximum_fusion.6
  138.6 5.7 %collective-permute-start.10 = (bf16[2,28,256]{2,1,0:T(8,128)(2,1)}, bf16[2,28,256]{2,1,0:T(8,128)(2,1)S(1)}, u32[]{:S(2)}, u32[]{:S(2)}) collective-permute-start(bf16[2,28,256]{2,1,0:T(8,128)(2,1)} %get-tuple-element.79), channel_id=1, source_target_pairs={{0,1},{1,2},{2,3},{4,5},{5,6},{6,7},{8,9},{9,10},{10,11},{12,13},{... | collective-permute-start | bytes 86024 | tf_op jit(solution)/shard_map/ppermute | solution.py:14
  144.4 2.2 collective-permute-start.11
  147.0 0.8 copy.35
  147.9 2.1 stack.181
  150.2 1.3 collective-permute-done.11
  151.4 2.6 maximum_convert_fusion.1
  154.2 26.3 %fusion.160 = f32[69,256]{1,0:T(8,128)S(1)} fusion(f32[64,69,24]{1,2,0:T(8,128)} %copy-done.12, f32[64,24,256]{2,1,0:T(8,128)} %get-tuple-element.65, f32[68,28,256]{2,1,0:T(8,128)} %maximum_convert_fusion.1, f32[256]{0:T(256)S(1)} %bitcast.329, f32[256]{0:T(256)S(1)} %bitcast.328, f32[256]{0:T(256)S(1)} %bitcast.327, f32[256]{0:T(256)S(1)} %bitcast.326, ...), kind=kOutput, calls=%fused_computation.280 | convolution fusion | flops 345243648 | bytes 41777152 | tf_op jit(solution)/shard_map/rvj,rjc->vc/dot_general | solution.py:150
  180.5 1.5 constant_dynamic-update-slice_fusion.6
  182.0 1.4 constant_dynamic-update-slice_fusion.5
  183.4 1.4 constant_dynamic-update-slice_fusion.4
  184.8 1.7 constant_dynamic-update-slice_fusion.3
  186.5 1.7 constant_dynamic-update-slice_fusion.2
  188.2 1.3 constant_dynamic-update-slice_fusion.1
  190.1 146.9 %all-reduce.2.cloned.1.call-done = f32[162048]{0:T(1024)} async-done(((f32[162048]{0:T(1024)}), f32[162048]{0:T(1024)}) %all-reduce.2.cloned.1.call-update) | async-done | bytes 648208 | tf_op jit(solution)/shard_map/psum | solution.py:24
  337.0 0.8 slice_multiply_fusion.79
  337.9 0.6 mul.1808
  338.5 0.6 mul.1806
  339.1 1.1 slice_multiply_fusion.76
  340.2 0.8 mul.1812
  341.0 0.9 slice_multiply_fusion.78
  341.9 0.7 mul.1804
  342.5 0.8 mul.1810
  343.3 1.3 slice_multiply_fusion.81
  (217 shorter events, 5.2 us)
Async XLA Ops:
  7.2 329.8 %all-reduce.2.cloned.1.call-start = ((), (), s32[]{:S(2)}) async-start(), calls=%async_computation | async-start | bytes 1302528 | tf_op jit(solution)/shard_map/psum | solution.py:24
  9.6 5.6 %copy-start.21 = (bf16[69,256]{1,0:T(8,128)(2,1)S(1)}, bf16[69,256]{1,0:T(8,128)(2,1)}, u32[]{:S(2)}) copy-start(bf16[69,256]{1,0:T(8,128)(2,1)} %param.12) | copy-start | bytes 105988
  15.2 9.5 %copy-start.19 = (bf16[25,256]{1,0:T(8,128)(2,1)S(1)}, bf16[25,256]{1,0:T(8,128)(2,1)}, u32[]{:S(2)}) copy-start(bf16[25,256]{1,0:T(8,128)(2,1)} %param.13) | copy-start | bytes 38404
  15.2 10.9 %copy-start.20 = (bf16[25,256]{1,0:T(8,128)(2,1)S(1)}, bf16[25,256]{1,0:T(8,128)(2,1)}, u32[]{:S(2)}) copy-start(bf16[25,256]{1,0:T(8,128)(2,1)} %param.16) | copy-start | bytes 38404
  16.7 12.0 %collective-permute-start = (bf16[64,4,256]{2,1,0:T(4,128)(2,1)}, bf16[64,4,256]{2,1,0:T(4,128)(2,1)S(1)}, u32[]{:S(2)}, u32[]{:S(2)}) collective-permute-start(bf16[64,4,256]{2,1,0:T(4,128)(2,1)} %get-tuple-element.87), channel_id=1, source_target_pairs={{0,4},{4,8},{8,12},{12,16},{16,20},{20,24},{24,28},{28,32},{32,36}... | collective-permute-start | bytes 393224 | tf_op jit(solution)/shard_map/ppermute | solution.py:14
  18.7 10.0 %collective-permute-start.1 = (bf16[64,4,256]{2,1,0:T(4,128)(2,1)S(1)}, bf16[64,4,256]{2,1,0:T(4,128)(2,1)S(1)}, u32[]{:S(2)}, u32[]{:S(2)}) collective-permute-start(bf16[64,4,256]{2,1,0:T(4,128)(2,1)S(1)} %get-tuple-element.88), channel_id=1, source_target_pairs={{4,0},{8,4},{12,8},{16,12},{20,16},{24,20},{28,24},{32,28},{36,32}... | collective-permute-start | bytes 393224 | tf_op jit(solution)/shard_map/ppermute | solution.py:15
  28.8 8.0 %collective-permute-start.2 = (bf16[4,32,256]{2,1,0:T(8,128)(2,1)S(1)}, bf16[4,32,256]{2,1,0:T(8,128)(2,1)S(1)}, u32[]{:S(2)}, u32[]{:S(2)}) collective-permute-start(bf16[4,32,256]{2,1,0:T(8,128)(2,1)S(1)} %get-tuple-element.77), channel_id=1, source_target_pairs={{0,1},{1,2},{2,3},{4,5},{5,6},{6,7},{8,9},{9,10},{10,11},{12,13},{... | collective-permute-start | bytes 196616 | tf_op jit(solution)/shard_map/ppermute | solution.py:14
  34.5 7.1 %collective-permute-start.3 = (bf16[4,32,256]{2,1,0:T(8,128)(2,1)S(1)}, bf16[4,32,256]{2,1,0:T(8,128)(2,1)S(1)}, u32[]{:S(2)}, u32[]{:S(2)}) collective-permute-start(bf16[4,32,256]{2,1,0:T(8,128)(2,1)S(1)} %get-tuple-element.78), channel_id=1, source_target_pairs={{1,0},{2,1},{3,2},{5,4},{6,5},{7,6},{9,8},{10,9},{11,10},{13,12},{... | collective-permute-start | bytes 196616 | tf_op jit(solution)/shard_map/ppermute | solution.py:15
  36.6 5.5 %copy-start.57 = (f32[1,256]{1,0:T(1,128)S(1)}, f32[1,256]{1,0:T(1,128)}, u32[]{:S(2)}) copy-start(f32[1,256]{1,0:T(1,128)} %get-tuple-element.176) | copy-start | bytes 3076
  36.6 5.5 %copy-start.58 = (f32[1,256]{1,0:T(1,128)S(1)}, f32[1,256]{1,0:T(1,128)}, u32[]{:S(2)}) copy-start(f32[1,256]{1,0:T(1,128)} %get-tuple-element.177) | copy-start | bytes 3076
  36.6 5.5 %copy-start.59 = (f32[1,256]{1,0:T(1,128)S(1)}, f32[1,256]{1,0:T(1,128)}, u32[]{:S(2)}) copy-start(f32[1,256]{1,0:T(1,128)} %get-tuple-element.178) | copy-start | bytes 3076
  36.6 5.5 %copy-start.60 = (f32[1,256]{1,0:T(1,128)S(1)}, f32[1,256]{1,0:T(1,128)}, u32[]{:S(2)}) copy-start(f32[1,256]{1,0:T(1,128)} %get-tuple-element.179) | copy-start | bytes 3076
  36.6 5.5 %copy-start.61 = (f32[1,256]{1,0:T(1,128)S(1)}, f32[1,256]{1,0:T(1,128)}, u32[]{:S(2)}) copy-start(f32[1,256]{1,0:T(1,128)} %get-tuple-element.180) | copy-start | bytes 3076
  36.7 5.5 %copy-start.62 = (f32[1,256]{1,0:T(1,128)S(1)}, f32[1,256]{1,0:T(1,128)}, u32[]{:S(2)}) copy-start(f32[1,256]{1,0:T(1,128)} %get-tuple-element.181) | copy-start | bytes 3076
  36.7 5.5 %copy-start.63 = (f32[1,256]{1,0:T(1,128)S(1)}, f32[1,256]{1,0:T(1,128)}, u32[]{:S(2)}) copy-start(f32[1,256]{1,0:T(1,128)} %get-tuple-element.182) | copy-start | bytes 3076
  36.7 5.5 %copy-start.64 = (f32[1,256]{1,0:T(1,128)S(1)}, f32[1,256]{1,0:T(1,128)}, u32[]{:S(2)}) copy-start(f32[1,256]{1,0:T(1,128)} %get-tuple-element.183) | copy-start | bytes 3076
  36.7 5.5 %copy-start.65 = (f32[1,256]{1,0:T(1,128)S(1)}, f32[1,256]{1,0:T(1,128)}, u32[]{:S(2)}) copy-start(f32[1,256]{1,0:T(1,128)} %get-tuple-element.184) | copy-start | bytes 3076
  36.7 5.5 %copy-start.66 = (f32[1,256]{1,0:T(1,128)S(1)}, f32[1,256]{1,0:T(1,128)}, u32[]{:S(2)}) copy-start(f32[1,256]{1,0:T(1,128)} %get-tuple-element.185) | copy-start | bytes 3076
  36.7 5.5 %copy-start.67 = (f32[1,256]{1,0:T(1,128)S(1)}, f32[1,256]{1,0:T(1,128)}, u32[]{:S(2)}) copy-start(f32[1,256]{1,0:T(1,128)} %get-tuple-element.186) | copy-start | bytes 3076
  36.7 5.5 %copy-start.68 = (f32[1,256]{1,0:T(1,128)S(1)}, f32[1,256]{1,0:T(1,128)}, u32[]{:S(2)}) copy-start(f32[1,256]{1,0:T(1,128)} %get-tuple-element.187) | copy-start | bytes 3076
  36.7 5.5 %copy-start.69 = (f32[1,256]{1,0:T(1,128)S(1)}, f32[1,256]{1,0:T(1,128)}, u32[]{:S(2)}) copy-start(f32[1,256]{1,0:T(1,128)} %get-tuple-element.188) | copy-start | bytes 3076
  36.7 5.5 %copy-start.70 = (f32[1,256]{1,0:T(1,128)S(1)}, f32[1,256]{1,0:T(1,128)}, u32[]{:S(2)}) copy-start(f32[1,256]{1,0:T(1,128)} %get-tuple-element.189) | copy-start | bytes 3076
  36.7 5.5 %copy-start.71 = (f32[1,256]{1,0:T(1,128)S(1)}, f32[1,256]{1,0:T(1,128)}, u32[]{:S(2)}) copy-start(f32[1,256]{1,0:T(1,128)} %get-tuple-element.190) | copy-start | bytes 3076
  36.8 5.5 %copy-start.72 = (f32[1,256]{1,0:T(1,128)S(1)}, f32[1,256]{1,0:T(1,128)}, u32[]{:S(2)}) copy-start(f32[1,256]{1,0:T(1,128)} %get-tuple-element.191) | copy-start | bytes 3076
  36.8 5.5 %copy-start.73 = (f32[1,256]{1,0:T(1,128)S(1)}, f32[1,256]{1,0:T(1,128)}, u32[]{:S(2)}) copy-start(f32[1,256]{1,0:T(1,128)} %get-tuple-element.192) | copy-start | bytes 3076
  36.8 5.5 %copy-start.74 = (f32[1,256]{1,0:T(1,128)S(1)}, f32[1,256]{1,0:T(1,128)}, u32[]{:S(2)}) copy-start(f32[1,256]{1,0:T(1,128)} %get-tuple-element.193) | copy-start | bytes 3076
  36.8 5.5 %copy-start.75 = (f32[1,256]{1,0:T(1,128)S(1)}, f32[1,256]{1,0:T(1,128)}, u32[]{:S(2)}) copy-start(f32[1,256]{1,0:T(1,128)} %get-tuple-element.194) | copy-start | bytes 3076
  42.3 7.0 %copy-start.31 = (f32[256]{0:T(256)S(1)}, f32[256]{0:T(256)}, u32[]{:S(2)}) copy-start(f32[256]{0:T(256)} %param.14) | copy-start | bytes 3076
  55.5 6.1 %copy-start.15 = (bf16[256,256]{1,0:T(8,128)(2,1)S(1)}, bf16[256,256]{1,0:T(8,128)(2,1)}, u32[]{:S(2)}) copy-start(bf16[256,256]{1,0:T(8,128)(2,1)} %param.18) | copy-start | bytes 393220
  55.5 6.1 %copy-start.30 = (f32[256]{0:T(256)S(1)}, f32[256]{0:T(256)}, u32[]{:S(2)}) copy-start(f32[256]{0:T(256)} %param.17) | copy-start | bytes 3076
  61.7 4.1 %copy-start.6 = (f32[64,24,256]{2,1,0:T(8,128)S(1)}, f32[64,24,256]{2,1,0:T(8,128)}, u32[]{:S(2)}) copy-start(f32[64,24,256]{2,1,0:T(8,128)} %get-tuple-element.67) | copy-start | bytes 4718596
  71.8 9.5 %copy-start.7 = (bf16[64,24,256]{2,1,0:T(8,128)(2,1)}, bf16[64,24,256]{2,1,0:T(8,128)(2,1)S(1)}, u32[]{:S(2)}) copy-start(bf16[64,24,256]{2,1,0:T(8,128)(2,1)S(1)} %get-tuple-element.62) | copy-start | bytes 2359300
  73.7 7.6 %collective-permute-start.4 = (bf16[64,2,256]{2,1,0:T(2,128)(2,1)S(1)}, bf16[64,2,256]{2,1,0:T(2,128)(2,1)S(1)}, u32[]{:S(2)}, u32[]{:S(2)}) collective-permute-start(bf16[64,2,256]{2,1,0:T(2,128)(2,1)S(1)} %get-tuple-element.85), channel_id=1, source_target_pairs={{0,4},{4,8},{8,12},{12,16},{16,20},{20,24},{24,28},{28,32},{32,36}... | collective-permute-start | bytes 196616 | tf_op jit(solution)/shard_map/ppermute | solution.py:14
  74.0 7.3 %collective-permute-start.5 = (bf16[64,2,256]{2,1,0:T(2,128)(2,1)S(1)}, bf16[64,2,256]{2,1,0:T(2,128)(2,1)S(1)}, u32[]{:S(2)}, u32[]{:S(2)}) collective-permute-start(bf16[64,2,256]{2,1,0:T(2,128)(2,1)S(1)} %get-tuple-element.86), channel_id=1, source_target_pairs={{4,0},{8,4},{12,8},{16,12},{20,16},{24,20},{28,24},{32,28},{36,32}... | collective-permute-start | bytes 196616 | tf_op jit(solution)/shard_map/ppermute | solution.py:15
  79.7 7.3 %copy-start.3 = (f32[68,28,256]{2,0,1:T(8,128)S(1)}, f32[68,28,256]{2,0,1:T(8,128)}, u32[]{:S(2)}) copy-start(f32[68,28,256]{2,0,1:T(8,128)} %copy-done.2) | copy-start | bytes 5849092
  82.0 10.7 %collective-permute-start.6 = (bf16[2,28,256]{2,1,0:T(8,128)(2,1)}, bf16[2,28,256]{2,1,0:T(8,128)(2,1)}, u32[]{:S(2)}, u32[]{:S(2)}) collective-permute-start(bf16[2,28,256]{2,1,0:T(8,128)(2,1)} %get-tuple-element.81), channel_id=1, source_target_pairs={{0,1},{1,2},{2,3},{4,5},{5,6},{6,7},{8,9},{9,10},{10,11},{12,13},{... | collective-permute-start | bytes 86024 | tf_op jit(solution)/shard_map/ppermute | solution.py:14
  85.0 7.7 %collective-permute-start.7 = (bf16[2,28,256]{2,1,0:T(8,128)(2,1)}, bf16[2,28,256]{2,1,0:T(8,128)(2,1)}, u32[]{:S(2)}, u32[]{:S(2)}) collective-permute-start(bf16[2,28,256]{2,1,0:T(8,128)(2,1)} %get-tuple-element.82), channel_id=1, source_target_pairs={{1,0},{2,1},{3,2},{5,4},{6,5},{7,6},{9,8},{10,9},{11,10},{13,12},{... | collective-permute-start | bytes 86024 | tf_op jit(solution)/shard_map/ppermute | solution.py:15
  87.0 5.7 %copy-start.8 = (bf16[64,24,256]{2,1,0:T(8,128)(2,1)S(1)}, bf16[64,24,256]{2,1,0:T(8,128)(2,1)}, u32[]{:S(2)}) copy-start(bf16[64,24,256]{2,1,0:T(8,128)(2,1)} %copy-done.7) | copy-start | bytes 2359300
  95.5 26.1 %copy-start.17 = (bf16[256,256]{1,0:T(8,128)(2,1)S(1)}, bf16[256,256]{1,0:T(8,128)(2,1)}, u32[]{:S(2)}) copy-start(bf16[256,256]{1,0:T(8,128)(2,1)} %param.15) | copy-start | bytes 393220
  129.9 8.0 %collective-permute-start.8 = (bf16[64,2,256]{2,1,0:T(2,128)(2,1)S(1)}, bf16[64,2,256]{2,1,0:T(2,128)(2,1)S(1)}, u32[]{:S(2)}, u32[]{:S(2)}) collective-permute-start(bf16[64,2,256]{2,1,0:T(2,128)(2,1)S(1)} %get-tuple-element.83), channel_id=1, source_target_pairs={{0,4},{4,8},{8,12},{12,16},{16,20},{20,24},{24,28},{28,32},{32,36}... | collective-permute-start | bytes 196616 | tf_op jit(solution)/shard_map/ppermute | solution.py:14
  130.0 16.5 %copy-start.10 = (bf16[68,28,256]{2,1,0:T(8,128)(2,1)S(1)}, bf16[68,28,256]{2,1,0:T(8,128)(2,1)}, u32[]{:S(2)}) copy-start(bf16[68,28,256]{2,1,0:T(8,128)(2,1)} %copy-done.9) | copy-start | bytes 2924548
  130.0 16.5 %copy-start.14 = (bf16[64,24,256]{2,1,0:T(8,128)(2,1)S(1)}, bf16[64,24,256]{2,1,0:T(8,128)(2,1)}, u32[]{:S(2)}) copy-start(bf16[64,24,256]{2,1,0:T(8,128)(2,1)} %copy-done.13) | copy-start | bytes 2359300
  130.0 7.9 %collective-permute-start.9 = (bf16[64,2,256]{2,1,0:T(2,128)(2,1)S(1)}, bf16[64,2,256]{2,1,0:T(2,128)(2,1)S(1)}, u32[]{:S(2)}, u32[]{:S(2)}) collective-permute-start(bf16[64,2,256]{2,1,0:T(2,128)(2,1)S(1)} %get-tuple-element.84), channel_id=1, source_target_pairs={{4,0},{8,4},{12,8},{16,12},{20,16},{24,20},{28,24},{32,28},{36,32}... | collective-permute-start | bytes 196616 | tf_op jit(solution)/shard_map/ppermute | solution.py:15
  138.6 11.6 %collective-permute-start.10 = (bf16[2,28,256]{2,1,0:T(8,128)(2,1)}, bf16[2,28,256]{2,1,0:T(8,128)(2,1)S(1)}, u32[]{:S(2)}, u32[]{:S(2)}) collective-permute-start(bf16[2,28,256]{2,1,0:T(8,128)(2,1)} %get-tuple-element.79), channel_id=1, source_target_pairs={{0,1},{1,2},{2,3},{4,5},{5,6},{6,7},{8,9},{9,10},{10,11},{12,13},{... | collective-permute-start | bytes 86024 | tf_op jit(solution)/shard_map/ppermute | solution.py:14
  144.3 3.6 %copy-start.33 = (f32[256]{0:T(256)S(1)}, f32[256]{0:T(256)}, u32[]{:S(2)}) copy-start(f32[256]{0:T(256)} %get-tuple-element.41) | copy-start | bytes 3076
  144.3 3.6 %copy-start.34 = (f32[256]{0:T(256)S(1)}, f32[256]{0:T(256)}, u32[]{:S(2)}) copy-start(f32[256]{0:T(256)} %get-tuple-element.42) | copy-start | bytes 3076
  144.4 7.1 %collective-permute-start.11 = (bf16[2,28,256]{2,1,0:T(8,128)(2,1)}, bf16[2,28,256]{2,1,0:T(8,128)(2,1)}, u32[]{:S(2)}, u32[]{:S(2)}) collective-permute-start(bf16[2,28,256]{2,1,0:T(8,128)(2,1)} %get-tuple-element.80), channel_id=1, source_target_pairs={{1,0},{2,1},{3,2},{5,4},{6,5},{7,6},{9,8},{10,9},{11,10},{13,12},{... | collective-permute-start | bytes 86024 | tf_op jit(solution)/shard_map/ppermute | solution.py:15
  150.0 4.0 %copy-start.77 = (f32[1,256]{1,0:T(1,128)S(1)}, f32[1,256]{1,0:T(1,128)}, u32[]{:S(2)}) copy-start(f32[1,256]{1,0:T(1,128)} %get-tuple-element.120) | copy-start | bytes 3076
  150.0 4.0 %copy-start.78 = (f32[1,256]{1,0:T(1,128)S(1)}, f32[1,256]{1,0:T(1,128)}, u32[]{:S(2)}) copy-start(f32[1,256]{1,0:T(1,128)} %get-tuple-element.121) | copy-start | bytes 3076
  150.0 4.0 %copy-start.79 = (f32[1,256]{1,0:T(1,128)S(1)}, f32[1,256]{1,0:T(1,128)}, u32[]{:S(2)}) copy-start(f32[1,256]{1,0:T(1,128)} %get-tuple-element.122) | copy-start | bytes 3076
  150.1 4.0 %copy-start.80 = (f32[1,256]{1,0:T(1,128)S(1)}, f32[1,256]{1,0:T(1,128)}, u32[]{:S(2)}) copy-start(f32[1,256]{1,0:T(1,128)} %get-tuple-element.123) | copy-start | bytes 3076
  150.1 4.0 %copy-start.81 = (f32[1,256]{1,0:T(1,128)S(1)}, f32[1,256]{1,0:T(1,128)}, u32[]{:S(2)}) copy-start(f32[1,256]{1,0:T(1,128)} %get-tuple-element.124) | copy-start | bytes 3076
  150.1 4.0 %copy-start.82 = (f32[1,256]{1,0:T(1,128)S(1)}, f32[1,256]{1,0:T(1,128)}, u32[]{:S(2)}) copy-start(f32[1,256]{1,0:T(1,128)} %get-tuple-element.125) | copy-start | bytes 3076
  150.1 4.0 %copy-start.83 = (f32[1,256]{1,0:T(1,128)S(1)}, f32[1,256]{1,0:T(1,128)}, u32[]{:S(2)}) copy-start(f32[1,256]{1,0:T(1,128)} %get-tuple-element.101) | copy-start | bytes 3076
  150.1 4.0 %copy-start.84 = (f32[1,256]{1,0:T(1,128)S(1)}, f32[1,256]{1,0:T(1,128)}, u32[]{:S(2)}) copy-start(f32[1,256]{1,0:T(1,128)} %get-tuple-element.102) | copy-start | bytes 3076
  150.1 4.0 %copy-start.85 = (f32[1,256]{1,0:T(1,128)S(1)}, f32[1,256]{1,0:T(1,128)}, u32[]{:S(2)}) copy-start(f32[1,256]{1,0:T(1,128)} %get-tuple-element.103) | copy-start | bytes 3076
  150.1 4.0 %copy-start.86 = (f32[1,256]{1,0:T(1,128)S(1)}, f32[1,256]{1,0:T(1,128)}, u32[]{:S(2)}) copy-start(f32[1,256]{1,0:T(1,128)} %get-tuple-element.104) | copy-start | bytes 3076
  150.1 4.0 %copy-start.87 = (f32[1,256]{1,0:T(1,128)S(1)}, f32[1,256]{1,0:T(1,128)}, u32[]{:S(2)}) copy-start(f32[1,256]{1,0:T(1,128)} %get-tuple-element.105) | copy-start | bytes 3076
  150.1 4.0 %copy-start.88 = (f32[1,256]{1,0:T(1,128)S(1)}, f32[1,256]{1,0:T(1,128)}, u32[]{:S(2)}) copy-start(f32[1,256]{1,0:T(1,128)} %get-tuple-element.106) | copy-start | bytes 3076
  150.1 4.0 %copy-start.89 = (f32[1,256]{1,0:T(1,128)S(1)}, f32[1,256]{1,0:T(1,128)}, u32[]{:S(2)}) copy-start(f32[1,256]{1,0:T(1,128)} %get-tuple-element.107) | copy-start | bytes 3076
  154.2 29.3 %copy-start.18 = (f32[6400]{0:T(1024)S(1)}, f32[6400]{0:T(1024)}, u32[]{:S(2)}) copy-start(f32[6400]{0:T(1024)} %reshape.504) | copy-start | bytes 76804
  154.2 30.6 %copy-start.11 = (f32[32,2,8,128]{3,1,2,0:T(2,128)S(1)}, f32[32,2,8,128]{3,1,2,0:T(2,128)}, u32[]{:S(2)}) copy-start(f32[32,2,8,128]{3,1,2,0:T(2,128)} %copy.35) | copy-start | bytes 786436
  154.2 34.0 %copy-start.90 = (f32[256]{0:T(256)S(1)}, f32[256]{0:T(256)}, u32[]{:S(2)}) copy-start(f32[256]{0:T(256)} %get-tuple-element.8) | copy-start | bytes 3076
  154.2 35.3 %copy-start.76 = (f32[256]{0:T(256)S(1)}, f32[256]{0:T(256)}, u32[]{:S(2)}) copy-start(f32[256]{0:T(256)} %get-tuple-element.10) | copy-start | bytes 3076
  (40 other events, 121.2 us)
Sparse Core Ops, SparseCore 0:
  190.2 146.7 all-reduce.1
where the time goes:
time: 352 us; the launch traced here: 351 us
  waiting for transfers between devices  154 us (44%)
  other arithmetic  69.7 us (20%)
  matrix products  42.7 us (12%)
  starting transfers between devices  40.3 us (11%)
  local copies, waits for them, and re-layouts  28.8 us (8%)
  between operations  15.5 us (4%)
    psum x1, waiting for transfers between devices, together(): total = lax.psum(jnp.concatenate([a.ravel() for a in arrays]), axis)  147 us
    dot_general x1, matrix products, on_device(): jnp.einsum('rvj,rjc->vc', regridded, grad0, precision=lax.Precision.HIGHEST)  26.3 us
    convert_element_type x1, other arithmetic, mix_backward(): dmixed = (upstream * sig * (1.0 + mixed * (1.0 - sig))).astype(jnp.bfloat16)  26.1 us
    ppermute x6, starting transfers between devices, with_halo(): after = lax.ppermute(initial, axis, down)  23.5 us
    ppermute x6, starting transfers between devices, with_halo(): before = lax.ppermute(last, axis, up)  16.7 us
    reduce_sum x4, other arithmetic, kernel_grad(): jnp.sum((wide[first:first + nrows, second:second + ncols] * back).reshape...  13.2 us
    reduce_sum x2, other arithmetic, mix_forward(): scale = lax.rsqrt(jnp.mean(conv * conv, -1, keepdims=True) + 1e-06)  13.1 us
    unnamed x190, local copies, waits for them, and re-layouts  12.2 us
  transfers between devices with their start and end apart: 13, of which 5 were waited for; matrix products, arithmetic and copies ran while one was open for 4% of the time, Pallas kernels for 0%

commit v1 on v0

--- a/solution.py
+++ b/solution.py
@@ -17,11 +17,20 @@
     return array
 
 
-def together(arrays, axis):
+def together(arrays, axes):
+    devices = 1
+    for axis in axes:
+        devices *= lax.axis_size(axis)
+    sizes = [a.size for a in arrays]
+    share = -(-sum(sizes) // (128 * devices)) * 128
+    padding = jnp.zeros((share * devices - sum(sizes),), jnp.float32)
+    flat = jnp.concatenate([a.ravel() for a in arrays] + [padding])
+    parts = lax.all_to_all(flat.reshape(devices, share), axes, 0, 0)
+    mine = jnp.broadcast_to(jnp.sum(parts, 0), (devices, share))
+    total = lax.all_to_all(mine, axes, 0, 0).ravel()
     ends = [0]
-    for a in arrays:
-        ends.append(ends[-1] + a.size)
-    total = lax.psum(jnp.concatenate([a.ravel() for a in arrays]), axis)
+    for size in sizes:
+        ends.append(ends[-1] + size)
     return tuple((total[b:e].reshape(a.shape) for a, b, e in zip(arrays, ends, ends[1:])))
 
 

time: 352 us -> 241 us (0.68)
  waiting for transfers between devices: 154 us -> 7.42 us
  blocking collectives: 0 us -> 42.3 us
  between operations: 15.5 us -> 2.55 us
    psum x1 -> x0, waiting for transfers between devices: 147 us -> none  [together(): total = lax.psum(jnp.concatenate([a.ravel() for a in arrays]), axis)]
    all_to_all x0 -> x2, blocking collectives: none -> 42.3 us  [the longest x1 23.5 us: together(): parts = lax.all_to_all(flat.reshape(devices, share), axes, 0, 0)]
    unnamed x190 -> x193, local copies, waits for them, and re-layouts: 12.2 us -> 14.3 us
  transfers between devices with their start and end apart: 13 -> 12, of which waited for: 5 -> 4; matrix products, arithmetic and copies ran while one was open for 4% -> 7% of each run, Pallas kernels for 0% -> 0%
where the time goes in v1:
time: 241 us; the launch traced here: 237 us
  other arithmetic  72 us (30%)
  matrix products  42.7 us (18%)
  blocking collectives  42.3 us (18%)
  starting transfers between devices  40.2 us (17%)
  local copies, waits for them, and re-layouts  29.8 us (12%)
  waiting for transfers between devices  7.42 us (3%)
  between operations  2.55 us (1%)
    dot_general x1, matrix products, on_device(): jnp.einsum('rvj,rjc->vc', regridded, grad0, precision=lax.Precision.HIGHEST)  26.3 us
    convert_element_type x1, other arithmetic, mix_backward(): dmixed = (upstream * sig * (1.0 + mixed * (1.0 - sig))).astype(jnp.bfloat16)  26.1 us
    ppermute x6, starting transfers between devices, with_halo(): after = lax.ppermute(initial, axis, down)  23.5 us
    all_to_all x1, blocking collectives, together(): parts = lax.all_to_all(flat.reshape(devices, share), axes, 0, 0)  23.5 us
    all_to_all x1, blocking collectives, together(): total = lax.all_to_all(mine, axes, 0, 0).ravel()  18.8 us
    ppermute x6, starting transfers between devices, with_halo(): before = lax.ppermute(last, axis, up)  16.8 us
    unnamed x193, local copies, waits for them, and re-layouts  14.3 us
    reduce_sum x4, other arithmetic, kernel_grad(): jnp.sum((wide[first:first + nrows, second:second + ncols] * back).reshape...  13.2 us
  transfers between devices with their start and end apart: 12, of which 4 were waited for; matrix products, arithmetic and copies ran while one was open for 7% of the time, Pallas kernels for 0%

profile of v1, /device:TPU:1, one launch (start us, length us, event | category | flops | bytes accessed | tf_op | source)
XLA Modules:
  0.0 237.0 jit_solution(17650552865577517136)
XLA Ops:
  0.7 0.8 and_select_fusion
  1.5 0.8 broadcast_subtract_fusion
  2.2 0.8 broadcast_subtract_fusion.1
  3.0 4.7 %fusion.155 = f32[64,69,24]{1,2,0:T(8,128)S(1)} fusion(bf16[64,69,163]{2,0,1:T(8,128)(2,1)S(1)} %copy-done, f32[64,24]{1,0:T(8,128)S(1)} %get-tuple-element.204, s32[64,24]{1,0:T(8,128)S(1)} %get-tuple-element.202, f32[64,24]{1,0:T(8,128)S(1)} %get-tuple-element.203, s32[64,24]{1,0:T(8,128)S(1)} %get-tuple-element.201), kind=kOutput, calls=%fused_computation.276 | convolution fusion | flops 208556544 | bytes 1888128 | tf_op jit(solution)/shard_map/rvsm,rsjm->rvsj/dot_general | solution.py:51
  7.7 0.9 copy-done.13
  8.6 0.8 convolution_convert_fusion
  9.4 0.8 fusion.217
  10.1 2.0 collective-permute-start
  12.2 5.9 %collective-permute-start.1 = (bf16[64,4,256]{2,1,0:T(4,128)(2,1)S(1)}, bf16[64,4,256]{2,1,0:T(4,128)(2,1)S(1)}, u32[]{:S(2)}, u32[]{:S(2)}) collective-permute-start(bf16[64,4,256]{2,1,0:T(4,128)(2,1)S(1)} %get-tuple-element.88), channel_id=1, source_target_pairs={{4,0},{8,4},{12,8},{16,12},{20,16},{24,20},{28,24},{32,28},{36,32}... | collective-permute-start | bytes 393224 | tf_op jit(solution)/shard_map/ppermute | solution.py:15
  18.8 0.7 fusion.218
  19.6 0.7 fusion.224
  20.3 0.7 fusion.222
  20.9 0.6 fusion.220
  22.2 5.7 %collective-permute-start.2 = (bf16[4,32,256]{2,1,0:T(8,128)(2,1)S(1)}, bf16[4,32,256]{2,1,0:T(8,128)(2,1)S(1)}, u32[]{:S(2)}, u32[]{:S(2)}) collective-permute-start(bf16[4,32,256]{2,1,0:T(8,128)(2,1)S(1)} %get-tuple-element.77), channel_id=1, source_target_pairs={{0,1},{1,2},{2,3},{4,5},{5,6},{6,7},{8,9},{9,10},{10,11},{12,13},{... | collective-permute-start | bytes 196616 | tf_op jit(solution)/shard_map/ppermute | solution.py:14
  27.9 2.1 collective-permute-start.3
  30.2 4.8 %collective-permute-done.3 = bf16[4,32,256]{2,1,0:T(8,128)(2,1)S(1)} collective-permute-done((bf16[4,32,256]{2,1,0:T(8,128)(2,1)S(1)}, bf16[4,32,256]{2,1,0:T(8,128)(2,1)S(1)}, u32[]{:S(2)}, u32[]{:S(2)}) %collective-permute-start.3) | collective-permute-done | bytes 65568 | tf_op jit(solution)/shard_map/ppermute | solution.py:15
  35.8 7.0 %multiply_reduce_fusion = (f32[68,28]{1,0:T(8,128)S(1)}, f32[68,28,256]{2,1,0:T(8,128)S(1)}) fusion(f32[256]{0:T(256)S(1)} %bitcast.289, f32[72,32,256]{2,1,0:T(8,128)S(1)} %get-tuple-element.76, f32[256]{0:T(256)S(1)} %bitcast.288, f32[256]{0:T(256)S(1)} %bitcast.287, f32[256]{0:T(256)S(1)} %bitcast.286, f32[256]{0:T(256)S(1)} %bitcast.285, ...), kind=kLoop, calls=%fused_computation.103 | loop fusion | flops 24856720 | bytes 50725312 | tf_op jit(solution)/shard_map/reduce_sum | solution.py:79
  43.2 1.0 copy-done.4
  44.2 1.2 fusion.163
  45.6 3.2 %fusion.213 = (f32[68,28,256]{2,1,0:T(8,128)S(1)}, bf16[68,28,256]{2,1,0:T(8,128)(2,1)}, f32[68,28,256]{2,1,0:T(8,128)}) fusion(f32[68,28,256]{2,0,1:T(8,128)S(1)} %fusion.163, bf16[72,32,256]{2,1,0:T(8,128)(2,1)S(1)} %get-tuple-element.75, pred[68]{0:T(512)(128)(4,1)S(1)} %compare_and_fusion), kind=kLoop, calls=%fused_computation.377 | loop fusion | flops 4386816 | bytes 7798852 | tf_op jit(solution)/shard_map/convert_element_type | solution.py:67
  49.0 6.1 %multiply_reduce_fusion.5 = (f32[64,24]{1,0:T(8,128)S(1)}, f32[64,24,256]{2,1,0:T(8,128)}) fusion(f32[256]{0:T(256)S(1)} %bitcast.283, f32[68,28,256]{2,1,0:T(8,128)S(1)} %get-tuple-element.68, f32[256]{0:T(256)S(1)} %bitcast.282, f32[256]{0:T(256)S(1)} %bitcast.281, f32[256]{0:T(256)S(1)} %bitcast.280, f32[256]{0:T(256)S(1)} %bitcast.279, ...), kind=kLoop, calls=%fused_computation.268 | loop fusion | flops 20052480 | bytes 40926208 | tf_op jit(solution)/shard_map/reduce_sum | solution.py:79
  55.1 4.1 %fusion.27 = (bf16[64,24,256]{2,1,0:T(8,128)(2,1)S(1)}, bf16[64,24,256]{2,1,0:T(8,128)(2,1)}) fusion(bf16[64,24,256]{2,1,0:T(8,128)(2,1)} %param.19, bf16[68,28,256]{2,1,0:T(8,128)(2,1)} %get-tuple-element.69, bf16[256,256]{1,0:T(8,128)(2,1)S(1)} %copy-done.16, f32[64,24,256]{2,1,0:T(8,128)} %get-tuple-element.67, f32[256]{0:T(256)S(1)} %copy-done.31, ...), kind=kOutput, calls=%fused_computation.107 | convolution fusion | flops 208011264 | bytes 4856832 | tf_op jit(solution)/shard_map/dot_general | solution.py:81
  59.2 1.3 multiply_reduce_fusion.1
  60.5 4.8 %fusion.77 = (f32[256]{0:T(256)}, f32[256]{0:T(256)}, f32[256]{0:T(256)}, f32[256]{0:T(256)}, f32[256]{0:T(256)}, /*index=5*/f32[256]{0:T(256)}, f32[256]{0:T(25...) fusion(f32[68,28,256]{2,1,0:T(8,128)S(1)} %get-tuple-element.68, ...), kind=kLoop, calls=%fused_computation.157 | loop fusion | flops 16903680 | bytes 32281600 | tf_op jit(solution)/shard_map/reduce_sum | solution.py:111
  65.2 1.8 fusion.76
  67.4 5.7 %collective-permute-start.5 = (bf16[64,2,256]{2,1,0:T(2,128)(2,1)S(1)}, bf16[64,2,256]{2,1,0:T(2,128)(2,1)S(1)}, u32[]{:S(2)}, u32[]{:S(2)}) collective-permute-start(bf16[64,2,256]{2,1,0:T(2,128)(2,1)S(1)} %get-tuple-element.86), channel_id=1, source_target_pairs={{4,0},{8,4},{12,8},{16,12},{20,16},{24,20},{28,24},{32,28},{36,32}... | collective-permute-start | bytes 196616 | tf_op jit(solution)/shard_map/ppermute | solution.py:15
  73.1 0.7 convolution_bitcast_fusion
  73.8 1.0 collective-permute-done.4
  74.8 0.7 pad_maximum_fusion.9
  75.4 3.0 %collective-permute-start.6 = (bf16[2,28,256]{2,1,0:T(8,128)(2,1)}, bf16[2,28,256]{2,1,0:T(8,128)(2,1)}, u32[]{:S(2)}, u32[]{:S(2)}) collective-permute-start(bf16[2,28,256]{2,1,0:T(8,128)(2,1)} %get-tuple-element.81), channel_id=1, source_target_pairs={{0,1},{1,2},{2,3},{4,5},{5,6},{6,7},{8,9},{9,10},{10,11},{12,13},{... | collective-permute-start | bytes 86024 | tf_op jit(solution)/shard_map/ppermute | solution.py:14
  78.4 1.9 collective-permute-start.7
  80.5 2.0 copy.48
  82.6 2.9 %stack.207 = f32[25,256]{1,0:T(8,128)S(1)} concatenate(f32[1,256]{1,0:T(1,128)} %bitcast.252, f32[1,256]{1,0:T(1,128)} %bitcast.229, f32[1,256]{1,0:T(1,128)} %bitcast.230, f32[1,256]{1,0:T(1,128)} %bitcast.231, f32[1,256]{1,0:T(1,128)} %bitcast.232, f32[1,256]{1,0:T(1,128)} %bitcast.233, f32[1,256]{1,0:T(1,128)} %bitcast.234, f32[1,256]{1,0:T(1,128)} %bitcast.235, ...), dimensions={0} | concatenate | bytes 51200 | tf_op jit(solution)/shard_map/stack | solution.py:118
  86.2 2.7 %maximum_convert_fusion = f32[68,28,256]{2,1,0:T(8,128)} fusion(bf16[2,28,256]{2,1,0:T(8,128)(2,1)} %collective-permute-done.7, bf16[64,2,256]{2,1,0:T(2,128)(2,1)S(1)} %collective-permute-done.5, bf16[64,24,256]{2,1,0:T(8,128)(2,1)S(1)} %copy-done.8, bf16[64,2,256]{2,1,0:T(2,128)(2,1)S(1)} %collective-permute-done.4, ...), kind=kLoop, calls=%fused_computation.282 | loop fusion | flops 4874240 | bytes 2924544 | tf_op jit(solution)/shard_map/convert_element_type | solution.py:67
  89.0 26.1 %multiply_convert_fusion.1 = (bf16[64,24,256]{2,1,0:T(8,128)(2,1)S(1)}, f32[64,24,256]{2,1,0:T(8,128)}) fusion(f32[68,28,256]{2,1,0:T(8,128)} %copy.48, f32[256]{0:T(256)} %bitcast.227, f32[68,28,256]{2,1,0:T(8,128)} %maximum_convert_fusion, f32[256]{0:T(256)} %bitcast.226, f32[256]{0:T(256)} %bitcast.225, f32[256]{0:T(256)} %bitcast.224, f32[256]{0:T(256)} %bitcast.223, ...), kind=kLoop, calls=%fused_computation.262 | loop fusion | flops 23592960 | bytes 44065792 | tf_op jit(solution)/shard_map/convert_element_type | solution.py:92
  115.1 3.3 %multiply_reduce_fusion.2 = (f32[256]{0:T(256)}, f32[64,24]{1,0:T(8,128)S(1)}, f32[64,24,256]{2,1,0:T(8,128)S(1)}) fusion(f32[68,28,256]{2,1,0:T(8,128)} %copy-done.4, f32[64,24]{1,0:T(8,128)S(1)} %get-tuple-element.96, f32[256]{0:T(256)} %param.14, bf16[64,24,256]{2,1,0:T(8,128)(2,1)S(1)} %get-tuple-element.64, bf16[256,256]{1,0:T(8,128)(2,1)S(1)} %copy-done.18), kind=kOutput, calls=%fused_computation.259 | convolution fusion | flops 203684096 | bytes 4077568 | tf_op jit(solution)/shard_map/dot_general | solution.py:96
  118.4 4.9 %fusion.52 = (f32[256]{0:T(256)S(1)}, f32[256]{0:T(256)S(1)}, f32[256]{0:T(256)S(1)}, f32[256]{0:T(256)S(1)}, f32[256]{0:T(256)}, /*index=5*/f32[256]{0:T(256)},...) fusion(f32[68,28,256]{2,1,0:T(8,128)S(1)} %copy-done.1, ...), kind=kLoop, calls=%fused_computation.132 | loop fusion | flops 16903680 | bytes 32281600 | tf_op jit(solution)/shard_map/reduce_sum | solution.py:111
  123.5 5.7 %collective-permute-start.9 = (bf16[64,2,256]{2,1,0:T(2,128)(2,1)S(1)}, bf16[64,2,256]{2,1,0:T(2,128)(2,1)S(1)}, u32[]{:S(2)}, u32[]{:S(2)}) collective-permute-start(bf16[64,2,256]{2,1,0:T(2,128)(2,1)S(1)} %get-tuple-element.84), channel_id=1, source_target_pairs={{4,0},{8,4},{12,8},{16,12},{20,16},{24,20},{28,24},{32,28},{36,32}... | collective-permute-start | bytes 196616 | tf_op jit(solution)/shard_map/ppermute | solution.py:15
  129.2 1.8 fusion.51
  131.4 0.7 pad_maximum_fusion.6
  132.0 5.7 %collective-permute-start.10 = (bf16[2,28,256]{2,1,0:T(8,128)(2,1)}, bf16[2,28,256]{2,1,0:T(8,128)(2,1)S(1)}, u32[]{:S(2)}, u32[]{:S(2)}) collective-permute-start(bf16[2,28,256]{2,1,0:T(8,128)(2,1)} %get-tuple-element.79), channel_id=1, source_target_pairs={{0,1},{1,2},{2,3},{4,5},{5,6},{6,7},{8,9},{9,10},{10,11},{12,13},{... | collective-permute-start | bytes 86024 | tf_op jit(solution)/shard_map/ppermute | solution.py:14
  137.8 2.2 collective-permute-start.11
  140.4 0.8 copy.52
  141.3 2.1 stack.181
  143.6 1.3 collective-permute-done.11
  144.9 2.6 %maximum_convert_fusion.1 = f32[68,28,256]{2,1,0:T(8,128)} fusion(bf16[2,28,256]{2,1,0:T(8,128)(2,1)} %collective-permute-done.11, bf16[64,2,256]{2,1,0:T(2,128)(2,1)S(1)} %collective-permute-done.9, bf16[64,24,256]{2,1,0:T(8,128)(2,1)S(1)} %get-tuple-element.63, bf16[64,2,256]{2,1,0:T(2,128)(2,1)S(1)} %collective-permute-done.8, ...), kind=kLoop, calls=%fused_computation.283 | loop fusion | flops 4874240 | bytes 2924544 | tf_op jit(solution)/shard_map/convert_element_type | solution.py:67
  147.6 26.3 %fusion.160 = f32[69,256]{1,0:T(8,128)S(1)} fusion(f32[64,69,24]{1,2,0:T(8,128)} %copy-done.13, f32[64,24,256]{2,1,0:T(8,128)} %get-tuple-element.65, f32[68,28,256]{2,1,0:T(8,128)} %maximum_convert_fusion.1, f32[256]{0:T(256)S(1)} %bitcast.333, f32[256]{0:T(256)S(1)} %bitcast.332, f32[256]{0:T(256)S(1)} %bitcast.331, f32[256]{0:T(256)S(1)} %bitcast.330, ...), kind=kOutput, calls=%fused_computation.280 | convolution fusion | flops 345243648 | bytes 41777152 | tf_op jit(solution)/shard_map/rvj,rjc->vc/dot_general | solution.py:159
  174.0 1.5 constant_dynamic-update-slice_fusion.7
  175.5 1.4 constant_dynamic-update-slice_fusion.6
  176.9 1.4 constant_dynamic-update-slice_fusion.5
  178.2 1.7 constant_dynamic-update-slice_fusion.4
  179.9 1.7 constant_dynamic-update-slice_fusion.3
  181.6 1.3 constant_dynamic-update-slice_fusion.2
  182.9 1.3 constant_dynamic-update-slice_fusion.1
  184.2 1.3 constant_dynamic-update-slice_fusion
  185.5 23.5 %all_to_all.15 = f32[128,1,1280]{2,1,0:T(1,128)S(1)} all-to-all(f32[128,1,1280]{2,1,0:T(1,128)} %bitcast.202), channel_id=1, replica_groups=mesh['lon'=32,'lat'=4] {'lon','lat'}, dimensions={0} | all-to-all | bytes 1310720 | tf_op jit(solution)/shard_map/all_to_all | solution.py:28
  209.7 18.8 %all_to_all.16 = f32[128,1,1280]{2,1,0:T(1,128)S(1)} all-to-all(f32[128,1,1280]{2,1,0:T(1,128)S(1)} %broadcast_in_dim.58), channel_id=1, replica_groups=mesh['lon'=32,'lat'=4] {'lon','lat'}, dimensions={0} | all-to-all | bytes 1310720 | tf_op jit(solution)/shard_map/all_to_all | solution.py:30
  228.5 0.8 copy-done.11
  229.4 2.5 %reduce.53 = f32[128,1280]{1,0:T(8,128)} reduce(f32[128,1,1280]{2,1,0:T(1,128)S(1)} %all_to_all.16, f32[]{:T(128)} %constant.72), dimensions={1}, to_apply=%all_to_all.12.reduce_sub_computation | reduce | bytes 1310724 | tf_op jit(solution)/shard_map/all_to_all | solution.py:30
  231.9 1.3 slice.1026
  233.2 0.6 slice_multiply_fusion.79
  233.8 0.6 slice_multiply_fusion.78
  234.4 0.8 slice_multiply_fusion.76
  235.3 1.3 slice_multiply_fusion.81
  (218 shorter events, 5.9 us)
Async XLA Ops:
  3.0 5.6 %copy-start.22 = (bf16[69,256]{1,0:T(8,128)(2,1)S(1)}, bf16[69,256]{1,0:T(8,128)(2,1)}, u32[]{:S(2)}) copy-start(bf16[69,256]{1,0:T(8,128)(2,1)} %param.12) | copy-start | bytes 105988
  8.6 9.5 %copy-start.20 = (bf16[25,256]{1,0:T(8,128)(2,1)S(1)}, bf16[25,256]{1,0:T(8,128)(2,1)}, u32[]{:S(2)}) copy-start(bf16[25,256]{1,0:T(8,128)(2,1)} %param.13) | copy-start | bytes 38404
  8.6 10.9 %copy-start.21 = (bf16[25,256]{1,0:T(8,128)(2,1)S(1)}, bf16[25,256]{1,0:T(8,128)(2,1)}, u32[]{:S(2)}) copy-start(bf16[25,256]{1,0:T(8,128)(2,1)} %param.16) | copy-start | bytes 38404
  10.1 12.1 %collective-permute-start = (bf16[64,4,256]{2,1,0:T(4,128)(2,1)}, bf16[64,4,256]{2,1,0:T(4,128)(2,1)S(1)}, u32[]{:S(2)}, u32[]{:S(2)}) collective-permute-start(bf16[64,4,256]{2,1,0:T(4,128)(2,1)} %get-tuple-element.87), channel_id=1, source_target_pairs={{0,4},{4,8},{8,12},{12,16},{16,20},{20,24},{24,28},{28,32},{32,36}... | collective-permute-start | bytes 393224 | tf_op jit(solution)/shard_map/ppermute | solution.py:14
  12.2 10.0 %collective-permute-start.1 = (bf16[64,4,256]{2,1,0:T(4,128)(2,1)S(1)}, bf16[64,4,256]{2,1,0:T(4,128)(2,1)S(1)}, u32[]{:S(2)}, u32[]{:S(2)}) collective-permute-start(bf16[64,4,256]{2,1,0:T(4,128)(2,1)S(1)} %get-tuple-element.88), channel_id=1, source_target_pairs={{4,0},{8,4},{12,8},{16,12},{20,16},{24,20},{28,24},{32,28},{36,32}... | collective-permute-start | bytes 393224 | tf_op jit(solution)/shard_map/ppermute | solution.py:15
  22.2 8.0 %collective-permute-start.2 = (bf16[4,32,256]{2,1,0:T(8,128)(2,1)S(1)}, bf16[4,32,256]{2,1,0:T(8,128)(2,1)S(1)}, u32[]{:S(2)}, u32[]{:S(2)}) collective-permute-start(bf16[4,32,256]{2,1,0:T(8,128)(2,1)S(1)} %get-tuple-element.77), channel_id=1, source_target_pairs={{0,1},{1,2},{2,3},{4,5},{5,6},{6,7},{8,9},{9,10},{10,11},{12,13},{... | collective-permute-start | bytes 196616 | tf_op jit(solution)/shard_map/ppermute | solution.py:14
  27.9 7.1 %collective-permute-start.3 = (bf16[4,32,256]{2,1,0:T(8,128)(2,1)S(1)}, bf16[4,32,256]{2,1,0:T(8,128)(2,1)S(1)}, u32[]{:S(2)}, u32[]{:S(2)}) collective-permute-start(bf16[4,32,256]{2,1,0:T(8,128)(2,1)S(1)} %get-tuple-element.78), channel_id=1, source_target_pairs={{1,0},{2,1},{3,2},{5,4},{6,5},{7,6},{9,8},{10,9},{11,10},{13,12},{... | collective-permute-start | bytes 196616 | tf_op jit(solution)/shard_map/ppermute | solution.py:15
  30.0 5.5 %copy-start.58 = (f32[1,256]{1,0:T(1,128)S(1)}, f32[1,256]{1,0:T(1,128)}, u32[]{:S(2)}) copy-start(f32[1,256]{1,0:T(1,128)} %get-tuple-element.176) | copy-start | bytes 3076
  30.0 5.5 %copy-start.59 = (f32[1,256]{1,0:T(1,128)S(1)}, f32[1,256]{1,0:T(1,128)}, u32[]{:S(2)}) copy-start(f32[1,256]{1,0:T(1,128)} %get-tuple-element.177) | copy-start | bytes 3076
  30.0 5.5 %copy-start.60 = (f32[1,256]{1,0:T(1,128)S(1)}, f32[1,256]{1,0:T(1,128)}, u32[]{:S(2)}) copy-start(f32[1,256]{1,0:T(1,128)} %get-tuple-element.178) | copy-start | bytes 3076
  30.1 5.5 %copy-start.61 = (f32[1,256]{1,0:T(1,128)S(1)}, f32[1,256]{1,0:T(1,128)}, u32[]{:S(2)}) copy-start(f32[1,256]{1,0:T(1,128)} %get-tuple-element.179) | copy-start | bytes 3076
  30.1 5.5 %copy-start.62 = (f32[1,256]{1,0:T(1,128)S(1)}, f32[1,256]{1,0:T(1,128)}, u32[]{:S(2)}) copy-start(f32[1,256]{1,0:T(1,128)} %get-tuple-element.180) | copy-start | bytes 3076
  30.1 5.5 %copy-start.63 = (f32[1,256]{1,0:T(1,128)S(1)}, f32[1,256]{1,0:T(1,128)}, u32[]{:S(2)}) copy-start(f32[1,256]{1,0:T(1,128)} %get-tuple-element.181) | copy-start | bytes 3076
  30.1 5.5 %copy-start.64 = (f32[1,256]{1,0:T(1,128)S(1)}, f32[1,256]{1,0:T(1,128)}, u32[]{:S(2)}) copy-start(f32[1,256]{1,0:T(1,128)} %get-tuple-element.182) | copy-start | bytes 3076
  30.1 5.5 %copy-start.65 = (f32[1,256]{1,0:T(1,128)S(1)}, f32[1,256]{1,0:T(1,128)}, u32[]{:S(2)}) copy-start(f32[1,256]{1,0:T(1,128)} %get-tuple-element.183) | copy-start | bytes 3076
  30.1 5.5 %copy-start.66 = (f32[1,256]{1,0:T(1,128)S(1)}, f32[1,256]{1,0:T(1,128)}, u32[]{:S(2)}) copy-start(f32[1,256]{1,0:T(1,128)} %get-tuple-element.184) | copy-start | bytes 3076
  30.1 5.5 %copy-start.67 = (f32[1,256]{1,0:T(1,128)S(1)}, f32[1,256]{1,0:T(1,128)}, u32[]{:S(2)}) copy-start(f32[1,256]{1,0:T(1,128)} %get-tuple-element.185) | copy-start | bytes 3076
  30.1 5.5 %copy-start.68 = (f32[1,256]{1,0:T(1,128)S(1)}, f32[1,256]{1,0:T(1,128)}, u32[]{:S(2)}) copy-start(f32[1,256]{1,0:T(1,128)} %get-tuple-element.186) | copy-start | bytes 3076
  30.1 5.5 %copy-start.69 = (f32[1,256]{1,0:T(1,128)S(1)}, f32[1,256]{1,0:T(1,128)}, u32[]{:S(2)}) copy-start(f32[1,256]{1,0:T(1,128)} %get-tuple-element.187) | copy-start | bytes 3076
  30.2 5.5 %copy-start.70 = (f32[1,256]{1,0:T(1,128)S(1)}, f32[1,256]{1,0:T(1,128)}, u32[]{:S(2)}) copy-start(f32[1,256]{1,0:T(1,128)} %get-tuple-element.188) | copy-start | bytes 3076
  30.2 5.5 %copy-start.71 = (f32[1,256]{1,0:T(1,128)S(1)}, f32[1,256]{1,0:T(1,128)}, u32[]{:S(2)}) copy-start(f32[1,256]{1,0:T(1,128)} %get-tuple-element.189) | copy-start | bytes 3076
  30.2 5.5 %copy-start.72 = (f32[1,256]{1,0:T(1,128)S(1)}, f32[1,256]{1,0:T(1,128)}, u32[]{:S(2)}) copy-start(f32[1,256]{1,0:T(1,128)} %get-tuple-element.190) | copy-start | bytes 3076
  30.2 5.5 %copy-start.73 = (f32[1,256]{1,0:T(1,128)S(1)}, f32[1,256]{1,0:T(1,128)}, u32[]{:S(2)}) copy-start(f32[1,256]{1,0:T(1,128)} %get-tuple-element.191) | copy-start | bytes 3076
  30.2 5.5 %copy-start.74 = (f32[1,256]{1,0:T(1,128)S(1)}, f32[1,256]{1,0:T(1,128)}, u32[]{:S(2)}) copy-start(f32[1,256]{1,0:T(1,128)} %get-tuple-element.192) | copy-start | bytes 3076
  30.2 5.5 %copy-start.75 = (f32[1,256]{1,0:T(1,128)S(1)}, f32[1,256]{1,0:T(1,128)}, u32[]{:S(2)}) copy-start(f32[1,256]{1,0:T(1,128)} %get-tuple-element.193) | copy-start | bytes 3076
  30.2 5.5 %copy-start.76 = (f32[1,256]{1,0:T(1,128)S(1)}, f32[1,256]{1,0:T(1,128)}, u32[]{:S(2)}) copy-start(f32[1,256]{1,0:T(1,128)} %get-tuple-element.194) | copy-start | bytes 3076
  35.8 7.0 %copy-start.32 = (f32[256]{0:T(256)S(1)}, f32[256]{0:T(256)}, u32[]{:S(2)}) copy-start(f32[256]{0:T(256)} %param.14) | copy-start | bytes 3076
  48.9 6.1 %copy-start.16 = (bf16[256,256]{1,0:T(8,128)(2,1)S(1)}, bf16[256,256]{1,0:T(8,128)(2,1)}, u32[]{:S(2)}) copy-start(bf16[256,256]{1,0:T(8,128)(2,1)} %param.18) | copy-start | bytes 393220
  48.9 6.1 %copy-start.31 = (f32[256]{0:T(256)S(1)}, f32[256]{0:T(256)}, u32[]{:S(2)}) copy-start(f32[256]{0:T(256)} %param.17) | copy-start | bytes 3076
  55.1 4.1 %copy-start.6 = (f32[64,24,256]{2,1,0:T(8,128)S(1)}, f32[64,24,256]{2,1,0:T(8,128)}, u32[]{:S(2)}) copy-start(f32[64,24,256]{2,1,0:T(8,128)} %get-tuple-element.67) | copy-start | bytes 4718596
  65.2 9.5 %copy-start.7 = (bf16[64,24,256]{2,1,0:T(8,128)(2,1)}, bf16[64,24,256]{2,1,0:T(8,128)(2,1)S(1)}, u32[]{:S(2)}) copy-start(bf16[64,24,256]{2,1,0:T(8,128)(2,1)S(1)} %get-tuple-element.62) | copy-start | bytes 2359300
  67.1 7.6 %collective-permute-start.4 = (bf16[64,2,256]{2,1,0:T(2,128)(2,1)S(1)}, bf16[64,2,256]{2,1,0:T(2,128)(2,1)S(1)}, u32[]{:S(2)}, u32[]{:S(2)}) collective-permute-start(bf16[64,2,256]{2,1,0:T(2,128)(2,1)S(1)} %get-tuple-element.85), channel_id=1, source_target_pairs={{0,4},{4,8},{8,12},{12,16},{16,20},{20,24},{24,28},{28,32},{32,36}... | collective-permute-start | bytes 196616 | tf_op jit(solution)/shard_map/ppermute | solution.py:14
  67.4 7.3 %collective-permute-start.5 = (bf16[64,2,256]{2,1,0:T(2,128)(2,1)S(1)}, bf16[64,2,256]{2,1,0:T(2,128)(2,1)S(1)}, u32[]{:S(2)}, u32[]{:S(2)}) collective-permute-start(bf16[64,2,256]{2,1,0:T(2,128)(2,1)S(1)} %get-tuple-element.86), channel_id=1, source_target_pairs={{4,0},{8,4},{12,8},{16,12},{20,16},{24,20},{28,24},{32,28},{36,32}... | collective-permute-start | bytes 196616 | tf_op jit(solution)/shard_map/ppermute | solution.py:15
  73.1 7.3 %copy-start.3 = (f32[68,28,256]{2,0,1:T(8,128)S(1)}, f32[68,28,256]{2,0,1:T(8,128)}, u32[]{:S(2)}) copy-start(f32[68,28,256]{2,0,1:T(8,128)} %copy-done.2) | copy-start | bytes 5849092
  75.4 10.8 %collective-permute-start.6 = (bf16[2,28,256]{2,1,0:T(8,128)(2,1)}, bf16[2,28,256]{2,1,0:T(8,128)(2,1)}, u32[]{:S(2)}, u32[]{:S(2)}) collective-permute-start(bf16[2,28,256]{2,1,0:T(8,128)(2,1)} %get-tuple-element.81), channel_id=1, source_target_pairs={{0,1},{1,2},{2,3},{4,5},{5,6},{6,7},{8,9},{9,10},{10,11},{12,13},{... | collective-permute-start | bytes 86024 | tf_op jit(solution)/shard_map/ppermute | solution.py:14
  78.4 7.7 %collective-permute-start.7 = (bf16[2,28,256]{2,1,0:T(8,128)(2,1)}, bf16[2,28,256]{2,1,0:T(8,128)(2,1)}, u32[]{:S(2)}, u32[]{:S(2)}) collective-permute-start(bf16[2,28,256]{2,1,0:T(8,128)(2,1)} %get-tuple-element.82), channel_id=1, source_target_pairs={{1,0},{2,1},{3,2},{5,4},{6,5},{7,6},{9,8},{10,9},{11,10},{13,12},{... | collective-permute-start | bytes 86024 | tf_op jit(solution)/shard_map/ppermute | solution.py:15
  80.5 5.7 %copy-start.8 = (bf16[64,24,256]{2,1,0:T(8,128)(2,1)S(1)}, bf16[64,24,256]{2,1,0:T(8,128)(2,1)}, u32[]{:S(2)}) copy-start(bf16[64,24,256]{2,1,0:T(8,128)(2,1)} %copy-done.7) | copy-start | bytes 2359300
  88.9 26.1 %copy-start.18 = (bf16[256,256]{1,0:T(8,128)(2,1)S(1)}, bf16[256,256]{1,0:T(8,128)(2,1)}, u32[]{:S(2)}) copy-start(bf16[256,256]{1,0:T(8,128)(2,1)} %param.15) | copy-start | bytes 393220
  123.4 8.0 %collective-permute-start.8 = (bf16[64,2,256]{2,1,0:T(2,128)(2,1)S(1)}, bf16[64,2,256]{2,1,0:T(2,128)(2,1)S(1)}, u32[]{:S(2)}, u32[]{:S(2)}) collective-permute-start(bf16[64,2,256]{2,1,0:T(2,128)(2,1)S(1)} %get-tuple-element.83), channel_id=1, source_target_pairs={{0,4},{4,8},{8,12},{12,16},{16,20},{20,24},{24,28},{28,32},{32,36}... | collective-permute-start | bytes 196616 | tf_op jit(solution)/shard_map/ppermute | solution.py:14
  123.4 16.5 %copy-start.10 = (bf16[68,28,256]{2,1,0:T(8,128)(2,1)S(1)}, bf16[68,28,256]{2,1,0:T(8,128)(2,1)}, u32[]{:S(2)}) copy-start(bf16[68,28,256]{2,1,0:T(8,128)(2,1)} %copy-done.9) | copy-start | bytes 2924548
  123.5 16.5 %copy-start.15 = (bf16[64,24,256]{2,1,0:T(8,128)(2,1)S(1)}, bf16[64,24,256]{2,1,0:T(8,128)(2,1)}, u32[]{:S(2)}) copy-start(bf16[64,24,256]{2,1,0:T(8,128)(2,1)} %copy-done.14) | copy-start | bytes 2359300
  123.5 7.9 %collective-permute-start.9 = (bf16[64,2,256]{2,1,0:T(2,128)(2,1)S(1)}, bf16[64,2,256]{2,1,0:T(2,128)(2,1)S(1)}, u32[]{:S(2)}, u32[]{:S(2)}) collective-permute-start(bf16[64,2,256]{2,1,0:T(2,128)(2,1)S(1)} %get-tuple-element.84), channel_id=1, source_target_pairs={{4,0},{8,4},{12,8},{16,12},{20,16},{24,20},{28,24},{32,28},{36,32}... | collective-permute-start | bytes 196616 | tf_op jit(solution)/shard_map/ppermute | solution.py:15
  132.0 11.6 %collective-permute-start.10 = (bf16[2,28,256]{2,1,0:T(8,128)(2,1)}, bf16[2,28,256]{2,1,0:T(8,128)(2,1)S(1)}, u32[]{:S(2)}, u32[]{:S(2)}) collective-permute-start(bf16[2,28,256]{2,1,0:T(8,128)(2,1)} %get-tuple-element.79), channel_id=1, source_target_pairs={{0,1},{1,2},{2,3},{4,5},{5,6},{6,7},{8,9},{9,10},{10,11},{12,13},{... | collective-permute-start | bytes 86024 | tf_op jit(solution)/shard_map/ppermute | solution.py:14
  137.7 3.5 %copy-start.34 = (f32[256]{0:T(256)S(1)}, f32[256]{0:T(256)}, u32[]{:S(2)}) copy-start(f32[256]{0:T(256)} %get-tuple-element.41) | copy-start | bytes 3076
  137.7 3.5 %copy-start.35 = (f32[256]{0:T(256)S(1)}, f32[256]{0:T(256)}, u32[]{:S(2)}) copy-start(f32[256]{0:T(256)} %get-tuple-element.42) | copy-start | bytes 3076
  137.7 3.5 %copy-start.36 = (f32[256]{0:T(256)S(1)}, f32[256]{0:T(256)}, u32[]{:S(2)}) copy-start(f32[256]{0:T(256)} %get-tuple-element.43) | copy-start | bytes 3076
  137.8 7.1 %collective-permute-start.11 = (bf16[2,28,256]{2,1,0:T(8,128)(2,1)}, bf16[2,28,256]{2,1,0:T(8,128)(2,1)}, u32[]{:S(2)}, u32[]{:S(2)}) collective-permute-start(bf16[2,28,256]{2,1,0:T(8,128)(2,1)} %get-tuple-element.80), channel_id=1, source_target_pairs={{1,0},{2,1},{3,2},{5,4},{6,5},{7,6},{9,8},{10,9},{11,10},{13,12},{... | collective-permute-start | bytes 86024 | tf_op jit(solution)/shard_map/ppermute | solution.py:15
  143.5 4.0 %copy-start.78 = (f32[1,256]{1,0:T(1,128)S(1)}, f32[1,256]{1,0:T(1,128)}, u32[]{:S(2)}) copy-start(f32[1,256]{1,0:T(1,128)} %get-tuple-element.120) | copy-start | bytes 3076
  143.5 4.0 %copy-start.79 = (f32[1,256]{1,0:T(1,128)S(1)}, f32[1,256]{1,0:T(1,128)}, u32[]{:S(2)}) copy-start(f32[1,256]{1,0:T(1,128)} %get-tuple-element.121) | copy-start | bytes 3076
  143.5 4.0 %copy-start.80 = (f32[1,256]{1,0:T(1,128)S(1)}, f32[1,256]{1,0:T(1,128)}, u32[]{:S(2)}) copy-start(f32[1,256]{1,0:T(1,128)} %get-tuple-element.122) | copy-start | bytes 3076
  143.5 4.0 %copy-start.81 = (f32[1,256]{1,0:T(1,128)S(1)}, f32[1,256]{1,0:T(1,128)}, u32[]{:S(2)}) copy-start(f32[1,256]{1,0:T(1,128)} %get-tuple-element.123) | copy-start | bytes 3076
  143.5 4.0 %copy-start.82 = (f32[1,256]{1,0:T(1,128)S(1)}, f32[1,256]{1,0:T(1,128)}, u32[]{:S(2)}) copy-start(f32[1,256]{1,0:T(1,128)} %get-tuple-element.124) | copy-start | bytes 3076
  143.5 4.0 %copy-start.83 = (f32[1,256]{1,0:T(1,128)S(1)}, f32[1,256]{1,0:T(1,128)}, u32[]{:S(2)}) copy-start(f32[1,256]{1,0:T(1,128)} %get-tuple-element.125) | copy-start | bytes 3076
  143.5 4.0 %copy-start.84 = (f32[1,256]{1,0:T(1,128)S(1)}, f32[1,256]{1,0:T(1,128)}, u32[]{:S(2)}) copy-start(f32[1,256]{1,0:T(1,128)} %get-tuple-element.101) | copy-start | bytes 3076
  143.5 4.0 %copy-start.85 = (f32[1,256]{1,0:T(1,128)S(1)}, f32[1,256]{1,0:T(1,128)}, u32[]{:S(2)}) copy-start(f32[1,256]{1,0:T(1,128)} %get-tuple-element.102) | copy-start | bytes 3076
  143.5 4.0 %copy-start.86 = (f32[1,256]{1,0:T(1,128)S(1)}, f32[1,256]{1,0:T(1,128)}, u32[]{:S(2)}) copy-start(f32[1,256]{1,0:T(1,128)} %get-tuple-element.103) | copy-start | bytes 3076
  143.5 4.0 %copy-start.87 = (f32[1,256]{1,0:T(1,128)S(1)}, f32[1,256]{1,0:T(1,128)}, u32[]{:S(2)}) copy-start(f32[1,256]{1,0:T(1,128)} %get-tuple-element.104) | copy-start | bytes 3076
  143.5 4.0 %copy-start.88 = (f32[1,256]{1,0:T(1,128)S(1)}, f32[1,256]{1,0:T(1,128)}, u32[]{:S(2)}) copy-start(f32[1,256]{1,0:T(1,128)} %get-tuple-element.105) | copy-start | bytes 3076
  143.6 4.0 %copy-start.89 = (f32[1,256]{1,0:T(1,128)S(1)}, f32[1,256]{1,0:T(1,128)}, u32[]{:S(2)}) copy-start(f32[1,256]{1,0:T(1,128)} %get-tuple-element.106) | copy-start | bytes 3076
  143.6 4.0 %copy-start.90 = (f32[1,256]{1,0:T(1,128)S(1)}, f32[1,256]{1,0:T(1,128)}, u32[]{:S(2)}) copy-start(f32[1,256]{1,0:T(1,128)} %get-tuple-element.107) | copy-start | bytes 3076
  147.6 29.3 %copy-start.19 = (f32[6400]{0:T(1024)S(1)}, f32[6400]{0:T(1024)}, u32[]{:S(2)}) copy-start(f32[6400]{0:T(1024)} %reshape.476) | copy-start | bytes 76804
  147.6 30.6 %copy-start.12 = (f32[32,2,8,128]{3,1,2,0:T(2,128)S(1)}, f32[32,2,8,128]{3,1,2,0:T(2,128)}, u32[]{:S(2)}) copy-start(f32[32,2,8,128]{3,1,2,0:T(2,128)} %copy.52) | copy-start | bytes 786436
  147.6 34.0 %copy-start.91 = (f32[256]{0:T(256)S(1)}, f32[256]{0:T(256)}, u32[]{:S(2)}) copy-start(f32[256]{0:T(256)} %get-tuple-element.8) | copy-start | bytes 3076
  147.6 35.3 %copy-start.77 = (f32[256]{0:T(256)S(1)}, f32[256]{0:T(256)}, u32[]{:S(2)}) copy-start(f32[256]{0:T(256)} %get-tuple-element.10) | copy-start | bytes 3076
  (40 other events, 118.4 us)

commit v2 on v0

v2 whole, which is shorter than its diff:
```python
import functools

import jax
import jax.numpy as jnp
from jax import lax
from jax.experimental import pallas as pl
from jax.experimental.pallas import tpu as pltpu
from jax.sharding import PartitionSpec as P

F32 = jnp.float32
BF16 = jnp.bfloat16
ROWS = 64
COLS = 24
HALO = 8
PITCH = COLS + 2 * HALO
TALL = ROWS + 2 * HALO
LEAD = 16
FLAT = LEAD + PITCH * TALL + 16
CHANS = 256
VARS = 69
TILES = 128
AXES = ("lon", "lat")


def regrid_kernel(row_len, sector, points, w_embed, h0, left, right, regridded, *, lon_total):
    step = pl.program_id(0)
    first = sector[0] * COLS
    cell = first.astype(F32) + lax.broadcasted_iota(jnp.int32, (COLS, 163), 0).astype(F32)
    mark = lax.broadcasted_iota(jnp.int32, (COLS, 163), 1).astype(F32)
    weight = w_embed[...]
    for group in range(points.shape[0] // 4):
        found = []
        for k in range(4):
            local = 4 * group + k
            count = row_len[step * points.shape[0] + local]
            start = (first * count // lon_total).astype(F32)
            product = cell * count.astype(F32)
            lower = jnp.floor((product + 2.0) * (1.0 / lon_total))
            share = (product - lower * lon_total) * 0.25
            away = mark - (lower - start)
            whole = lon_total // 4
            mix = jnp.where(away == 0.0, whole - share, jnp.where(away == 1.0, share, 0.0))
            found.append(
                lax.dot_general(
                    mix.astype(BF16),
                    points[local],
                    (((1,), (1,)), ((), ())),
                    preferred_element_type=F32,
                )
            )
        values = jnp.concatenate(found, 0) * (4.0 / lon_total)
        high = values.astype(BF16)
        low = (values - high.astype(F32)).astype(BF16)
        field = jnp.dot(high, weight, preferred_element_type=F32) + jnp.dot(
            low, weight, preferred_element_type=F32
        )
        field = field.reshape(4, COLS, CHANS).astype(BF16)
        rows = slice(4 * group, 4 * group + 4)
        h0[rows] = field
        left[rows] = field[:, :HALO]
        right[rows] = field[:, COLS - HALO :]
        regridded[slice(4 * COLS * group, 4 * COLS * (group + 1)), :VARS] = high


def regrid_embed(points, row_len, w_embed, lon_total):
    steps = 4
    rows = ROWS // steps
    slots = points.shape[2]
    return pl.pallas_call(
        functools.partial(regrid_kernel, lon_total=lon_total),
        grid_spec=pltpu.PrefetchScalarGridSpec(
            num_scalar_prefetch=2,
            grid=(steps,),
            in_specs=[
                pl.BlockSpec((rows, VARS, slots), lambda i, *_: (i, 0, 0)),
                pl.BlockSpec((VARS, CHANS), lambda i, *_: (0, 0)),
            ],
            out_specs=[
                pl.BlockSpec((rows, COLS, CHANS), lambda i, *_: (i, 0, 0)),
                pl.BlockSpec((rows, HALO, CHANS), lambda i, *_: (i, 0, 0)),
                pl.BlockSpec((rows, HALO, CHANS), lambda i, *_: (i, 0, 0)),
                pl.BlockSpec((rows * COLS, 128), lambda i, *_: (i, 0)),
            ],
        ),
        out_shape=[
            jax.ShapeDtypeStruct((ROWS, COLS, CHANS), BF16),
            jax.ShapeDtypeStruct((ROWS, HALO, CHANS), BF16),
            jax.ShapeDtypeStruct((ROWS, HALO, CHANS), BF16),
            jax.ShapeDtypeStruct((ROWS * COLS, 128), BF16),
        ],
        name="regrid_embed",
    )(row_len, jnp.reshape(lax.axis_index("lon"), (1,)).astype(jnp.int32), points, w_embed)


def at(row):
    return LEAD + PITCH * row


def conv(source, half, start, rows, cols, taps, visit=None):
    sums = [None] * rows
    for e in range(5):
        weights = [taps[half, 5 * a + e] for a in range(5)]
        for i in range(rows + 4):
            x = source[half, pl.ds(start + PITCH * (i - 2) + e - 2, cols), :]
            x = x.reshape(cols // 8, 8, 128)
            for a in range(5):
                r = i - a
                if 0 <= r < rows:
                    term = x * weights[a]
                    sums[r] = term if sums[r] is None else sums[r] + term
                    if visit is not None:
                        visit(a, e, r, x)
        if visit is not None:
            visit(None, e, None, None)
    return sums


class TapSums:
    def __init__(self, store, half, centre):
        self.store, self.half, self.centre, self.live = store, half, centre, {}

    def __call__(self, a, e, r, x):
        if a is None:
            for tap, value in self.live.items():
                self.store[self.half, tap] += value
            self.live = {}
            return
        tap = 24 - (5 * a + e)
        if x.shape[0] == 5:
            x = x[1:4]
        term = jnp.sum(self.centre[r] * x, 0)
        self.live[tap] = term if tap not in self.live else self.live[tap] + term


def local_part(x, rows):
    return x.reshape(rows, PITCH, x.shape[-1])[:, HALO : HALO + COLS].reshape(
        rows * COLS, x.shape[-1]
    )


def blocks_kernel(
    lat, h0, left, right, above, below, cot, cot_left, cot_right,
    kernel1, gain1, point1, kernel2, gain2, point2, regridded,
    out, packed,
    x0, cots, d, h1, xhat1, scale1, slope1, dd2, g1, dd1,
    taps1, taps2, flip1, flip2, turned1, turned2,
    u1, dp1, u2, dp2, g0, gk1, gk2, gg1, gg2,
    *, lat_devices,
):
    halves = (slice(0, 128), slice(128, 256))

    for k in range(25):
        for h in (0, 1):
            one = jnp.broadcast_to(kernel1[k : k + 1, halves[h]].astype(F32), (8, 128))
            two = jnp.broadcast_to(kernel2[k : k + 1, halves[h]].astype(F32), (8, 128))
            taps1[h, k] = one
            flip1[h, 24 - k] = one
            taps2[h, k] = two
            flip2[h, 24 - k] = two
    turned1[...] = jnp.transpose(point1[...].astype(F32)).astype(BF16)
    turned2[...] = jnp.transpose(point2[...].astype(F32)).astype(BF16)
    zeros = jnp.zeros((8, 128), F32)
    for h in (0, 1):
        for ref in (gg1, gg2):
            ref[h] = zeros
        for ref in (gk1, gk2):
            ref[h] = jnp.zeros((25, 8, 128), F32)
        for ref in (x0, cots, h1, dd2, dd1):
            ref[h, 0:LEAD] = jnp.zeros((LEAD, 128), F32)
            ref[h, FLAT - 16 : FLAT] = jnp.zeros((16, 128), F32)

    def put(ref, row, value):
        for h in (0, 1):
            ref[h, pl.ds(pl.multiple_of(at(row), 8), PITCH), :] = value[:, halves[h]]

    def fill(pair, carry):
        sides = [cot_left[pair].astype(F32), cot_right[pair].astype(F32)]
        swapped = [pltpu.roll(s, 4, 0) for s in sides]
        for odd in (0, 1):
            row = 2 * pair + odd
            field = [left[row].astype(F32), h0[row].astype(F32), right[row].astype(F32)]
            put(x0, row + HALO, jnp.concatenate(field, 0))
            west = sides[0] if odd else swapped[0]
            east = swapped[1] if odd else sides[1]
            put(cots, row + HALO, jnp.concatenate([west, cot[row].astype(F32), east], 0))
        return carry

    lax.fori_loop(0, ROWS // 2, fill, 0)
    for k in range(HALO):
        put(x0, k, above[k].astype(F32))
        put(x0, k + HALO + ROWS, below[k].astype(F32))
    for k in range(4):
        put(cots, k + 4, above[k + HALO].astype(F32))
        put(cots, k + HALO + ROWS, below[k + HALO].astype(F32))

    def get(ref, start, rows):
        return [ref[h, pl.ds(pl.multiple_of(start, 8), rows * PITCH), :] for h in (0, 1)]

    def keep(ref, start, rows, values):
        for h in (0, 1):
            ref[h, pl.ds(pl.multiple_of(start, 8), rows * PITCH), :] = values[h]

    def plain_conv(source, taps, target, start, rows):
        for h in (0, 1):
            sums = conv(source, h, start, rows, PITCH, taps)
            flat = jnp.concatenate(sums, 0).reshape(rows * PITCH, 128)
            target[h, pl.ds(pl.multiple_of(start, 8), rows * PITCH), :] = flat

    def gains(ref):
        return [ref[:, halves[h]] for h in (0, 1)]

    def normalised(start, rows):
        raw = get(d, start, rows)
        mean = jnp.sum(raw[0] * raw[0] + raw[1] * raw[1], -1, keepdims=True) * (1.0 / CHANS)
        scale = lax.rsqrt(mean + 1e-06)
        return scale, [raw[h] * scale for h in (0, 1)]

    def activated(xhat, gain, point):
        u = [xhat[h] * gain[h] for h in (0, 1)]
        p = jnp.dot(
            jnp.concatenate(u, 1).astype(BF16), point[...], preferred_element_type=F32
        )
        p = [p[:, s] for s in halves]
        sig = [0.5 * jnp.tanh(0.5 * v) + 0.5 for v in p]
        silu = [p[h] * sig[h] for h in (0, 1)]
        slope = [sig[h] + silu[h] * (1.0 - sig[h]) for h in (0, 1)]
        return u, silu, slope

    def through_norm(grad, slope, xhat, scale, gain, turned):
        dp = [grad[h] * slope[h] for h in (0, 1)]
        du = jnp.dot(
            jnp.concatenate(dp, 1).astype(BF16), turned[...], preferred_element_type=F32
        )
        du = [du[:, s] for s in halves]
        gained = [du[h] * gain[h] for h in (0, 1)]
        mean = jnp.sum(gained[0] * xhat[0] + gained[1] * xhat[1], -1, keepdims=True) * (
            1.0 / CHANS
        )
        dd = [
            (scale * (gained[h] - xhat[h] * mean)).astype(BF16).astype(F32) for h in (0, 1)
        ]
        return dp, du, dd

    def gain_sums(store, du, xhat, rows):
        for h in (0, 1):
            terms = local_part(du[h] * xhat[h], rows).reshape(-1, 8, 128)
            store[h] += jnp.sum(terms, 0)

    def pipeline(blocks, first, second):
        first(0)

        def step(i, carry):
            second(i - 1)
            first(i)
            return carry

        lax.fori_loop(1, blocks, step, 0)
        second(blocks - 1)

    size = 4 * PITCH

    def first_conv(i):
        plain_conv(x0, taps1, d, at(2) + i * size, 4)

    def first_mix(i):
        start = at(2) + i * size
        scale, xhat = normalised(start, 4)
        _, silu, slope = activated(xhat, gains(gain1), point1)
        x = get(x0, start, 4)
        keep(h1, start, 4, [(x[h] + silu[h]).astype(BF16).astype(F32) for h in (0, 1)])
        keep(xhat1, start, 4, xhat)
        keep(slope1, start, 4, slope)
        scale1[pl.ds(pl.multiple_of(start, 8), size), :] = jnp.broadcast_to(scale, (size, 128))

    pipeline((TALL - 4) // 4, first_conv, first_mix)

    def clear(ref, row, rows):
        for h in (0, 1):
            ref[h, at(row) : at(row + rows)] = jnp.zeros((rows * PITCH, 128), F32)

    @pl.when(lat[0] == 0)
    def _():
        clear(h1, 2, 6)

    @pl.when(lat[0] == lat_devices - 1)
    def _():
        clear(h1, HALO + ROWS, 6)

    def second_conv(start):
        plain_conv(h1, taps2, d, start, 4)

    def second_mix(start, local):
        scale, xhat = normalised(start, 4)
        gain = gains(gain2)
        u, silu, slope = activated(xhat, gain, point2)
        dp, du, dd = through_norm(get(cots, start, 4), slope, xhat, scale, gain, turned2)
        keep(dd2, start, 4, dd)
        if local is not None:
            x = get(h1, start, 4)
            result = [local_part(x[h] + silu[h], 4) for h in (0, 1)]
            out[pl.ds(local * 4, 4)] = (
                jnp.concatenate(result, 1).reshape(4, COLS, CHANS).astype(BF16)
            )
            spot = pl.ds(pl.multiple_of(local * 96, 96), 96)
            u2[spot] = jnp.concatenate([local_part(v, 4) for v in u], 1).astype(BF16)
            dp2[spot] = jnp.concatenate([local_part(v, 4) for v in dp], 1).astype(BF16)
            gain_sums(gg2, du, xhat, 4)

    def outer(k, carry):
        start = at(4) + k * PITCH * (ROWS + 4)
        second_conv(start)
        second_mix(start, None)
        return carry

    lax.fori_loop(0, 2, outer, 0)
    pipeline(
        ROWS // 4,
        lambda i: second_conv(at(HALO) + i * size),
        lambda i: second_mix(at(HALO) + i * size, i),
    )

    def third_conv(start, rows, local):
        for h in (0, 1):
            visit = None
            if local:
                centre = [
                    h1[h, pl.ds(pl.multiple_of(start + PITCH * r + HALO, 8), COLS), :].reshape(
                        3, 8, 128
                    )
                    for r in range(rows)
                ]
                visit = TapSums(gk2, h, centre)
            sums = conv(dd2, h, start, rows, PITCH, flip2, visit)
            spot = pl.ds(pl.multiple_of(start, 8), rows * PITCH)
            flat = jnp.concatenate(sums, 0).reshape(rows * PITCH, 128)
            g1[h, spot, :] = flat + cots[h, spot, :]

    def third_mix(start, rows, local):
        gain = gains(gain1)
        xhat = get(xhat1, start, rows)
        spot = pl.ds(pl.multiple_of(start, 8), rows * PITCH)
        dp, du, dd = through_norm(
            get(g1, start, rows), get(slope1, start, rows), xhat, scale1[spot], gain, turned1
        )
        keep(dd1, start, rows, dd)
        if local is not None:
            spot = pl.ds(pl.multiple_of(local * 96, 96), 96)
            u = [local_part(xhat[h] * gain[h], 4) for h in (0, 1)]
            u1[spot] = jnp.concatenate(u, 1).astype(BF16)
            dp1[spot] = jnp.concatenate([local_part(v, 4) for v in dp], 1).astype(BF16)
            gain_sums(gg1, du, xhat, 4)

    def margin(k, carry):
        start = at(6) + k * PITCH * (ROWS + 2)
        third_conv(start, 2, False)
        third_mix(start, 2, None)
        return carry

    lax.fori_loop(0, 2, margin, 0)
    pipeline(
        ROWS // 4,
        lambda i: third_conv(at(HALO) + i * size, 4, True),
        lambda i: third_mix(at(HALO) + i * size, 4, i),
    )

    @pl.when(lat[0] == 0)
    def _():
        clear(dd1, 6, 2)

    @pl.when(lat[0] == lat_devices - 1)
    def _():
        clear(dd1, HALO + ROWS, 2)

    def fourth_conv(i, carry):
        start = at(HALO) + i * size + HALO
        total = []
        for h in (0, 1):
            centre = [
                x0[h, pl.ds(pl.multiple_of(start + PITCH * r, 8), COLS), :].reshape(3, 8, 128)
                for r in range(4)
            ]
            sums = conv(dd1, h, start, 4, COLS, flip1, TapSums(gk1, h, centre))
            base = [
                g1[h, pl.ds(pl.multiple_of(start + PITCH * r, 8), COLS), :] for r in range(4)
            ]
            total.append(
                jnp.concatenate([sums[r].reshape(COLS, 128) + base[r] for r in range(4)], 0)
            )
        g0[pl.ds(pl.multiple_of(i * 96, 96), 96)] = jnp.concatenate(total, 1).astype(BF16)
        return carry

    lax.fori_loop(0, ROWS // 4, fourth_conv, 0)

    def across(a, b):
        return lax.dot_general(
            a, b, (((0,), (0,)), ((), ())), preferred_element_type=F32
        )

    def pack(place, value):
        rows = value.shape[0]
        for h in (0, 1):
            packed[place : place + rows // 8, h] = value[:, halves[h]].reshape(rows // 8, 8, 128)

    pack(0, across(u1[...], dp1[...]))
    pack(32, across(u2[...], dp2[...]))
    embed = across(regridded[:, :VARS], g0[...])

    def tidy(ref, rows):
        return [jnp.sum(ref[h], -2) for h in (0, 1)]

    top1 = [jnp.sum(gg1[h], 0, keepdims=True) for h in (0, 1)]
    top2 = [jnp.sum(gg2[h], 0, keepdims=True) for h in (0, 1)]
    gain_rows = jnp.concatenate(
        [jnp.concatenate(top1, 1), jnp.concatenate(top2, 1), jnp.zeros((1, CHANS), F32)], 0
    )
    pack(64, jnp.concatenate([embed, gain_rows], 0))
    for place, ref in ((73, gk1), (77, gk2)):
        both = jnp.concatenate([jnp.sum(ref[h], 1) for h in (0, 1)], 1)
        pack(place, jnp.concatenate([both, jnp.zeros((7, CHANS), F32)], 0))
    packed[81:TILES] = jnp.zeros((TILES - 81, 2, 8, 128), F32)


def blocks(fields, weights, regridded, lat_devices):
    wide = pltpu.VMEM((2, FLAT, 128), F32)
    taps = pltpu.VMEM((2, 25, 8, 128), F32)
    square = pltpu.VMEM((CHANS, CHANS), BF16)
    local = pltpu.VMEM((ROWS * COLS, CHANS), BF16)
    eight = pltpu.VMEM((2, 8, 128), F32)
    lat = jnp.reshape(lax.axis_index("lat"), (1,)).astype(jnp.int32)
    operands = (*fields, *weights, regridded)
    vmem = pl.BlockSpec(memory_space=pltpu.VMEM)
    return pl.pallas_call(
        functools.partial(blocks_kernel, lat_devices=lat_devices),
        in_specs=[pl.BlockSpec(memory_space=pltpu.SMEM)] + [vmem] * len(operands),
        out_specs=[vmem, vmem],
        out_shape=[
            jax.ShapeDtypeStruct((ROWS, COLS, CHANS), BF16),
            jax.ShapeDtypeStruct((TILES, 2, 8, 128), F32),
        ],
        scratch_shapes=[wide] * 5
        + [pltpu.VMEM((FLAT, 128), F32)]
        + [wide] * 4
        + [taps] * 4
        + [square] * 2
        + [local] * 5
        + [taps] * 2
        + [eight] * 2,
        compiler_params=pltpu.CompilerParams(vmem_limit_bytes=60 * 1024 * 1024),
        name="both_blocks",
    )(lat, *operands)


def unpack_kernel(packed, embed, kernel1, kernel2, point1, point2, gain1, gain2, *, factor):
    for h in (0, 1):
        lanes = slice(128 * h, 128 * h + 128)
        point1[:, lanes] = packed[0:32, h].reshape(CHANS, 128) * factor
        point2[:, lanes] = packed[32:64, h].reshape(CHANS, 128) * factor
        mixed = packed[64:73, h].reshape(72, 128) * factor
        embed[:, lanes] = mixed[:VARS]
        gain1[:, lanes] = mixed[VARS : VARS + 1]
        gain2[:, lanes] = mixed[VARS + 1 : VARS + 2]
        kernel1[:, lanes] = (packed[73:77, h].reshape(32, 128) * factor)[:25]
        kernel2[:, lanes] = (packed[77:81, h].reshape(32, 128) * factor)[:25]


def summed(packed, factor):
    devices = lax.axis_size(AXES)
    parts = lax.all_to_all(packed, AXES, 0, 0, tiled=True)
    mine = jnp.sum(parts.reshape(devices, -1, 2, 8, 128), 0)
    total = lax.all_to_all(jnp.tile(mine, (devices, 1, 1, 1)), AXES, 0, 0, tiled=True)
    shapes = [(VARS, CHANS), (25, CHANS), (25, CHANS), (CHANS, CHANS), (CHANS, CHANS)]
    results = pl.pallas_call(
        functools.partial(unpack_kernel, factor=factor),
        out_shape=[jax.ShapeDtypeStruct(s, F32) for s in shapes + [(1, CHANS)] * 2],
        name="unpack",
    )(total)
    return (*results[:5], results[5].reshape(CHANS), results[6].reshape(CHANS))


def shifted(before, after, axis, wrap):
    devices = lax.axis_size(axis)
    up = [(i, (i + 1) % devices) for i in range(devices if wrap else devices - 1)]
    down = [(j, i) for i, j in up]
    return lax.ppermute(after, axis, up), lax.ppermute(before, axis, down)


def on_device(points, row_len, w_embed, kernel1, gain1, point1, kernel2, gain2, point2, cotangent):
    lon_total = COLS * lax.axis_size("lon")
    rows_total = ROWS * lax.axis_size("lat")
    cot_left, cot_right = shifted(
        cotangent[:, :4].reshape(ROWS // 2, 8, CHANS),
        cotangent[:, COLS - 4 :].reshape(ROWS // 2, 8, CHANS),
        "lon",
        True,
    )
    h0, west, east, regridded = regrid_embed(points, row_len, w_embed, lon_total)
    left, right = shifted(west, east, "lon", True)
    blank = jnp.zeros((4, 4, CHANS), BF16)

    def band(rows, narrow, pairs):
        field = jnp.concatenate([left[rows], h0[rows], right[rows]], 1)
        sides = [c[pairs].reshape(4, 4, CHANS) for c in (cot_left, cot_right)]
        given = jnp.concatenate([blank, sides[0], cotangent[narrow], sides[1], blank], 1)
        return jnp.concatenate([field, given], 0)

    above, below = shifted(
        band(slice(0, HALO), slice(0, 4), slice(0, 2)),
        band(slice(ROWS - HALO, ROWS), slice(ROWS - 4, ROWS), slice(-2, None)),
        "lat",
        False,
    )
    fields = (h0, left, right, above, below, cotangent, cot_left, cot_right)
    weights = (
        kernel1, gain1.reshape(1, CHANS), point1, kernel2, gain2.reshape(1, CHANS), point2,
    )
    out, packed = blocks(fields, weights, regridded, lax.axis_size("lat"))
    return (out, *summed(packed, float(rows_total * lon_total) ** (-0.5)))


def solution(mesh):
    in_specs = (
        P("lat", None, "lon"),
        P("lat"),
        P(),
        P(),
        P(),
        P(),
        P(),
        P(),
        P(),
        P("lat", "lon", None),
    )
    out_specs = (P("lat", "lon", None), P(), P(), P(), P(), P(), P(), P())
    return jax.shard_map(
        on_device, mesh=mesh, in_specs=in_specs, out_specs=out_specs, check_vma=False
    )
```

time: 352 us -> 147 us (0.42)
  waiting for transfers between devices: 154 us -> 12.8 us
  other arithmetic: 69.7 us -> 0.17 us
  Pallas kernels: 0 us -> 54.3 us
  blocking collectives: 0 us -> 47.5 us
  matrix products: 42.7 us -> 0 us
  local copies, waits for them, and re-layouts: 28.8 us -> 8.26 us
  starting transfers between devices: 40.3 us -> 22.1 us
  between operations: 15.5 us -> 0.82 us
    psum x1 -> x0, waiting for transfers between devices: 147 us -> none  [together(): total = lax.psum(jnp.concatenate([a.ravel() for a in arrays]), axis)]
    pallas_call x0 -> x3, Pallas kernels: none -> 54.3 us  [the longest x1 46.1 us: blocks(): pl.pallas_call(functools.partial(blocks_kernel, lat_devices=lat_devices),...]
    all_to_all x0 -> x2, blocking collectives: none -> 47.5 us  [the longest x1 24 us: summed(): parts = lax.all_to_all(packed, AXES, 0, 0, tiled=True)]
    dot_general x9 -> x0, matrix products: 42.7 us -> none  [the longest x1 26.3 us: on_device(): jnp.einsum('rvj,rjc->vc', regridded, grad0, precision=lax.Precision.HIGHEST)]
    convert_element_type x5 -> x0, other arithmetic: 35 us -> none  [the longest x1 26.1 us: mix_backward(): dmixed = (upstream * sig * (1.0 + mixed * (1.0 - sig))).astype(jnp.bfloat16)]
    reduce_sum x6 -> x1, other arithmetic: 26.3 us -> 0.14 us  [summed(): mine = jnp.sum(parts.reshape(devices, -1, 2, 8, 128), 0)]
    ppermute x12 -> x6, starting transfers between devices: 40.2 us -> 22.1 us  [shifted(): return (lax.ppermute(after, axis, up), lax.ppermute(before, axis, down))]
    unnamed x190 -> x13, local copies, waits for them, and re-layouts: 12.2 us -> 5.02 us
  transfers between devices with their start and end apart: 13 -> 6, of which waited for: 5 -> 3; matrix products, arithmetic and copies ran while one was open for 4% -> 2% of each run, Pallas kernels for 0% -> 0%
where the time goes in v2:
time: 147 us; the launch traced here: 146 us
  Pallas kernels  54.3 us (37%)
  blocking collectives  47.5 us (32%)
  starting transfers between devices  22.1 us (15%)
  waiting for transfers between devices  12.8 us (9%)
  local copies, waits for them, and re-layouts  8.26 us (6%)
    pallas_call x1, Pallas kernels, blocks(): pl.pallas_call(functools.partial(blocks_kernel, lat_devices=lat_devices),...  46.1 us
    all_to_all x1, blocking collectives, summed(): parts = lax.all_to_all(packed, AXES, 0, 0, tiled=True)  24 us
    all_to_all x1, blocking collectives, summed(): lax.all_to_all(jnp.tile(mine, (devices, 1, 1, 1)), AXES, 0, 0, tiled=True)  23.5 us
    ppermute x6, starting transfers between devices, shifted(): return (lax.ppermute(after, axis, up), lax.ppermute(before, axis, down))  22.1 us
    ppermute x6, waiting for transfers between devices, shifted(): return (lax.ppermute(after, axis, up), lax.ppermute(before, axis, down))  12.8 us
    pallas_call x1, Pallas kernels, regrid_embed(): pl.pallas_call(functools.partial(regrid_kernel, lon_total=lon_total), gri...  6.19 us
    unnamed x13, local copies, waits for them, and re-layouts  5.02 us
  transfers between devices with their start and end apart: 6, of which 3 were waited for; matrix products, arithmetic and copies ran while one was open for 2% of the time, Pallas kernels for 0%

profile of v2, /device:TPU:1, one launch (start us, length us, event | category | flops | bytes accessed | tf_op | source)
XLA Modules:
  0.0 146.0 jit_solution(13746252738373962364)
XLA Ops:
  0.6 4.3 %copy.19.points = bf16[64,69,163]{2,1,0:T(8,128)(2,1)} copy(bf16[64,69,163]{2,0,1:T(8,128)(2,1)} %param.10) | data formatting | bytes 2879232 | tf_op args[0]
  5.0 6.2 %regrid_embed.1 = (bf16[64,24,256]{2,1,0:T(8,128)(2,1)}, bf16[64,8,256]{2,1,0:T(8,128)(2,1)}, bf16[64,8,256]{2,1,0:T(8,128)(2,1)}, bf16[1536,128]{1,0:T(8,128)(2,1)}) custom-call(s32[64]{0:T(128)} %row_len.1, s32[1]{0:T(128)} %bitcast.1.sector, bf16[64,69,163]{2,1,0:T(8,128)(2,1)} %copy.19.points, bf16[69,256]{1,0:T(8,128)(2,1)} %w_embed.1), custom_call_target="tpu_custom_call" | custom-call | tf_op jit(solution)/shard_map/regrid_embed/pallas_call | solution.py:69
  11.2 2.0 %collective-permute-start = (bf16[64,8,256]{2,1,0:T(8,128)(2,1)}, bf16[64,8,256]{2,1,0:T(8,128)(2,1)S(1)}, u32[]{:S(2)}, u32[]{:S(2)}) collective-permute-start(bf16[64,8,256]{2,1,0:T(8,128)(2,1)} %get-tuple-element.22), channel_id=1, source_target_pairs={{0,4},{4,8},{8,12},{12,16},{16,20},{20,24},{24,28},{28,32},{32,36}... | collective-permute-start | bytes 786440 | tf_op jit(solution)/shard_map/ppermute | solution.py:484
  13.2 6.0 %collective-permute-start.1 = (bf16[64,8,256]{2,1,0:T(8,128)(2,1)}, bf16[64,8,256]{2,1,0:T(8,128)(2,1)S(1)}, u32[]{:S(2)}, u32[]{:S(2)}) collective-permute-start(bf16[64,8,256]{2,1,0:T(8,128)(2,1)} %get-tuple-element.23), channel_id=1, source_target_pairs={{4,0},{8,4},{12,8},{16,12},{20,16},{24,20},{28,24},{32,28},{36,32}... | collective-permute-start | bytes 786440 | tf_op jit(solution)/shard_map/ppermute | solution.py:484
  19.2 1.1 fusion.2
  20.4 0.1 collective-permute-start.2
  20.5 5.7 %collective-permute-start.3 = (bf16[32,8,256]{2,1,0:T(8,128)(2,1)S(1)}, bf16[32,8,256]{2,1,0:T(8,128)(2,1)S(1)}, u32[]{:S(2)}, u32[]{:S(2)}) collective-permute-start(bf16[32,8,256]{2,1,0:T(8,128)(2,1)S(1)} %reshape.62), channel_id=1, source_target_pairs={{4,0},{8,4},{12,8},{16,12},{20,16},{24,20},{28,24},{32,28},{36,32}... | collective-permute-start | bytes 393224 | tf_op jit(solution)/shard_map/ppermute | solution.py:484
  26.2 1.0 fusion
  27.2 0.8 fusion.1
  28.0 5.7 %collective-permute-done.2.cot_left = bf16[32,8,256]{2,1,0:T(8,128)(2,1)S(1)} collective-permute-done((bf16[32,8,256]{2,1,0:T(8,128)(2,1)S(1)}, bf16[32,8,256]{2,1,0:T(8,128)(2,1)S(1)}, u32[]{:S(2)}, u32[]{:S(2)}) %collective-permute-start.2) | collective-permute-done | bytes 131104 | tf_op jit(solution)/shard_map/ppermute | solution.py:484
  33.8 0.0 copy-start.4
  33.8 0.0 collective-permute-done.3.cot_right
  33.8 0.0 copy-start.5
  33.9 0.1 concatenate.19
  33.9 0.1 concatenate.22
  34.0 0.0 collective-permute-done.1.right
  34.0 0.0 copy-start.1
  34.0 0.0 collective-permute-done.left
  34.0 0.0 copy-start
  34.1 6.3 %collective-permute-start.4 = (bf16[12,40,256]{2,1,0:T(8,128)(2,1)S(1)}, bf16[12,40,256]{2,1,0:T(8,128)(2,1)S(1)}, u32[]{:S(2)}, u32[]{:S(2)}) collective-permute-start(bf16[12,40,256]{2,1,0:T(8,128)(2,1)S(1)} %pad_maximum_fusion), channel_id=1, source_target_pairs={{0,1},{1,2},{2,3},{4,5},{5,6},{6,7},{8,9},{9,10},{10,11},{12,13},{... | collective-permute-start | bytes 737288 | tf_op jit(solution)/shard_map/ppermute | solution.py:484
  40.4 1.9 %collective-permute-start.5 = (bf16[12,40,256]{2,1,0:T(8,128)(2,1)S(1)}, bf16[12,40,256]{2,1,0:T(8,128)(2,1)S(1)}, u32[]{:S(2)}, u32[]{:S(2)}) collective-permute-start(bf16[12,40,256]{2,1,0:T(8,128)(2,1)S(1)} %pad_maximum_fusion.1), channel_id=1, source_target_pairs={{1,0},{2,1},{3,2},{5,4},{6,5},{7,6},{9,8},{10,9},{11,10},{13,12},{... | collective-permute-start | bytes 737288 | tf_op jit(solution)/shard_map/ppermute | solution.py:484
  42.4 1.2 collective-permute-done.4.above
  43.5 0.0 copy-start.2
  43.5 5.9 %collective-permute-done.5.below = bf16[12,40,256]{2,1,0:T(8,128)(2,1)S(1)} collective-permute-done((bf16[12,40,256]{2,1,0:T(8,128)(2,1)S(1)}, bf16[12,40,256]{2,1,0:T(8,128)(2,1)S(1)}, u32[]{:S(2)}, u32[]{:S(2)}) %collective-permute-start.5) | collective-permute-done | bytes 245792 | tf_op jit(solution)/shard_map/ppermute | solution.py:484
  49.5 0.0 copy-start.3
  49.5 0.0 copy-done.4
  49.5 0.0 copy-done.5
  49.5 0.0 copy-done.1
  49.5 0.0 copy-done
  49.5 0.0 copy-done.2
  49.5 0.7 copy-done.3
  50.2 46.1 %both_blocks.1 = (bf16[64,24,256]{2,1,0:T(8,128)(2,1)}, f32[128,2,8,128]{3,2,1,0:T(8,128)}) custom-call(s32[1]{0:T(128)} %bitcast.lat, bf16[64,24,256]{2,1,0:T(8,128)(2,1)} %get-tuple-element.21.h0, bf16[64,8,256]{2,1,0:T(8,128)(2,1)} %copy-done, bf16[64,8,256]{2,1,0:T(8,128)(2,1)} %copy-done.1, bf16[12,40,256]{2,1,0:T(8,128)(2,1)} %copy-done.2, ...), custom_call_target="tpu_custom_call" | custom-call | tf_op jit(solution)/shard_map/both_blocks/pallas_call | solution.py:432
  96.2 24.0 %all_to_all.10 = f32[128,2,8,128]{3,2,1,0:T(8,128)S(1)} all-to-all(f32[128,2,8,128]{3,2,1,0:T(8,128)} %get-tuple-element.26), channel_id=1, replica_groups=mesh['lon'=32,'lat'=4] {'lon','lat'}, dimensions={0} | all-to-all | bytes 2097152 | tf_op jit(solution)/shard_map/all_to_all | solution.py:468
  120.2 0.1 reduce_sum.9
  120.4 0.1 tile.2
  120.5 23.5 %all_to_all.11.packed = f32[128,2,8,128]{3,2,1,0:T(8,128)} all-to-all(f32[128,2,8,128]{3,2,1,0:T(8,128)S(1)} %tile.2), channel_id=1, replica_groups=mesh['lon'=32,'lat'=4] {'lon','lat'}, dimensions={0} | all-to-all | bytes 2097152 | tf_op jit(solution)/shard_map/all_to_all | solution.py:470
  144.0 2.1 %unpack.1 = (f32[69,256]{1,0:T(8,128)}, f32[25,256]{1,0:T(8,128)}, f32[25,256]{1,0:T(8,128)}, f32[256,256]{1,0:T(8,128)}, f32[256,256]{1,0:T(8,128)}, /*index=5*/f32[1,256]{1,0:T(1,128)}, f32[1,256]{1,0:T(1,128)}) custom-call(f32[128,2,8,128]{3,2,1,0:T(8,128)} %all_to_all.11.packed), custom_call_target="tpu_custom_call" | custom-call | tf_op jit(solution)/shard_map/unpack/pallas_call | solution.py:472
  (13 shorter events, 0.2 us)
Async XLA Ops:
  11.2 22.8 %collective-permute-start = (bf16[64,8,256]{2,1,0:T(8,128)(2,1)}, bf16[64,8,256]{2,1,0:T(8,128)(2,1)S(1)}, u32[]{:S(2)}, u32[]{:S(2)}) collective-permute-start(bf16[64,8,256]{2,1,0:T(8,128)(2,1)} %get-tuple-element.22), channel_id=1, source_target_pairs={{0,4},{4,8},{8,12},{12,16},{16,20},{20,24},{24,28},{28,32},{32,36}... | collective-permute-start | bytes 786440 | tf_op jit(solution)/shard_map/ppermute | solution.py:484
  13.2 20.8 %collective-permute-start.1 = (bf16[64,8,256]{2,1,0:T(8,128)(2,1)}, bf16[64,8,256]{2,1,0:T(8,128)(2,1)S(1)}, u32[]{:S(2)}, u32[]{:S(2)}) collective-permute-start(bf16[64,8,256]{2,1,0:T(8,128)(2,1)} %get-tuple-element.23), channel_id=1, source_target_pairs={{4,0},{8,4},{12,8},{16,12},{20,16},{24,20},{28,24},{32,28},{36,32}... | collective-permute-start | bytes 786440 | tf_op jit(solution)/shard_map/ppermute | solution.py:484
  20.4 13.4 %collective-permute-start.2 = (bf16[32,8,256]{2,1,0:T(8,128)(2,1)S(1)}, bf16[32,8,256]{2,1,0:T(8,128)(2,1)S(1)}, u32[]{:S(2)}, u32[]{:S(2)}) collective-permute-start(bf16[32,8,256]{2,1,0:T(8,128)(2,1)S(1)} %reshape.60), channel_id=1, source_target_pairs={{0,4},{4,8},{8,12},{12,16},{16,20},{20,24},{24,28},{28,32},{32,36}... | collective-permute-start | bytes 393224 | tf_op jit(solution)/shard_map/ppermute | solution.py:484
  20.5 13.3 %collective-permute-start.3 = (bf16[32,8,256]{2,1,0:T(8,128)(2,1)S(1)}, bf16[32,8,256]{2,1,0:T(8,128)(2,1)S(1)}, u32[]{:S(2)}, u32[]{:S(2)}) collective-permute-start(bf16[32,8,256]{2,1,0:T(8,128)(2,1)S(1)} %reshape.62), channel_id=1, source_target_pairs={{4,0},{8,4},{12,8},{16,12},{20,16},{24,20},{28,24},{32,28},{36,32}... | collective-permute-start | bytes 393224 | tf_op jit(solution)/shard_map/ppermute | solution.py:484
  33.8 15.7 %copy-start.4 = (bf16[32,8,256]{2,1,0:T(8,128)(2,1)}, bf16[32,8,256]{2,1,0:T(8,128)(2,1)S(1)}, u32[]{:S(2)}) copy-start(bf16[32,8,256]{2,1,0:T(8,128)(2,1)S(1)} %collective-permute-done.2.cot_left) | copy-start | bytes 393220
  33.8 15.7 %copy-start.5 = (bf16[32,8,256]{2,1,0:T(8,128)(2,1)}, bf16[32,8,256]{2,1,0:T(8,128)(2,1)S(1)}, u32[]{:S(2)}) copy-start(bf16[32,8,256]{2,1,0:T(8,128)(2,1)S(1)} %collective-permute-done.3.cot_right) | copy-start | bytes 393220
  34.0 15.5 %copy-start.1 = (bf16[64,8,256]{2,1,0:T(8,128)(2,1)}, bf16[64,8,256]{2,1,0:T(8,128)(2,1)S(1)}, u32[]{:S(2)}) copy-start(bf16[64,8,256]{2,1,0:T(8,128)(2,1)S(1)} %collective-permute-done.1.right) | copy-start | bytes 786436
  34.0 15.5 %copy-start = (bf16[64,8,256]{2,1,0:T(8,128)(2,1)}, bf16[64,8,256]{2,1,0:T(8,128)(2,1)S(1)}, u32[]{:S(2)}) copy-start(bf16[64,8,256]{2,1,0:T(8,128)(2,1)S(1)} %collective-permute-done.left) | copy-start | bytes 786436
  34.1 9.5 %collective-permute-start.4 = (bf16[12,40,256]{2,1,0:T(8,128)(2,1)S(1)}, bf16[12,40,256]{2,1,0:T(8,128)(2,1)S(1)}, u32[]{:S(2)}, u32[]{:S(2)}) collective-permute-start(bf16[12,40,256]{2,1,0:T(8,128)(2,1)S(1)} %pad_maximum_fusion), channel_id=1, source_target_pairs={{0,1},{1,2},{2,3},{4,5},{5,6},{6,7},{8,9},{9,10},{10,11},{12,13},{... | collective-permute-start | bytes 737288 | tf_op jit(solution)/shard_map/ppermute | solution.py:484
  40.4 9.0 %collective-permute-start.5 = (bf16[12,40,256]{2,1,0:T(8,128)(2,1)S(1)}, bf16[12,40,256]{2,1,0:T(8,128)(2,1)S(1)}, u32[]{:S(2)}, u32[]{:S(2)}) collective-permute-start(bf16[12,40,256]{2,1,0:T(8,128)(2,1)S(1)} %pad_maximum_fusion.1), channel_id=1, source_target_pairs={{1,0},{2,1},{3,2},{5,4},{6,5},{7,6},{9,8},{10,9},{11,10},{13,12},{... | collective-permute-start | bytes 737288 | tf_op jit(solution)/shard_map/ppermute | solution.py:484
  43.5 6.0 %copy-start.2 = (bf16[12,40,256]{2,1,0:T(8,128)(2,1)}, bf16[12,40,256]{2,1,0:T(8,128)(2,1)S(1)}, u32[]{:S(2)}) copy-start(bf16[12,40,256]{2,1,0:T(8,128)(2,1)S(1)} %collective-permute-done.4.above) | copy-start | bytes 737284
  49.5 0.7 copy-start.3

commit v3 on v2

v3 whole, which is shorter than its diff:
```python
import functools

import jax
import jax.numpy as jnp
from jax import lax
from jax.experimental import pallas as pl
from jax.experimental.pallas import tpu as pltpu
from jax.sharding import PartitionSpec as P

F32 = jnp.float32
BF16 = jnp.bfloat16
ROWS = 64
COLS = 24
HALO = 8
PITCH = COLS + 2 * HALO
TALL = ROWS + 2 * HALO
INNER = COLS + 8
LEAD = 16
FLAT = LEAD + PITCH * TALL + 16
SLIM = LEAD + INNER * TALL + 16
CHANS = 256
VARS = 69
TILES = 128
AXES = ("lon", "lat")


GROUP = 8 * COLS
STRIP = 8 * HALO


def regrid_kernel(row_len, sector, points, high, low, west, east, *, lon_total):
    first = (sector[0] * COLS).astype(F32)
    whole = lon_total // 4
    lane = lax.broadcasted_iota(jnp.int32, (8, GROUP), 1)
    row = lane % 8
    cell = first + (lane // 8).astype(F32)
    own = lax.broadcasted_iota(jnp.int32, (8, GROUP), 0) == row
    mark = lax.broadcasted_iota(jnp.int32, (points.shape[3], GROUP), 0).astype(F32)
    found = []
    for k in range(points.shape[1]):
        group = pl.program_id(0) * points.shape[1] + k
        count = jnp.zeros((8, GROUP), F32)
        for q in range(8):
            count = jnp.where(row == q, row_len[8 * group + q].astype(F32), count)
        product = cell * count
        lower = jnp.floor((product + 2.0) * (1.0 / lon_total))
        start = jnp.floor((first * count + 2.0) * (1.0 / lon_total))
        share = (product - lower * lon_total) * 0.25
        away = mark - (lower - start)[:1]
        mix = jnp.where(
            away == 0.0, whole - share[:1], jnp.where(away == 1.0, share[:1], 0.0)
        )
        rows = points[:, k].reshape(VARS * 8, points.shape[3])
        every = jnp.dot(rows, mix.astype(BF16), preferred_element_type=F32)
        kept = jnp.where(own[None], every.reshape(VARS, 8, GROUP), 0.0)
        found.append(jnp.sum(kept, 1) * (1.0 / whole))
    values = jnp.concatenate(found, 1)
    rounded = values.astype(BF16)
    high[...] = rounded
    low[...] = (values - rounded.astype(F32)).astype(BF16)
    west[...] = jnp.concatenate([f[:, :STRIP] for f in found], 1).astype(BF16)
    east[...] = jnp.concatenate([f[:, GROUP - STRIP :] for f in found], 1).astype(BF16)


def regrid(points, row_len, lon_total):
    nvars, nrows, slots = points.shape
    groups = 2
    steps = nrows // (8 * groups)
    strips = jax.ShapeDtypeStruct((nvars, nrows * HALO), BF16)
    full = jax.ShapeDtypeStruct((nvars, nrows * COLS), BF16)
    return pl.pallas_call(
        functools.partial(regrid_kernel, lon_total=lon_total),
        grid_spec=pltpu.PrefetchScalarGridSpec(
            num_scalar_prefetch=2,
            grid=(steps,),
            in_specs=[pl.BlockSpec((nvars, groups, 8, slots), lambda i, *_: (0, i, 0, 0))],
            out_specs=[
                pl.BlockSpec((nvars, groups * GROUP), lambda i, *_: (0, i)),
                pl.BlockSpec((nvars, groups * GROUP), lambda i, *_: (0, i)),
                pl.BlockSpec((nvars, groups * STRIP), lambda i, *_: (0, i)),
                pl.BlockSpec((nvars, groups * STRIP), lambda i, *_: (0, i)),
            ],
        ),
        out_shape=[full, full, strips, strips],
        name="regrid",
    )(
        row_len,
        jnp.reshape(lax.axis_index("lon"), (1,)).astype(jnp.int32),
        points.reshape(nvars, nrows // 8, 8, slots),
    )


def at(row):
    return LEAD + PITCH * row


def inner(row):
    return LEAD + INNER * row


def conv(source, half, start, pitch, rows, cols, taps, visit=None):
    sums = [None] * rows
    for e in range(5):
        weights = [taps[half, 5 * a + e] for a in range(5)]
        for i in range(rows + 4):
            x = source[half, pl.ds(start + pitch * (i - 2) + e - 2, cols), :]
            x = x.reshape(cols // 8, 8, 128)
            for a in range(5):
                r = i - a
                if 0 <= r < rows:
                    term = x * weights[a]
                    sums[r] = term if sums[r] is None else sums[r] + term
                    if visit is not None:
                        visit(a, e, r, x)
        if visit is not None:
            visit(None, e, None, None)
    return sums


class TapSums:
    def __init__(self, store, half, centre):
        self.store, self.half, self.centre, self.live = store, half, centre, {}

    def __call__(self, a, e, r, x):
        if a is None:
            for tap, value in self.live.items():
                self.store[self.half, tap] += value
            self.live = {}
            return
        tap = 24 - (5 * a + e)
        term = jnp.sum(self.centre[r] * x, 0)
        self.live[tap] = term if tap not in self.live else self.live[tap] + term


def blocks_kernel(
    lat, high, low, left, right, above, below, cot, cot_left, cot_right, cot_above, cot_below,
    w_embed, kernel1, gain1, point1, kernel2, gain2, point2,
    out, packed,
    x0, cots, d, h1, xhat1, scale1, slope1, dd2, g1, dd1,
    taps1, taps2, flip1, flip2, turned1, turned2,
    u1, dp1, u2, dp2, g0, gk1, gk2, gg1, gg2, swap, lifted,
    *, lat_devices,
):
    halves = (slice(0, 128), slice(128, 256))

    for k in range(25):
        for h in (0, 1):
            one = jnp.broadcast_to(kernel1[k : k + 1, halves[h]].astype(F32), (8, 128))
            two = jnp.broadcast_to(kernel2[k : k + 1, halves[h]].astype(F32), (8, 128))
            taps1[h, k] = one
            flip1[h, 24 - k] = one
            taps2[h, k] = two
            flip2[h, 24 - k] = two
    turned1[...] = jnp.transpose(point1[...].astype(F32)).astype(BF16)
    turned2[...] = jnp.transpose(point2[...].astype(F32)).astype(BF16)
    zeros = jnp.zeros((8, 128), F32)
    for h in (0, 1):
        for ref in (gg1, gg2):
            ref[h] = zeros
        for ref in (gk1, gk2):
            ref[h] = jnp.zeros((25, 8, 128), F32)
        for ref, size in ((x0, FLAT), (h1, FLAT), (dd2, SLIM), (dd1, SLIM)):
            ref[h, 0:LEAD] = jnp.zeros((LEAD, 128), F32)
            ref[h, size - 16 : size] = jnp.zeros((16, 128), F32)

    weight = w_embed[...]

    def across(a, b):
        return lax.dot_general(a, b, (((0,), (0,)), ((), ())), preferred_element_type=F32)

    def embed(spot, values):
        values = values.astype(BF16).astype(F32)
        for h in (0, 1):
            swap[h, pl.ds(pl.multiple_of(spot, 64), values.shape[0]), :] = values[:, halves[h]]

    def spread(spot, row):
        for k in range(8):
            for h in (0, 1):
                x0[h, pl.ds(pl.multiple_of(at(row + k), 8), PITCH), :] = swap[
                    h, pl.ds(spot + k, PITCH, stride=8), :
                ]

    for i in range(ROWS // 16):
        edge = slice(2 * STRIP * i, 2 * STRIP * (i + 1))
        middle = slice(2 * GROUP * i, 2 * GROUP * (i + 1))
        west = across(left[:, edge], weight)
        east = across(right[:, edge], weight)
        centre = across(high[:, middle], weight) + across(low[:, middle], weight)
        for k in (0, 1):
            spot = 8 * PITCH * (2 * i + k)
            embed(spot, west[STRIP * k : STRIP * (k + 1)])
            embed(spot + STRIP, centre[GROUP * k : GROUP * (k + 1)])
            embed(spot + STRIP + GROUP, east[STRIP * k : STRIP * (k + 1)])
    embed(8 * PITCH * (ROWS // 8), across(above[...], weight))
    embed(8 * PITCH * (ROWS // 8 + 1), across(below[...], weight))

    def unravel(i, carry):
        spread(8 * PITCH * i, HALO + 8 * i)
        return carry

    lax.fori_loop(0, ROWS // 8, unravel, 0)
    spread(8 * PITCH * (ROWS // 8), 0)
    spread(8 * PITCH * (ROWS // 8 + 1), HALO + ROWS)

    later = lax.broadcasted_iota(jnp.int32, (8, 128), 0) >= 4

    def put(row, value):
        for h in (0, 1):
            cots[h, pl.ds(pl.multiple_of(inner(row), 8), INNER), :] = value[:, halves[h]]

    def fill(pair, carry):
        sides = [cot_left[pair].astype(F32), cot_right[pair].astype(F32)]
        for odd in (0, 1):
            row = 2 * pair + odd
            edges = [s[4 * odd : 4 * odd + 4] for s in sides]
            put(
                row + HALO, jnp.concatenate([edges[0], cot[row].astype(F32), edges[1]], 0)
            )
        return carry

    lax.fori_loop(0, ROWS // 2, fill, 0)
    for k in range(4):
        put(k + 4, cot_above[k].astype(F32))
        put(k + HALO + ROWS, cot_below[k].astype(F32))

    def get(ref, start, count):
        return [ref[h, pl.ds(pl.multiple_of(start, 8), count), :] for h in (0, 1)]

    def keep(ref, start, values):
        for h in (0, 1):
            ref[h, pl.ds(pl.multiple_of(start, 8), values[h].shape[0]), :] = values[h]

    def from_wide(ref, row, rows):
        return [
            jnp.concatenate(
                [ref[h, pl.ds(at(row + r) + 4, INNER), :] for r in range(rows)], 0
            )
            for h in (0, 1)
        ]

    def joined(sums):
        return jnp.concatenate(sums, 0).reshape(-1, 128)

    def local_part(x):
        x = x.reshape(-1, 4, 8, 128)
        ends = jnp.where(later, x[:, 0], x[:, 3])
        return jnp.stack([ends, x[:, 1], x[:, 2]], 1).reshape(-1, 128)

    def gains(ref):
        return [ref[:, halves[h]] for h in (0, 1)]

    def normalised(raw):
        mean = jnp.sum(raw[0] * raw[0] + raw[1] * raw[1], -1, keepdims=True) * (1.0 / CHANS)
        scale = lax.rsqrt(mean + 1e-06)
        return scale, [raw[h] * scale for h in (0, 1)]

    def activated(xhat, gain, point):
        u = [xhat[h] * gain[h] for h in (0, 1)]
        p = jnp.dot(
            jnp.concatenate(u, 1).astype(BF16), point[...], preferred_element_type=F32
        )
        p = [p[:, s] for s in halves]
        sig = [0.5 * jnp.tanh(0.5 * v) + 0.5 for v in p]
        silu = [p[h] * sig[h] for h in (0, 1)]
        slope = [sig[h] + silu[h] * (1.0 - sig[h]) for h in (0, 1)]
        return u, silu, slope

    def through_norm(grad, slope, xhat, scale, gain, turned):
        dp = [grad[h] * slope[h] for h in (0, 1)]
        du = jnp.dot(
            jnp.concatenate(dp, 1).astype(BF16), turned[...], preferred_element_type=F32
        )
        gained = [du[:, halves[h]] * gain[h] for h in (0, 1)]
        both = [gained[h] * xhat[h] for h in (0, 1)]
        mean = jnp.sum(both[0] + both[1], -1, keepdims=True) * (1.0 / CHANS)
        dd = [
            (scale * (gained[h] - xhat[h] * mean)).astype(BF16).astype(F32) for h in (0, 1)
        ]
        return dp, both, dd

    def gain_sums(store, both):
        for h in (0, 1):
            store[h] += jnp.sum(local_part(both[h]).reshape(-1, 8, 128), 0)

    def pipeline(blocks, first, second):
        first(0)

        def step(i, carry):
            second(i - 1)
            first(i)
            return carry

        lax.fori_loop(1, blocks, step, 0)
        second(blocks - 1)

    size = 4 * PITCH

    def first_conv(i):
        start = at(2) + i * size
        keep(d, start, [joined(conv(x0, h, start, PITCH, 4, PITCH, taps1)) for h in (0, 1)])

    def first_mix(i):
        start = at(2) + i * size
        scale, xhat = normalised(get(d, start, size))
        _, silu, slope = activated(xhat, gains(gain1), point1)
        x = get(x0, start, size)
        keep(h1, start, [(x[h] + silu[h]).astype(BF16).astype(F32) for h in (0, 1)])
        keep(xhat1, start, xhat)
        keep(slope1, start, slope)
        scale1[pl.ds(pl.multiple_of(start, 8), size), :] = jnp.broadcast_to(scale, (size, 128))

    pipeline((TALL - 4) // 4, first_conv, first_mix)

    @pl.when(lat[0] == 0)
    def _():
        for h in (0, 1):
            h1[h, at(2) : at(HALO)] = jnp.zeros((6 * PITCH, 128), F32)

    @pl.when(lat[0] == lat_devices - 1)
    def _():
        for h in (0, 1):
            h1[h, at(HALO + ROWS) : at(HALO + ROWS + 6)] = jnp.zeros((6 * PITCH, 128), F32)

    def second_conv(row):
        keep(
            d,
            inner(row),
            [joined(conv(h1, h, at(row) + 4, PITCH, 4, INNER, taps2)) for h in (0, 1)],
        )

    def second_mix(row, local):
        start = inner(row)
        scale, xhat = normalised(get(d, start, 4 * INNER))
        gain = gains(gain2)
        u, silu, slope = activated(xhat, gain, point2)
        dp, both, dd = through_norm(
            get(cots, start, 4 * INNER), slope, xhat, scale, gain, turned2
        )
        keep(dd2, start, dd)
        if local is not None:
            keep(lifted, LEAD + 4 * INNER * local, silu)
            spot = pl.ds(pl.multiple_of(local * 96, 96), 96)
            u2[spot] = jnp.concatenate([local_part(v) for v in u], 1).astype(BF16)
            dp2[spot] = jnp.concatenate([local_part(v) for v in dp], 1).astype(BF16)
            gain_sums(gg2, both)

    def result(i):
        total = []
        for h in (0, 1):
            rows = []
            for r in range(4):
                place = LEAD + INNER * (4 * i + r) + 4
                base = h1[h, pl.ds(pl.multiple_of(at(HALO + 4 * i + r) + HALO, 8), COLS), :]
                rows.append(base + lifted[h, pl.ds(place, COLS), :])
            total.append(jnp.concatenate(rows, 0))
        out[pl.ds(i * 4, 4)] = jnp.concatenate(total, 1).reshape(4, COLS, CHANS).astype(BF16)

    def outer(k, carry):
        row = 4 + k * (ROWS + 4)
        second_conv(row)
        second_mix(row, None)
        return carry

    lax.fori_loop(0, 2, outer, 0)
    pipeline(
        ROWS // 4,
        lambda i: second_conv(HALO + 4 * i),
        lambda i: second_mix(HALO + 4 * i, i),
    )

    def third_conv(row, rows, local):
        start = inner(row)
        total = []
        for h in (0, 1):
            visit = None
            if local:
                centre = [
                    h1[h, pl.ds(at(row + r) + 4, INNER), :].reshape(4, 8, 128)
                    for r in range(rows)
                ]
                centre = [
                    jnp.stack(
                        [jnp.where(later, c[0], 0.0), c[1], c[2], jnp.where(later, 0.0, c[3])]
                    )
                    for c in centre
                ]
                visit = TapSums(gk2, h, centre)
            sums = joined(conv(dd2, h, start, INNER, rows, INNER, flip2, visit))
            total.append(sums + cots[h, pl.ds(pl.multiple_of(start, 8), rows * INNER), :])
        keep(g1, start, total)

    def third_mix(row, rows, local):
        start = inner(row)
        gain = gains(gain1)
        xhat = from_wide(xhat1, row, rows)
        scale = jnp.concatenate(
            [scale1[pl.ds(at(row + r) + 4, INNER), :] for r in range(rows)], 0
        )
        dp, both, dd = through_norm(
            get(g1, start, rows * INNER), from_wide(slope1, row, rows), xhat, scale, gain, turned1
        )
        keep(dd1, start, dd)
        if local is not None:
            spot = pl.ds(pl.multiple_of(local * 96, 96), 96)
            u = [local_part(xhat[h] * gain[h]) for h in (0, 1)]
            u1[spot] = jnp.concatenate(u, 1).astype(BF16)
            dp1[spot] = jnp.concatenate([local_part(v) for v in dp], 1).astype(BF16)
            gain_sums(gg1, both)
            result(local)

    def margin(k, carry):
        row = 6 + k * (ROWS + 2)
        third_conv(row, 2, False)
        third_mix(row, 2, None)
        return carry

    lax.fori_loop(0, 2, margin, 0)
    pipeline(
        ROWS // 4,
        lambda i: third_conv(HALO + 4 * i, 4, True),
        lambda i: third_mix(HALO + 4 * i, 4, i),
    )

    @pl.when(lat[0] == 0)
    def _():
        for h in (0, 1):
            dd1[h, inner(6) : inner(HALO)] = jnp.zeros((2 * INNER, 128), F32)

    @pl.when(lat[0] == lat_devices - 1)
    def _():
        for h in (0, 1):
            dd1[h, inner(HALO + ROWS) : inner(HALO + ROWS + 2)] = jnp.zeros(
                (2 * INNER, 128), F32
            )

    def fourth(i, carry):
        row = HALO + 4 * i
        for h in (0, 1):
            centre = [
                x0[h, pl.ds(pl.multiple_of(at(row + r) + HALO, 8), COLS), :].reshape(3, 8, 128)
                for r in range(4)
            ]
            sums = conv(dd1, h, inner(row) + 4, INNER, 4, COLS, flip1, TapSums(gk1, h, centre))
            for r in range(4):
                base = g1[h, pl.ds(inner(row + r) + 4, COLS), :]
                place = GROUP * (i // 2) + 4 * (i % 2) + r
                g0[h, pl.ds(place, COLS, stride=8), :] = sums[r].reshape(COLS, 128) + base
        return carry

    lax.fori_loop(0, ROWS // 4, fourth, 0)

    def pack(place, value):
        rows = value.shape[0]
        value = value.astype(BF16)
        for h in (0, 1):
            packed[place : place + rows // 8, h] = value[:, halves[h]].reshape(rows // 8, 8, 128)

    pack(0, across(u1[...], dp1[...]))
    pack(32, across(u2[...], dp2[...]))
    field = jnp.concatenate([g0[h] for h in (0, 1)], 1).astype(BF16)
    embedded = jnp.dot(high[...], field, preferred_element_type=F32)

    def gain_row(ref, gain):
        total = [jnp.sum(ref[h], 0, keepdims=True) for h in (0, 1)]
        return jnp.concatenate(total, 1) / gain[...]

    pack(
        64,
        jnp.concatenate(
            [embedded, gain_row(gg1, gain1), gain_row(gg2, gain2), jnp.zeros((1, CHANS), F32)], 0
        ),
    )
    for place, ref in ((73, gk1), (77, gk2)):
        total = jnp.concatenate([jnp.sum(ref[h], 1) for h in (0, 1)], 1)
        pack(place, jnp.concatenate([total, jnp.zeros((7, CHANS), F32)], 0))
    packed[81:TILES] = jnp.zeros((TILES - 81, 2, 8, 128), BF16)


def blocks(fields, weights, lat_devices):
    wide = pltpu.VMEM((2, FLAT, 128), F32)
    slim = pltpu.VMEM((2, SLIM, 128), F32)
    taps = pltpu.VMEM((2, 25, 8, 128), F32)
    square = pltpu.VMEM((CHANS, CHANS), BF16)
    local = pltpu.VMEM((ROWS * COLS, CHANS), BF16)
    eight = pltpu.VMEM((2, 8, 128), F32)
    lat = jnp.reshape(lax.axis_index("lat"), (1,)).astype(jnp.int32)
    operands = (*fields, *weights)
    vmem = pl.BlockSpec(memory_space=pltpu.VMEM)
    return pl.pallas_call(
        functools.partial(blocks_kernel, lat_devices=lat_devices),
        in_specs=[pl.BlockSpec(memory_space=pltpu.SMEM)] + [vmem] * len(operands),
        out_specs=[vmem, vmem],
        out_shape=[
            jax.ShapeDtypeStruct((ROWS, COLS, CHANS), BF16),
            jax.ShapeDtypeStruct((TILES, 2, 8, 128), BF16),
        ],
        scratch_shapes=[wide, slim, wide, wide, wide, pltpu.VMEM((FLAT, 128), F32), wide]
        + [slim] * 3
        + [taps] * 4
        + [square] * 2
        + [local] * 4
        + [pltpu.VMEM((2, ROWS * COLS, 128), F32)]
        + [taps] * 2
        + [eight] * 2
        + [pltpu.VMEM((2, PITCH * TALL, 128), F32)]
        + [pltpu.VMEM((2, LEAD + INNER * ROWS + 16, 128), F32)],
        compiler_params=pltpu.CompilerParams(vmem_limit_bytes=60 * 1024 * 1024),
        name="both_blocks",
    )(lat, *operands)


def unpack_kernel(packed, embed, kernel1, kernel2, point1, point2, gain1, gain2, *, factor):
    for h in (0, 1):
        lanes = slice(128 * h, 128 * h + 128)
        point1[:, lanes] = packed[0:32, h].astype(F32).reshape(CHANS, 128) * factor
        point2[:, lanes] = packed[32:64, h].astype(F32).reshape(CHANS, 128) * factor
        mixed = packed[64:73, h].astype(F32).reshape(72, 128) * factor
        embed[:, lanes] = mixed[:VARS]
        gain1[:, lanes] = mixed[VARS : VARS + 1]
        gain2[:, lanes] = mixed[VARS + 1 : VARS + 2]
        kernel1[:, lanes] = (packed[73:77, h].astype(F32).reshape(32, 128) * factor)[:25]
        kernel2[:, lanes] = (packed[77:81, h].astype(F32).reshape(32, 128) * factor)[:25]


def summed(packed, factor):
    devices = lax.axis_size(AXES)
    parts = lax.all_to_all(packed, AXES, 0, 0, tiled=True)
    mine = jnp.sum(parts.reshape(devices, -1, 2, 8, 128).astype(F32), 0).astype(BF16)
    total = lax.all_to_all(jnp.tile(mine, (devices, 1, 1, 1)), AXES, 0, 0, tiled=True)
    shapes = [(VARS, CHANS), (25, CHANS), (25, CHANS), (CHANS, CHANS), (CHANS, CHANS)]
    results = pl.pallas_call(
        functools.partial(unpack_kernel, factor=factor),
        out_shape=[jax.ShapeDtypeStruct(s, F32) for s in shapes + [(1, CHANS)] * 2],
        name="unpack",
    )(total)
    return (*results[:5], results[5].reshape(CHANS), results[6].reshape(CHANS))


def shifted(before, after, axis, wrap):
    devices = lax.axis_size(axis)
    up = [(i, (i + 1) % devices) for i in range(devices if wrap else devices - 1)]
    down = [(j, i) for i, j in up]
    return lax.ppermute(after, axis, up), lax.ppermute(before, axis, down)


def on_device(points, row_len, w_embed, kernel1, gain1, point1, kernel2, gain2, point2, cotangent):
    lon_total = COLS * lax.axis_size("lon")
    rows_total = ROWS * lax.axis_size("lat")
    cot_left, cot_right = shifted(
        cotangent[:, :4].reshape(ROWS // 2, 8, CHANS),
        cotangent[:, COLS - 4 :].reshape(ROWS // 2, 8, CHANS),
        "lon",
        True,
    )
    high, low, west, east = regrid(jnp.swapaxes(points, 0, 1), row_len, lon_total)
    left, right = shifted(west, east, "lon", True)

    def cot_band(rows, pairs):
        sides = [c[pairs].reshape(4, 4, CHANS) for c in (cot_left, cot_right)]
        return jnp.concatenate([sides[0], cotangent[rows], sides[1]], 1)

    cot_above, cot_below = shifted(
        cot_band(slice(0, 4), slice(0, 2)),
        cot_band(slice(ROWS - 4, ROWS), slice(ROWS // 2 - 2, ROWS // 2)),
        "lat",
        False,
    )
    above, below = shifted(
        jnp.concatenate([left[:, :STRIP], high[:, :GROUP], right[:, :STRIP]], 1),
        jnp.concatenate([left[:, -STRIP:], high[:, -GROUP:], right[:, -STRIP:]], 1),
        "lat",
        False,
    )
    fields = (
        high, low, left, right, above, below,
        cotangent, cot_left, cot_right, cot_above, cot_below,
    )
    weights = (
        w_embed, kernel1, gain1.reshape(1, CHANS), point1,
        kernel2, gain2.reshape(1, CHANS), point2,
    )
    out, packed = blocks(fields, weights, lax.axis_size("lat"))
    return (out, *summed(packed, float(rows_total * lon_total) ** (-0.5)))


def solution(mesh):
    in_specs = (
        P("lat", None, "lon"),
        P("lat"),
        P(),
        P(),
        P(),
        P(),
        P(),
        P(),
        P(),
        P("lat", "lon", None),
    )
    out_specs = (P("lat", "lon", None), P(), P(), P(), P(), P(), P(), P())
    return jax.shard_map(
        on_device, mesh=mesh, in_specs=in_specs, out_specs=out_specs, check_vma=False
    )
```

time: 147 us -> 128 us (0.87)
  blocking collectives: 47.5 us -> 38.2 us
  waiting for transfers between devices: 12.8 us -> 5.29 us
  local copies, waits for them, and re-layouts: 8.26 us -> 3.81 us
  starting transfers between devices: 22.1 us -> 26.5 us
  Pallas kernels: 54.3 us -> 52.2 us
    ppermute x6 -> x8, waiting for transfers between devices: 12.8 us -> 5.29 us  [shifted(): return (lax.ppermute(after, axis, up), lax.ppermute(before, axis, down))]
    all_to_all x1, blocking collectives: 23.5 us -> 17.9 us  [summed(): lax.all_to_all(jnp.tile(mine, (devices, 1, 1, 1)), AXES, 0, 0, tiled=True)]
    ppermute x6 -> x8, starting transfers between devices: 22.1 us -> 26.5 us  [shifted(): return (lax.ppermute(after, axis, up), lax.ppermute(before, axis, down))]
    unnamed x13 -> x16, local copies, waits for them, and re-layouts: 5.02 us -> 0.63 us
    all_to_all x1, blocking collectives: 24 us -> 20.3 us  [summed(): parts = lax.all_to_all(packed, AXES, 0, 0, tiled=True)]
  transfers between devices with their start and end apart: 6 -> 8, of which waited for: 3 -> 2; matrix products, arithmetic and copies ran while one was open for 2% -> 2% of each run, Pallas kernels for 0% -> 4%
where the time goes in v3:
time: 128 us; the launch traced here: 127 us
  Pallas kernels  52.2 us (41%)
  blocking collectives  38.2 us (30%)
  starting transfers between devices  26.5 us (21%)
  waiting for transfers between devices  5.29 us (4%)
  local copies, waits for them, and re-layouts  3.81 us (3%)
    pallas_call x1, Pallas kernels, blocks(): pl.pallas_call(functools.partial(blocks_kernel, lat_devices=lat_devices),...  45.1 us
    ppermute x8, starting transfers between devices, shifted(): return (lax.ppermute(after, axis, up), lax.ppermute(before, axis, down))  26.5 us
    all_to_all x1, blocking collectives, summed(): parts = lax.all_to_all(packed, AXES, 0, 0, tiled=True)  20.3 us
    all_to_all x1, blocking collectives, summed(): lax.all_to_all(jnp.tile(mine, (devices, 1, 1, 1)), AXES, 0, 0, tiled=True)  17.9 us
    ppermute x8, waiting for transfers between devices, shifted(): return (lax.ppermute(after, axis, up), lax.ppermute(before, axis, down))  5.29 us
    pallas_call x1, Pallas kernels, regrid(): pl.pallas_call(functools.partial(regrid_kernel, lon_total=lon_total), gri...  5.23 us
  transfers between devices with their start and end apart: 8, of which 2 were waited for; matrix products, arithmetic and copies ran while one was open for 2% of the time, Pallas kernels for 4%

profile of v3, /device:TPU:1, one launch (start us, length us, event | category | flops | bytes accessed | tf_op | source)
XLA Modules:
  0.0 127.3 jit_solution(17858036396371065917)
XLA Ops:
  0.6 1.1 fusion.1
  1.8 2.1 %collective-permute-start.4 = (bf16[32,8,256]{2,1,0:T(8,128)(2,1)S(1)}, bf16[32,8,256]{2,1,0:T(8,128)(2,1)S(1)}, u32[]{:S(2)}, u32[]{:S(2)}) collective-permute-start(bf16[32,8,256]{2,1,0:T(8,128)(2,1)S(1)} %reshape.64), channel_id=1, source_target_pairs={{0,4},{4,8},{8,12},{12,16},{16,20},{20,24},{24,28},{28,32},{32,36}... | collective-permute-start | bytes 393224 | tf_op jit(solution)/shard_map/ppermute | solution.py:543
  4.0 6.0 %collective-permute-start.5 = (bf16[32,8,256]{2,1,0:T(8,128)(2,1)S(1)}, bf16[32,8,256]{2,1,0:T(8,128)(2,1)S(1)}, u32[]{:S(2)}, u32[]{:S(2)}) collective-permute-start(bf16[32,8,256]{2,1,0:T(8,128)(2,1)S(1)} %reshape.65), channel_id=1, source_target_pairs={{4,0},{8,4},{12,8},{16,12},{20,16},{24,20},{28,24},{32,28},{36,32}... | collective-permute-start | bytes 393224 | tf_op jit(solution)/shard_map/ppermute | solution.py:543
  10.0 5.2 %regrid.1 = (bf16[69,1536]{1,0:T(8,128)(2,1)}, bf16[69,1536]{1,0:T(8,128)(2,1)}, bf16[69,512]{1,0:T(8,128)(2,1)}, bf16[69,512]{1,0:T(8,128)(2,1)}) custom-call(s32[64]{0:T(128)} %row_len.1, s32[1]{0:T(128)} %bitcast.1.sector, bf16[69,8,8,163]{3,2,1,0:T(8,128)(2,1)} %bitcast.9), custom_call_target="tpu_custom_call" | custom-call | tf_op jit(solution)/shard_map/regrid/pallas_call | solution.py:71
  15.2 0.0 collective-permute-start
  15.2 5.7 %collective-permute-start.1 = (bf16[69,512]{1,0:T(8,128)(2,1)}, bf16[69,512]{1,0:T(8,128)(2,1)S(1)}, u32[]{:S(2)}, u32[]{:S(2)}) collective-permute-start(bf16[69,512]{1,0:T(8,128)(2,1)} %get-tuple-element.24), channel_id=1, source_target_pairs={{4,0},{8,4},{12,8},{16,12},{20,16},{24,20},{28,24},{32,28},{36,32}... | collective-permute-start | bytes 211976 | tf_op jit(solution)/shard_map/ppermute | solution.py:543
  20.9 0.8 fusion
  21.7 0.9 fusion.2
  22.6 0.3 collective-permute-done.left
  22.8 0.0 copy-start
  22.8 0.1 fusion.5
  22.9 0.0 collective-permute-done.1.right
  22.9 0.0 copy-start.1
  22.9 0.1 fusion.6
  23.0 0.1 pad_maximum_fusion.2
  23.1 6.5 %collective-permute-start.2 = (bf16[69,320]{1,0:T(8,128)(2,1)S(1)}, bf16[69,320]{1,0:T(8,128)(2,1)S(1)}, u32[]{:S(2)}, u32[]{:S(2)}) collective-permute-start(bf16[69,320]{1,0:T(8,128)(2,1)S(1)} %pad_maximum_fusion.2), channel_id=1, source_target_pairs={{0,1},{1,2},{2,3},{4,5},{5,6},{6,7},{8,9},{9,10},{10,11},{12,13},{... | collective-permute-start | bytes 132488 | tf_op jit(solution)/shard_map/ppermute | solution.py:543
  29.6 0.0 collective-permute-done.4.cot_left
  29.6 0.0 copy-start.2
  29.7 0.0 collective-permute-done.5.cot_right
  29.7 0.0 copy-start.3
  29.8 1.9 %collective-permute-start.6 = (bf16[4,32,256]{2,1,0:T(8,128)(2,1)S(1)}, bf16[4,32,256]{2,1,0:T(8,128)(2,1)S(1)}, u32[]{:S(2)}, u32[]{:S(2)}) collective-permute-start(bf16[4,32,256]{2,1,0:T(8,128)(2,1)S(1)} %pad_maximum_fusion), channel_id=1, source_target_pairs={{0,1},{1,2},{2,3},{4,5},{5,6},{6,7},{8,9},{9,10},{10,11},{12,13},{... | collective-permute-start | bytes 196616 | tf_op jit(solution)/shard_map/ppermute | solution.py:543
  31.7 2.4 %collective-permute-start.7 = (bf16[4,32,256]{2,1,0:T(8,128)(2,1)S(1)}, bf16[4,32,256]{2,1,0:T(8,128)(2,1)S(1)}, u32[]{:S(2)}, u32[]{:S(2)}) collective-permute-start(bf16[4,32,256]{2,1,0:T(8,128)(2,1)S(1)} %pad_maximum_fusion.1), channel_id=1, source_target_pairs={{1,0},{2,1},{3,2},{5,4},{6,5},{7,6},{9,8},{10,9},{11,10},{13,12},{... | collective-permute-start | bytes 196616 | tf_op jit(solution)/shard_map/ppermute | solution.py:543
  34.1 0.1 pad_maximum_fusion.3
  34.2 1.9 %collective-permute-start.3 = (bf16[69,320]{1,0:T(8,128)(2,1)S(1)}, bf16[69,320]{1,0:T(8,128)(2,1)S(1)}, u32[]{:S(2)}, u32[]{:S(2)}) collective-permute-start(bf16[69,320]{1,0:T(8,128)(2,1)S(1)} %pad_maximum_fusion.3), channel_id=1, source_target_pairs={{1,0},{2,1},{3,2},{5,4},{6,5},{7,6},{9,8},{10,9},{11,10},{13,12},{... | collective-permute-start | bytes 132488 | tf_op jit(solution)/shard_map/ppermute | solution.py:543
  36.2 0.0 collective-permute-done.2.above
  36.2 0.0 copy-start.6
  36.2 5.0 %collective-permute-done.3.below = bf16[69,320]{1,0:T(8,128)(2,1)S(1)} collective-permute-done((bf16[69,320]{1,0:T(8,128)(2,1)S(1)}, bf16[69,320]{1,0:T(8,128)(2,1)S(1)}, u32[]{:S(2)}, u32[]{:S(2)}) %collective-permute-start.3) | collective-permute-done | bytes 44192 | tf_op jit(solution)/shard_map/ppermute | solution.py:543
  41.2 0.0 copy-start.7
  41.2 0.0 collective-permute-done.6.cot_above
  41.2 0.0 copy-start.4
  41.2 0.0 collective-permute-done.7.cot_below
  41.2 0.0 copy-start.5
  41.2 0.0 copy-done
  41.2 0.0 copy-done.1
  41.3 0.0 copy-done.2
  41.3 0.0 copy-done.3
  41.3 0.0 copy-done.6
  41.3 0.5 copy-done.7
  41.8 0.0 copy-done.4
  41.9 0.0 copy-done.5
  41.9 45.1 %both_blocks.1 = (bf16[64,24,256]{2,1,0:T(8,128)(2,1)}, bf16[128,2,8,128]{3,2,1,0:T(8,128)(2,1)}) custom-call(s32[1]{0:T(128)} %bitcast.lat, bf16[69,1536]{1,0:T(8,128)(2,1)} %get-tuple-element.21.high, bf16[69,1536]{1,0:T(8,128)(2,1)} %get-tuple-element.22.low, bf16[69,512]{1,0:T(8,128)(2,1)} %copy-done, bf16[69,512]{1,0:T(8,128)(2,1)} %copy-done.1, ...), custom_call_target="tpu_custom_call" | custom-call | tf_op jit(solution)/shard_map/both_blocks/pallas_call | solution.py:489
  87.0 20.3 %all_to_all.10 = bf16[128,2,8,128]{3,2,1,0:T(8,128)(2,1)S(1)} all-to-all(bf16[128,2,8,128]{3,2,1,0:T(8,128)(2,1)} %get-tuple-element.26), channel_id=1, replica_groups=mesh['lon'=32,'lat'=4] {'lon','lat'}, dimensions={0} | all-to-all | bytes 1048576 | tf_op jit(solution)/shard_map/all_to_all | solution.py:527
  107.3 0.1 reduce_sum.12
  107.4 0.1 tile.2
  107.5 17.9 %all_to_all.11.packed = bf16[128,2,8,128]{3,2,1,0:T(8,128)(2,1)} all-to-all(bf16[128,2,8,128]{3,2,1,0:T(8,128)(2,1)S(1)} %tile.2), channel_id=1, replica_groups=mesh['lon'=32,'lat'=4] {'lon','lat'}, dimensions={0} | all-to-all | bytes 1048576 | tf_op jit(solution)/shard_map/all_to_all | solution.py:529
  125.4 1.9 %unpack.1 = (f32[69,256]{1,0:T(8,128)}, f32[25,256]{1,0:T(8,128)}, f32[25,256]{1,0:T(8,128)}, f32[256,256]{1,0:T(8,128)}, f32[256,256]{1,0:T(8,128)}, /*index=5*/f32[1,256]{1,0:T(1,128)}, f32[1,256]{1,0:T(1,128)}) custom-call(bf16[128,2,8,128]{3,2,1,0:T(8,128)(2,1)} %all_to_all.11.packed), custom_call_target="tpu_custom_call" | custom-call | tf_op jit(solution)/shard_map/unpack/pallas_call | solution.py:531
  (10 shorter events, 0.2 us)
Async XLA Ops:
  1.8 27.8 %collective-permute-start.4 = (bf16[32,8,256]{2,1,0:T(8,128)(2,1)S(1)}, bf16[32,8,256]{2,1,0:T(8,128)(2,1)S(1)}, u32[]{:S(2)}, u32[]{:S(2)}) collective-permute-start(bf16[32,8,256]{2,1,0:T(8,128)(2,1)S(1)} %reshape.64), channel_id=1, source_target_pairs={{0,4},{4,8},{8,12},{12,16},{16,20},{20,24},{24,28},{28,32},{32,36}... | collective-permute-start | bytes 393224 | tf_op jit(solution)/shard_map/ppermute | solution.py:543
  4.0 25.7 %collective-permute-start.5 = (bf16[32,8,256]{2,1,0:T(8,128)(2,1)S(1)}, bf16[32,8,256]{2,1,0:T(8,128)(2,1)S(1)}, u32[]{:S(2)}, u32[]{:S(2)}) collective-permute-start(bf16[32,8,256]{2,1,0:T(8,128)(2,1)S(1)} %reshape.65), channel_id=1, source_target_pairs={{4,0},{8,4},{12,8},{16,12},{20,16},{24,20},{28,24},{32,28},{36,32}... | collective-permute-start | bytes 393224 | tf_op jit(solution)/shard_map/ppermute | solution.py:543
  15.2 7.6 %collective-permute-start = (bf16[69,512]{1,0:T(8,128)(2,1)}, bf16[69,512]{1,0:T(8,128)(2,1)S(1)}, u32[]{:S(2)}, u32[]{:S(2)}) collective-permute-start(bf16[69,512]{1,0:T(8,128)(2,1)} %get-tuple-element.23), channel_id=1, source_target_pairs={{0,4},{4,8},{8,12},{12,16},{16,20},{20,24},{24,28},{28,32},{32,36}... | collective-permute-start | bytes 211976 | tf_op jit(solution)/shard_map/ppermute | solution.py:543
  15.2 7.7 %collective-permute-start.1 = (bf16[69,512]{1,0:T(8,128)(2,1)}, bf16[69,512]{1,0:T(8,128)(2,1)S(1)}, u32[]{:S(2)}, u32[]{:S(2)}) collective-permute-start(bf16[69,512]{1,0:T(8,128)(2,1)} %get-tuple-element.24), channel_id=1, source_target_pairs={{4,0},{8,4},{12,8},{16,12},{20,16},{24,20},{28,24},{32,28},{36,32}... | collective-permute-start | bytes 211976 | tf_op jit(solution)/shard_map/ppermute | solution.py:543
  22.8 18.4 %copy-start = (bf16[69,512]{1,0:T(8,128)(2,1)}, bf16[69,512]{1,0:T(8,128)(2,1)S(1)}, u32[]{:S(2)}) copy-start(bf16[69,512]{1,0:T(8,128)(2,1)S(1)} %collective-permute-done.left) | copy-start | bytes 211972
  22.9 18.3 %copy-start.1 = (bf16[69,512]{1,0:T(8,128)(2,1)}, bf16[69,512]{1,0:T(8,128)(2,1)S(1)}, u32[]{:S(2)}) copy-start(bf16[69,512]{1,0:T(8,128)(2,1)S(1)} %collective-permute-done.1.right) | copy-start | bytes 211972
  23.1 13.1 %collective-permute-start.2 = (bf16[69,320]{1,0:T(8,128)(2,1)S(1)}, bf16[69,320]{1,0:T(8,128)(2,1)S(1)}, u32[]{:S(2)}, u32[]{:S(2)}) collective-permute-start(bf16[69,320]{1,0:T(8,128)(2,1)S(1)} %pad_maximum_fusion.2), channel_id=1, source_target_pairs={{0,1},{1,2},{2,3},{4,5},{5,6},{6,7},{8,9},{9,10},{10,11},{12,13},{... | collective-permute-start | bytes 132488 | tf_op jit(solution)/shard_map/ppermute | solution.py:543
  29.6 11.6 %copy-start.2 = (bf16[32,8,256]{2,1,0:T(8,128)(2,1)}, bf16[32,8,256]{2,1,0:T(8,128)(2,1)S(1)}, u32[]{:S(2)}) copy-start(bf16[32,8,256]{2,1,0:T(8,128)(2,1)S(1)} %collective-permute-done.4.cot_left) | copy-start | bytes 393220
  29.7 11.6 %copy-start.3 = (bf16[32,8,256]{2,1,0:T(8,128)(2,1)}, bf16[32,8,256]{2,1,0:T(8,128)(2,1)S(1)}, u32[]{:S(2)}) copy-start(bf16[32,8,256]{2,1,0:T(8,128)(2,1)S(1)} %collective-permute-done.5.cot_right) | copy-start | bytes 393220
  29.8 11.5 %collective-permute-start.6 = (bf16[4,32,256]{2,1,0:T(8,128)(2,1)S(1)}, bf16[4,32,256]{2,1,0:T(8,128)(2,1)S(1)}, u32[]{:S(2)}, u32[]{:S(2)}) collective-permute-start(bf16[4,32,256]{2,1,0:T(8,128)(2,1)S(1)} %pad_maximum_fusion), channel_id=1, source_target_pairs={{0,1},{1,2},{2,3},{4,5},{5,6},{6,7},{8,9},{9,10},{10,11},{12,13},{... | collective-permute-start | bytes 196616 | tf_op jit(solution)/shard_map/ppermute | solution.py:543
  31.7 9.5 %collective-permute-start.7 = (bf16[4,32,256]{2,1,0:T(8,128)(2,1)S(1)}, bf16[4,32,256]{2,1,0:T(8,128)(2,1)S(1)}, u32[]{:S(2)}, u32[]{:S(2)}) collective-permute-start(bf16[4,32,256]{2,1,0:T(8,128)(2,1)S(1)} %pad_maximum_fusion.1), channel_id=1, source_target_pairs={{1,0},{2,1},{3,2},{5,4},{6,5},{7,6},{9,8},{10,9},{11,10},{13,12},{... | collective-permute-start | bytes 196616 | tf_op jit(solution)/shard_map/ppermute | solution.py:543
  34.2 7.0 %collective-permute-start.3 = (bf16[69,320]{1,0:T(8,128)(2,1)S(1)}, bf16[69,320]{1,0:T(8,128)(2,1)S(1)}, u32[]{:S(2)}, u32[]{:S(2)}) collective-permute-start(bf16[69,320]{1,0:T(8,128)(2,1)S(1)} %pad_maximum_fusion.3), channel_id=1, source_target_pairs={{1,0},{2,1},{3,2},{5,4},{6,5},{7,6},{9,8},{10,9},{11,10},{13,12},{... | collective-permute-start | bytes 132488 | tf_op jit(solution)/shard_map/ppermute | solution.py:543
  36.2 5.1 %copy-start.6 = (bf16[69,320]{1,0:T(8,128)(2,1)}, bf16[69,320]{1,0:T(8,128)(2,1)S(1)}, u32[]{:S(2)}) copy-start(bf16[69,320]{1,0:T(8,128)(2,1)S(1)} %collective-permute-done.2.above) | copy-start | bytes 132484
  41.2 0.6 copy-start.7
  41.2 0.6 copy-start.4
  41.2 0.7 copy-start.5

commit v4 on v3

--- a/solution.py
+++ b/solution.py
@@ -28,13 +28,17 @@
 STRIP = 8 * HALO
 
 
-def regrid_kernel(row_len, sector, points, high, low, west, east, *, lon_total):
+def regrid_kernel(row_len, sector, points, values, west, east, *, lon_total):
     first = (sector[0] * COLS).astype(F32)
     whole = lon_total // 4
     lane = lax.broadcasted_iota(jnp.int32, (8, GROUP), 1)
     row = lane % 8
     cell = first + (lane // 8).astype(F32)
     own = lax.broadcasted_iota(jnp.int32, (8, GROUP), 0) == row
+    own = jnp.where(own, 1.0 / whole, 0.0)
+    every8 = lax.broadcasted_iota(jnp.int32, (VARS, 8 * VARS), 1) // 8
+    fold = jnp.where(every8 == lax.broadcasted_iota(jnp.int32, every8.shape, 0), 1.0, 0.0)
+    fold = fold.astype(BF16)
     mark = lax.broadcasted_iota(jnp.int32, (points.shape[3], GROUP), 0).astype(F32)
     found = []
     for k in range(points.shape[1]):
@@ -52,12 +56,9 @@
         )
         rows = points[:, k].reshape(VARS * 8, points.shape[3])
         every = jnp.dot(rows, mix.astype(BF16), preferred_element_type=F32)
-        kept = jnp.where(own[None], every.reshape(VARS, 8, GROUP), 0.0)
-        found.append(jnp.sum(kept, 1) * (1.0 / whole))
-    values = jnp.concatenate(found, 1)
-    rounded = values.astype(BF16)
-    high[...] = rounded
-    low[...] = (values - rounded.astype(F32)).astype(BF16)
+        kept = (every.reshape(VARS, 8, GROUP) * own[None]).reshape(VARS * 8, GROUP)
+        found.append(jnp.dot(fold, kept.astype(BF16), preferred_element_type=F32))
+    values[...] = jnp.concatenate(found, 1).astype(BF16)
     west[...] = jnp.concatenate([f[:, :STRIP] for f in found], 1).astype(BF16)
     east[...] = jnp.concatenate([f[:, GROUP - STRIP :] for f in found], 1).astype(BF16)
 
@@ -76,12 +77,11 @@
             in_specs=[pl.BlockSpec((nvars, groups, 8, slots), lambda i, *_: (0, i, 0, 0))],
             out_specs=[
                 pl.BlockSpec((nvars, groups * GROUP), lambda i, *_: (0, i)),
-                pl.BlockSpec((nvars, groups * GROUP), lambda i, *_: (0, i)),
                 pl.BlockSpec((nvars, groups * STRIP), lambda i, *_: (0, i)),
                 pl.BlockSpec((nvars, groups * STRIP), lambda i, *_: (0, i)),
             ],
         ),
-        out_shape=[full, full, strips, strips],
+        out_shape=[full, strips, strips],
         name="regrid",
     )(
         row_len,
@@ -117,9 +117,15 @@
     return sums
 
 
+def own_tiles(x):
+    later = lax.broadcasted_iota(jnp.int32, (8, 128), 0) >= 4
+    return jnp.stack([jnp.where(later, x[0], x[3]), x[1], x[2]])
+
+
 class TapSums:
     def __init__(self, store, half, centre):
         self.store, self.half, self.centre, self.live = store, half, centre, {}
+        self.seen = self.own = None
 
     def __call__(self, a, e, r, x):
         if a is None:
@@ -128,16 +134,20 @@
             self.live = {}
             return
         tap = 24 - (5 * a + e)
+        if x.shape[0] == 4:
+            if self.seen is not x:
+                self.seen, self.own = x, own_tiles(x)
+            x = self.own
         term = jnp.sum(self.centre[r] * x, 0)
         self.live[tap] = term if tap not in self.live else self.live[tap] + term
 
 
 def blocks_kernel(
-    lat, high, low, left, right, above, below, cot, cot_left, cot_right, cot_above, cot_below,
+    lat, regridded, left, right, above, below, cot, cot_left, cot_right,
     w_embed, kernel1, gain1, point1, kernel2, gain2, point2,
     out, packed,
     x0, cots, d, h1, xhat1, scale1, slope1, dd2, g1, dd1,
-    taps1, taps2, flip1, flip2, turned1, turned2,
+    taps1, taps2, flip1, flip2, half1, half2, turned1, turned2,
     u1, dp1, u2, dp2, g0, gk1, gk2, gg1, gg2, swap, lifted,
     *, lat_devices,
 ):
@@ -151,8 +161,10 @@
             flip1[h, 24 - k] = one
             taps2[h, k] = two
             flip2[h, 24 - k] = two
-    turned1[...] = jnp.transpose(point1[...].astype(F32)).astype(BF16)
-    turned2[...] = jnp.transpose(point2[...].astype(F32)).astype(BF16)
+    for point, half, turned in ((point1, half1, turned1), (point2, half2, turned2)):
+        value = point[...].astype(F32) * 0.5
+        half[...] = value.astype(BF16)
+        turned[...] = jnp.transpose(value).astype(BF16)
     zeros = jnp.zeros((8, 128), F32)
     for h in (0, 1):
         for ref in (gg1, gg2):
@@ -185,14 +197,16 @@
         middle = slice(2 * GROUP * i, 2 * GROUP * (i + 1))
         west = across(left[:, edge], weight)
         east = across(right[:, edge], weight)
-        centre = across(high[:, middle], weight) + across(low[:, middle], weight)
+        centre = across(regridded[:, middle], weight)
         for k in (0, 1):
             spot = 8 * PITCH * (2 * i + k)
             embed(spot, west[STRIP * k : STRIP * (k + 1)])
             embed(spot + STRIP, centre[GROUP * k : GROUP * (k + 1)])
             embed(spot + STRIP + GROUP, east[STRIP * k : STRIP * (k + 1)])
-    embed(8 * PITCH * (ROWS // 8), across(above[...], weight))
-    embed(8 * PITCH * (ROWS // 8 + 1), across(below[...], weight))
+    for k, given in ((0, above), (1, below)):
+        spot = 8 * PITCH * (ROWS // 8 + k)
+        embed(spot, across(given[128 : 128 + VARS], weight))
+        embed(spot + CHANS, across(given[208 : 208 + VARS, : 8 * PITCH - CHANS], weight))
 
     def unravel(i, carry):
         spread(8 * PITCH * i, HALO + 8 * i)
@@ -220,8 +234,9 @@
 
     lax.fori_loop(0, ROWS // 2, fill, 0)
     for k in range(4):
-        put(k + 4, cot_above[k].astype(F32))
-        put(k + HALO + ROWS, cot_below[k].astype(F32))
+        rows = slice(INNER * k, INNER * (k + 1))
+        put(k + 4, above[rows].astype(F32))
+        put(k + HALO + ROWS, below[rows].astype(F32))
 
     def get(ref, start, count):
         return [ref[h, pl.ds(pl.multiple_of(start, 8), count), :] for h in (0, 1)]
@@ -260,9 +275,9 @@
             jnp.concatenate(u, 1).astype(BF16), point[...], preferred_element_type=F32
         )
         p = [p[:, s] for s in halves]
-        sig = [0.5 * jnp.tanh(0.5 * v) + 0.5 for v in p]
-        silu = [p[h] * sig[h] for h in (0, 1)]
-        slope = [sig[h] + silu[h] * (1.0 - sig[h]) for h in (0, 1)]
+        rise = [jnp.tanh(v) + 1.0 for v in p]
+        silu = [p[h] * rise[h] for h in (0, 1)]
+        slope = [rise[h] + silu[h] * (2.0 - rise[h]) for h in (0, 1)]
         return u, silu, slope
 
     def through_norm(grad, slope, xhat, scale, gain, turned):
@@ -302,7 +317,7 @@
     def first_mix(i):
         start = at(2) + i * size
         scale, xhat = normalised(get(d, start, size))
-        _, silu, slope = activated(xhat, gains(gain1), point1)
+        _, silu, slope = activated(xhat, gains(gain1), half1)
         x = get(x0, start, size)
         keep(h1, start, [(x[h] + silu[h]).astype(BF16).astype(F32) for h in (0, 1)])
         keep(xhat1, start, xhat)
@@ -332,7 +347,7 @@
         start = inner(row)
         scale, xhat = normalised(get(d, start, 4 * INNER))
         gain = gains(gain2)
-        u, silu, slope = activated(xhat, gain, point2)
+        u, silu, slope = activated(xhat, gain, half2)
         dp, both, dd = through_norm(
             get(cots, start, 4 * INNER), slope, xhat, scale, gain, turned2
         )
@@ -355,13 +370,10 @@
             total.append(jnp.concatenate(rows, 0))
         out[pl.ds(i * 4, 4)] = jnp.concatenate(total, 1).reshape(4, COLS, CHANS).astype(BF16)
 
-    def outer(k, carry):
-        row = 4 + k * (ROWS + 4)
+    for row in (4, HALO + ROWS):
         second_conv(row)
+    for row in (4, HALO + ROWS):
         second_mix(row, None)
-        return carry
-
-    lax.fori_loop(0, 2, outer, 0)
     pipeline(
         ROWS // 4,
         lambda i: second_conv(HALO + 4 * i),
@@ -375,14 +387,8 @@
             visit = None
             if local:
                 centre = [
-                    h1[h, pl.ds(at(row + r) + 4, INNER), :].reshape(4, 8, 128)
+                    own_tiles(h1[h, pl.ds(at(row + r) + 4, INNER), :].reshape(4, 8, 128))
                     for r in range(rows)
-                ]
-                centre = [
-                    jnp.stack(
-                        [jnp.where(later, c[0], 0.0), c[1], c[2], jnp.where(later, 0.0, c[3])]
-                    )
-                    for c in centre
                 ]
                 visit = TapSums(gk2, h, centre)
             sums = joined(conv(dd2, h, start, INNER, rows, INNER, flip2, visit))
@@ -408,13 +414,10 @@
             gain_sums(gg1, both)
             result(local)
 
-    def margin(k, carry):
-        row = 6 + k * (ROWS + 2)
+    for row in (6, HALO + ROWS):
         third_conv(row, 2, False)
+    for row in (6, HALO + ROWS):
         third_mix(row, 2, None)
-        return carry
-
-    lax.fori_loop(0, 2, margin, 0)
     pipeline(
         ROWS // 4,
         lambda i: third_conv(HALO + 4 * i, 4, True),
@@ -455,10 +458,10 @@
         for h in (0, 1):
             packed[place : place + rows // 8, h] = value[:, halves[h]].reshape(rows // 8, 8, 128)
 
-    pack(0, across(u1[...], dp1[...]))
-    pack(32, across(u2[...], dp2[...]))
+    pack(0, across(u1[...], dp1[...]) * 0.5)
+    pack(32, across(u2[...], dp2[...]) * 0.5)
     field = jnp.concatenate([g0[h] for h in (0, 1)], 1).astype(BF16)
-    embedded = jnp.dot(high[...], field, preferred_element_type=F32)
+    embedded = jnp.dot(regridded[...], field, preferred_element_type=F32)
 
     def gain_row(ref, gain):
         total = [jnp.sum(ref[h], 0, keepdims=True) for h in (0, 1)]
@@ -497,7 +500,7 @@
         scratch_shapes=[wide, slim, wide, wide, wide, pltpu.VMEM((FLAT, 128), F32), wide]
         + [slim] * 3
         + [taps] * 4
-        + [square] * 2
+        + [square] * 4
         + [local] * 4
         + [pltpu.VMEM((2, ROWS * COLS, 128), F32)]
         + [taps] * 2
@@ -552,29 +555,31 @@
         "lon",
         True,
     )
-    high, low, west, east = regrid(jnp.swapaxes(points, 0, 1), row_len, lon_total)
+    values, west, east = regrid(jnp.swapaxes(points, 0, 1), row_len, lon_total)
     left, right = shifted(west, east, "lon", True)
 
-    def cot_band(rows, pairs):
+    def band(rows, pairs, lanes, edge):
         sides = [c[pairs].reshape(4, 4, CHANS) for c in (cot_left, cot_right)]
-        return jnp.concatenate([sides[0], cotangent[rows], sides[1]], 1)
-
-    cot_above, cot_below = shifted(
-        cot_band(slice(0, 4), slice(0, 2)),
-        cot_band(slice(ROWS - 4, ROWS), slice(ROWS // 2 - 2, ROWS // 2)),
+        given = jnp.concatenate([sides[0], cotangent[rows], sides[1]], 1).reshape(-1, CHANS)
+        field = jnp.concatenate([left[:, edge], values[:, lanes], right[:, edge]], 1)
+        pieces = [field[:, :CHANS], field[:, CHANS:]]
+        pieces = [
+            jnp.pad(x, ((0, 80 - VARS), (0, CHANS - x.shape[1]))) for x in pieces
+        ]
+        return jnp.concatenate([given, *pieces], 0)
+
+    above, below = shifted(
+        band(slice(0, 4), slice(0, 2), slice(0, GROUP), slice(0, STRIP)),
+        band(
+            slice(ROWS - 4, ROWS),
+            slice(ROWS // 2 - 2, ROWS // 2),
+            slice(GROUP * (ROWS // 8 - 1), GROUP * (ROWS // 8)),
+            slice(STRIP * (ROWS // 8 - 1), STRIP * (ROWS // 8)),
+        ),
         "lat",
         False,
     )
-    above, below = shifted(
-        jnp.concatenate([left[:, :STRIP], high[:, :GROUP], right[:, :STRIP]], 1),
-        jnp.concatenate([left[:, -STRIP:], high[:, -GROUP:], right[:, -STRIP:]], 1),
-        "lat",
-        False,
-    )
-    fields = (
-        high, low, left, right, above, below,
-        cotangent, cot_left, cot_right, cot_above, cot_below,
-    )
+    fields = (values, left, right, above, below, cotangent, cot_left, cot_right)
     weights = (
         w_embed, kernel1, gain1.reshape(1, CHANS), point1,
         kernel2, gain2.reshape(1, CHANS), point2,

time: 128 us -> 123 us (0.961)
  starting transfers between devices: 26.5 us -> 22.9 us
  Pallas kernels: 52.2 us -> 50.9 us
    ppermute x8 -> x6, starting transfers between devices: 26.5 us -> 22.9 us  [shifted(): return (lax.ppermute(after, axis, up), lax.ppermute(before, axis, down))]
    pallas_call x1, Pallas kernels: 45.1 us -> 42.9 us  [blocks(): pl.pallas_call(functools.partial(blocks_kernel, lat_devices=lat_devices),...]
    ppermute x8 -> x6, waiting for transfers between devices: 5.29 us -> 6.25 us  [shifted(): return (lax.ppermute(after, axis, up), lax.ppermute(before, axis, down))]
  transfers between devices with their start and end apart: 8 -> 6, of which waited for: 2 -> 3; matrix products, arithmetic and copies ran while one was open for 2% -> 2% of each run, Pallas kernels for 4% -> 5%
where the time goes in v4:
time: 123 us
  Pallas kernels  50.9 us (41%)
  blocking collectives  37.7 us (31%)
  starting transfers between devices  22.9 us (19%)
  waiting for transfers between devices  6.25 us (5%)
  local copies, waits for them, and re-layouts  3.83 us (3%)
    pallas_call x1, Pallas kernels, blocks(): pl.pallas_call(functools.partial(blocks_kernel, lat_devices=lat_devices),...  42.9 us
    ppermute x6, starting transfers between devices, shifted(): return (lax.ppermute(after, axis, up), lax.ppermute(before, axis, down))  22.9 us
    all_to_all x1, blocking collectives, summed(): parts = lax.all_to_all(packed, AXES, 0, 0, tiled=True)  19.7 us
    all_to_all x1, blocking collectives, summed(): lax.all_to_all(jnp.tile(mine, (devices, 1, 1, 1)), AXES, 0, 0, tiled=True)  17.9 us
    ppermute x6, waiting for transfers between devices, shifted(): return (lax.ppermute(after, axis, up), lax.ppermute(before, axis, down))  6.25 us
    pallas_call x1, Pallas kernels, regrid(): pl.pallas_call(functools.partial(regrid_kernel, lon_total=lon_total), gri...  6.09 us
  transfers between devices with their start and end apart: 6, of which 3 were waited for; matrix products, arithmetic and copies ran while one was open for 2% of the time, Pallas kernels for 5%

profile of v4, /device:TPU:1, one launch (start us, length us, event | category | flops | bytes accessed | tf_op | source)
XLA Modules:
  0.0 122.7 jit_solution(10981316740649804226)
XLA Ops:
  0.6 1.1 fusion.11
  1.8 8.0 %collective-permute-start.3 = (bf16[32,8,256]{2,1,0:T(8,128)(2,1)S(1)}, bf16[32,8,256]{2,1,0:T(8,128)(2,1)S(1)}, u32[]{:S(2)}, u32[]{:S(2)}) collective-permute-start(bf16[32,8,256]{2,1,0:T(8,128)(2,1)S(1)} %reshape.72), channel_id=1, source_target_pairs={{4,0},{8,4},{12,8},{16,12},{20,16},{24,20},{28,24},{32,28},{36,32}... | collective-permute-start | bytes 393224 | tf_op jit(solution)/shard_map/ppermute | solution.py:546
  9.9 0.1 collective-permute-start.2
  10.0 6.1 %regrid.1 = (bf16[69,1536]{1,0:T(8,128)(2,1)}, bf16[69,512]{1,0:T(8,128)(2,1)}, bf16[69,512]{1,0:T(8,128)(2,1)}) custom-call(s32[64]{0:T(128)} %row_len.1, s32[1]{0:T(128)} %bitcast.1.sector, bf16[69,8,8,163]{3,2,1,0:T(8,128)(2,1)} %bitcast.11), custom_call_target="tpu_custom_call" | custom-call | tf_op jit(solution)/shard_map/regrid/pallas_call | solution.py:72
  16.1 0.0 collective-permute-start
  16.1 5.7 %collective-permute-start.1 = (bf16[69,512]{1,0:T(8,128)(2,1)}, bf16[69,512]{1,0:T(8,128)(2,1)S(1)}, u32[]{:S(2)}, u32[]{:S(2)}) collective-permute-start(bf16[69,512]{1,0:T(8,128)(2,1)} %get-tuple-element.22), channel_id=1, source_target_pairs={{4,0},{8,4},{12,8},{16,12},{20,16},{24,20},{28,24},{32,28},{36,32}... | collective-permute-start | bytes 211976 | tf_op jit(solution)/shard_map/ppermute | solution.py:546
  21.8 0.8 fusion.10
  22.6 0.9 fusion.12
  23.5 0.2 collective-permute-done.left
  23.7 0.0 copy-start.2
  23.7 0.1 fusion.15
  23.8 0.0 collective-permute-done.1.right
  23.8 0.0 copy-start.3
  23.8 0.1 fusion.16
  23.9 0.1 fusion.9
  23.9 0.1 fusion.8
  24.0 0.0 collective-permute-done.3.cot_right
  24.0 0.0 copy-start
  24.1 0.0 collective-permute-done.2.cot_left
  24.1 0.0 copy-start.1
  24.2 0.1 pad_maximum_fusion
  24.2 7.1 %collective-permute-start.4 = (bf16[288,256]{1,0:T(8,128)(2,1)S(1)}, bf16[288,256]{1,0:T(8,128)(2,1)S(1)}, u32[]{:S(2)}, u32[]{:S(2)}) collective-permute-start(bf16[288,256]{1,0:T(8,128)(2,1)S(1)} %fusion.2), channel_id=1, source_target_pairs={{0,1},{1,2},{2,3},{4,5},{5,6},{6,7},{8,9},{9,10},{10,11},{12,13},{... | collective-permute-start | bytes 442376 | tf_op jit(solution)/shard_map/ppermute | solution.py:546
  31.4 1.9 %collective-permute-start.5 = (bf16[288,256]{1,0:T(8,128)(2,1)S(1)}, bf16[288,256]{1,0:T(8,128)(2,1)S(1)}, u32[]{:S(2)}, u32[]{:S(2)}) collective-permute-start(bf16[288,256]{1,0:T(8,128)(2,1)S(1)} %fusion.3), channel_id=1, source_target_pairs={{1,0},{2,1},{3,2},{5,4},{6,5},{7,6},{9,8},{10,9},{11,10},{13,12},{... | collective-permute-start | bytes 442376 | tf_op jit(solution)/shard_map/ppermute | solution.py:546
  33.3 0.1 collective-permute-done.4.above
  33.4 0.0 copy-start.4
  33.4 5.9 %collective-permute-done.5.below = bf16[288,256]{1,0:T(8,128)(2,1)S(1)} collective-permute-done((bf16[288,256]{1,0:T(8,128)(2,1)S(1)}, bf16[288,256]{1,0:T(8,128)(2,1)S(1)}, u32[]{:S(2)}, u32[]{:S(2)}) %collective-permute-start.5) | collective-permute-done | bytes 147488 | tf_op jit(solution)/shard_map/ppermute | solution.py:546
  39.3 0.0 copy-start.5
  39.3 0.0 copy-done.2
  39.3 0.0 copy-done.3
  39.3 0.0 copy-done
  39.3 0.0 copy-done.1
  39.4 0.0 copy-done.4
  39.4 0.6 copy-done.5
  40.0 42.9 %both_blocks.1 = (bf16[64,24,256]{2,1,0:T(8,128)(2,1)}, bf16[128,2,8,128]{3,2,1,0:T(8,128)(2,1)}) custom-call(s32[1]{0:T(128)} %bitcast.lat, bf16[69,1536]{1,0:T(8,128)(2,1)} %get-tuple-element.20.regridded, bf16[69,512]{1,0:T(8,128)(2,1)} %copy-done.2, bf16[69,512]{1,0:T(8,128)(2,1)} %copy-done.3, bf16[288,256]{1,0:T(8,128)(2,1)} %copy-done.4, ...), custom_call_target="tpu_custom_call" | custom-call | tf_op jit(solution)/shard_map/both_blocks/pallas_call | solution.py:492
  82.9 19.7 %all_to_all.10 = bf16[128,2,8,128]{3,2,1,0:T(8,128)(2,1)S(1)} all-to-all(bf16[128,2,8,128]{3,2,1,0:T(8,128)(2,1)} %get-tuple-element.24), channel_id=1, replica_groups=mesh['lon'=32,'lat'=4] {'lon','lat'}, dimensions={0} | all-to-all | bytes 1048576 | tf_op jit(solution)/shard_map/all_to_all | solution.py:530
  102.6 0.1 reduce_sum.12
  102.8 0.1 tile.2
  102.8 17.9 %all_to_all.11.packed = bf16[128,2,8,128]{3,2,1,0:T(8,128)(2,1)} all-to-all(bf16[128,2,8,128]{3,2,1,0:T(8,128)(2,1)S(1)} %tile.2), channel_id=1, replica_groups=mesh['lon'=32,'lat'=4] {'lon','lat'}, dimensions={0} | all-to-all | bytes 1048576 | tf_op jit(solution)/shard_map/all_to_all | solution.py:532
  120.8 1.9 %unpack.1 = (f32[69,256]{1,0:T(8,128)}, f32[25,256]{1,0:T(8,128)}, f32[25,256]{1,0:T(8,128)}, f32[256,256]{1,0:T(8,128)}, f32[256,256]{1,0:T(8,128)}, /*index=5*/f32[1,256]{1,0:T(1,128)}, f32[1,256]{1,0:T(1,128)}) custom-call(bf16[128,2,8,128]{3,2,1,0:T(8,128)(2,1)} %all_to_all.11.packed), custom_call_target="tpu_custom_call" | custom-call | tf_op jit(solution)/shard_map/unpack/pallas_call | solution.py:534
  (10 shorter events, 0.2 us)
Async XLA Ops:
  1.8 22.2 %collective-permute-start.3 = (bf16[32,8,256]{2,1,0:T(8,128)(2,1)S(1)}, bf16[32,8,256]{2,1,0:T(8,128)(2,1)S(1)}, u32[]{:S(2)}, u32[]{:S(2)}) collective-permute-start(bf16[32,8,256]{2,1,0:T(8,128)(2,1)S(1)} %reshape.72), channel_id=1, source_target_pairs={{4,0},{8,4},{12,8},{16,12},{20,16},{24,20},{28,24},{32,28},{36,32}... | collective-permute-start | bytes 393224 | tf_op jit(solution)/shard_map/ppermute | solution.py:546
  9.9 14.2 %collective-permute-start.2 = (bf16[32,8,256]{2,1,0:T(8,128)(2,1)S(1)}, bf16[32,8,256]{2,1,0:T(8,128)(2,1)S(1)}, u32[]{:S(2)}, u32[]{:S(2)}) collective-permute-start(bf16[32,8,256]{2,1,0:T(8,128)(2,1)S(1)} %reshape.70), channel_id=1, source_target_pairs={{0,4},{4,8},{8,12},{12,16},{16,20},{20,24},{24,28},{28,32},{32,36}... | collective-permute-start | bytes 393224 | tf_op jit(solution)/shard_map/ppermute | solution.py:546
  16.1 7.6 %collective-permute-start = (bf16[69,512]{1,0:T(8,128)(2,1)}, bf16[69,512]{1,0:T(8,128)(2,1)S(1)}, u32[]{:S(2)}, u32[]{:S(2)}) collective-permute-start(bf16[69,512]{1,0:T(8,128)(2,1)} %get-tuple-element.21), channel_id=1, source_target_pairs={{0,4},{4,8},{8,12},{12,16},{16,20},{20,24},{24,28},{28,32},{32,36}... | collective-permute-start | bytes 211976 | tf_op jit(solution)/shard_map/ppermute | solution.py:546
  16.1 7.7 %collective-permute-start.1 = (bf16[69,512]{1,0:T(8,128)(2,1)}, bf16[69,512]{1,0:T(8,128)(2,1)S(1)}, u32[]{:S(2)}, u32[]{:S(2)}) collective-permute-start(bf16[69,512]{1,0:T(8,128)(2,1)} %get-tuple-element.22), channel_id=1, source_target_pairs={{4,0},{8,4},{12,8},{16,12},{20,16},{24,20},{28,24},{32,28},{36,32}... | collective-permute-start | bytes 211976 | tf_op jit(solution)/shard_map/ppermute | solution.py:546
  23.7 15.7 %copy-start.2 = (bf16[69,512]{1,0:T(8,128)(2,1)}, bf16[69,512]{1,0:T(8,128)(2,1)S(1)}, u32[]{:S(2)}) copy-start(bf16[69,512]{1,0:T(8,128)(2,1)S(1)} %collective-permute-done.left) | copy-start | bytes 211972
  23.8 15.6 %copy-start.3 = (bf16[69,512]{1,0:T(8,128)(2,1)}, bf16[69,512]{1,0:T(8,128)(2,1)S(1)}, u32[]{:S(2)}) copy-start(bf16[69,512]{1,0:T(8,128)(2,1)S(1)} %collective-permute-done.1.right) | copy-start | bytes 211972
  24.0 15.3 %copy-start = (bf16[32,8,256]{2,1,0:T(8,128)(2,1)}, bf16[32,8,256]{2,1,0:T(8,128)(2,1)S(1)}, u32[]{:S(2)}) copy-start(bf16[32,8,256]{2,1,0:T(8,128)(2,1)S(1)} %collective-permute-done.3.cot_right) | copy-start | bytes 393220
  24.1 15.3 %copy-start.1 = (bf16[32,8,256]{2,1,0:T(8,128)(2,1)}, bf16[32,8,256]{2,1,0:T(8,128)(2,1)S(1)}, u32[]{:S(2)}) copy-start(bf16[32,8,256]{2,1,0:T(8,128)(2,1)S(1)} %collective-permute-done.2.cot_left) | copy-start | bytes 393220
  24.2 9.2 %collective-permute-start.4 = (bf16[288,256]{1,0:T(8,128)(2,1)S(1)}, bf16[288,256]{1,0:T(8,128)(2,1)S(1)}, u32[]{:S(2)}, u32[]{:S(2)}) collective-permute-start(bf16[288,256]{1,0:T(8,128)(2,1)S(1)} %fusion.2), channel_id=1, source_target_pairs={{0,1},{1,2},{2,3},{4,5},{5,6},{6,7},{8,9},{9,10},{10,11},{12,13},{... | collective-permute-start | bytes 442376 | tf_op jit(solution)/shard_map/ppermute | solution.py:546
  31.4 8.0 %collective-permute-start.5 = (bf16[288,256]{1,0:T(8,128)(2,1)S(1)}, bf16[288,256]{1,0:T(8,128)(2,1)S(1)}, u32[]{:S(2)}, u32[]{:S(2)}) collective-permute-start(bf16[288,256]{1,0:T(8,128)(2,1)S(1)} %fusion.3), channel_id=1, source_target_pairs={{1,0},{2,1},{3,2},{5,4},{6,5},{7,6},{9,8},{10,9},{11,10},{13,12},{... | collective-permute-start | bytes 442376 | tf_op jit(solution)/shard_map/ppermute | solution.py:546
  33.4 5.9 %copy-start.4 = (bf16[288,256]{1,0:T(8,128)(2,1)}, bf16[288,256]{1,0:T(8,128)(2,1)S(1)}, u32[]{:S(2)}) copy-start(bf16[288,256]{1,0:T(8,128)(2,1)S(1)} %collective-permute-done.4.above) | copy-start | bytes 442372
  39.3 0.7 copy-start.5

commit v5 on v4

--- a/solution.py
+++ b/solution.py
@@ -28,7 +28,16 @@
 STRIP = 8 * HALO
 
 
-def regrid_kernel(row_len, sector, points, values, west, east, *, lon_total):
+def regrid_kernel(row_len, sector, points, values, west, east, held, arrived, *, lon_total):
+    batch = held.shape[2]
+    copies = [
+        pltpu.make_async_copy(
+            points.at[:, batch * i : batch * (i + 1)], held.at[i], arrived.at[i]
+        )
+        for i in range(held.shape[0])
+    ]
+    for copy in copies:
+        copy.start()
     first = (sector[0] * COLS).astype(F32)
     whole = lon_total // 4
     lane = lax.broadcasted_iota(jnp.int32, (8, GROUP), 1)
@@ -39,55 +48,103 @@
     every8 = lax.broadcasted_iota(jnp.int32, (VARS, 8 * VARS), 1) // 8
     fold = jnp.where(every8 == lax.broadcasted_iota(jnp.int32, every8.shape, 0), 1.0, 0.0)
     fold = fold.astype(BF16)
-    mark = lax.broadcasted_iota(jnp.int32, (points.shape[3], GROUP), 0).astype(F32)
-    found = []
-    for k in range(points.shape[1]):
-        group = pl.program_id(0) * points.shape[1] + k
-        count = jnp.zeros((8, GROUP), F32)
-        for q in range(8):
-            count = jnp.where(row == q, row_len[8 * group + q].astype(F32), count)
-        product = cell * count
-        lower = jnp.floor((product + 2.0) * (1.0 / lon_total))
-        start = jnp.floor((first * count + 2.0) * (1.0 / lon_total))
-        share = (product - lower * lon_total) * 0.25
-        away = mark - (lower - start)[:1]
-        mix = jnp.where(
-            away == 0.0, whole - share[:1], jnp.where(away == 1.0, share[:1], 0.0)
-        )
-        rows = points[:, k].reshape(VARS * 8, points.shape[3])
-        every = jnp.dot(rows, mix.astype(BF16), preferred_element_type=F32)
-        kept = (every.reshape(VARS, 8, GROUP) * own[None]).reshape(VARS * 8, GROUP)
-        found.append(jnp.dot(fold, kept.astype(BF16), preferred_element_type=F32))
-    values[...] = jnp.concatenate(found, 1).astype(BF16)
-    west[...] = jnp.concatenate([f[:, :STRIP] for f in found], 1).astype(BF16)
-    east[...] = jnp.concatenate([f[:, GROUP - STRIP :] for f in found], 1).astype(BF16)
+    slots = points.shape[3]
+    mark = lax.broadcasted_iota(jnp.int32, (slots, GROUP), 0).astype(F32)
+    for i, copy in enumerate(copies):
+        found = []
+        copy.wait()
+        for k in range(batch):
+            count = jnp.zeros((8, GROUP), F32)
+            for q in range(8):
+                length = row_len[8 * (batch * i + k) + q]
+                count = jnp.where(row == q, length.astype(F32), count)
+            product = cell * count
+            lower = jnp.floor((product + 2.0) * (1.0 / lon_total))
+            start = jnp.floor((first * count + 2.0) * (1.0 / lon_total))
+            share = (product - lower * lon_total) * 0.25
+            away = mark - (lower - start)[:1]
+            mix = jnp.where(
+                away == 0.0, whole - share[:1], jnp.where(away == 1.0, share[:1], 0.0)
+            )
+            rows = held[i, :, k].reshape(VARS * 8, slots)
+            every = jnp.dot(rows, mix.astype(BF16), preferred_element_type=F32)
+            kept = (every.reshape(VARS, 8, GROUP) * own[None]).reshape(VARS * 8, GROUP)
+            found.append(jnp.dot(fold, kept.astype(BF16), preferred_element_type=F32))
+        lanes = slice(batch * GROUP * i, batch * GROUP * (i + 1))
+        edge = slice(batch * STRIP * i, batch * STRIP * (i + 1))
+        values[:, lanes] = jnp.concatenate(found, 1).astype(BF16)
+        west[:, edge] = jnp.concatenate([f[:, :STRIP] for f in found], 1).astype(BF16)
+        east[:, edge] = jnp.concatenate([f[:, GROUP - STRIP :] for f in found], 1).astype(BF16)
 
 
 def regrid(points, row_len, lon_total):
     nvars, nrows, slots = points.shape
-    groups = 2
-    steps = nrows // (8 * groups)
+    batches = 2
     strips = jax.ShapeDtypeStruct((nvars, nrows * HALO), BF16)
     full = jax.ShapeDtypeStruct((nvars, nrows * COLS), BF16)
+    smem = pl.BlockSpec(memory_space=pltpu.SMEM)
+    vmem = pl.BlockSpec(memory_space=pltpu.VMEM)
     return pl.pallas_call(
         functools.partial(regrid_kernel, lon_total=lon_total),
-        grid_spec=pltpu.PrefetchScalarGridSpec(
-            num_scalar_prefetch=2,
-            grid=(steps,),
-            in_specs=[pl.BlockSpec((nvars, groups, 8, slots), lambda i, *_: (0, i, 0, 0))],
-            out_specs=[
-                pl.BlockSpec((nvars, groups * GROUP), lambda i, *_: (0, i)),
-                pl.BlockSpec((nvars, groups * STRIP), lambda i, *_: (0, i)),
-                pl.BlockSpec((nvars, groups * STRIP), lambda i, *_: (0, i)),
-            ],
-        ),
+        in_specs=[smem, smem, pl.BlockSpec(memory_space=pl.ANY)],
+        out_specs=[vmem] * 3,
         out_shape=[full, strips, strips],
+        scratch_shapes=[
+            pltpu.VMEM((batches, nvars, nrows // (8 * batches), 8, slots), BF16),
+            pltpu.SemaphoreType.DMA((batches,)),
+        ],
         name="regrid",
     )(
         row_len,
         jnp.reshape(lax.axis_index("lon"), (1,)).astype(jnp.int32),
         points.reshape(nvars, nrows // 8, 8, slots),
     )
+
+
+BAND = 288
+
+
+def bands_kernel(*refs):
+    for k, band in ((0, refs[12]), (1, refs[13])):
+        values, left, right, cot, cot_left, cot_right = (ref[...] for ref in refs[k:12:2])
+        for row in range(4):
+            edge = slice(4 * (row % 2), 4 * (row % 2) + 4)
+            whole = [cot_left[row // 2].astype(F32)[edge], cot[row].astype(F32)]
+            whole.append(cot_right[row // 2].astype(F32)[edge])
+            band[INNER * row : INNER * (row + 1)] = jnp.concatenate(whole, 0).astype(BF16)
+        edge = slice(STRIP * k, STRIP * (k + 1))
+        lanes = slice(GROUP * k, GROUP * (k + 1))
+        field = [x.astype(F32) for x in (left[:, edge], values[:, lanes], right[:, edge])]
+        field = jnp.concatenate(field, 1).astype(BF16)
+        band[128 : 128 + VARS] = field[:, :CHANS]
+        band[208 : 208 + VARS, : 8 * PITCH - CHANS] = field[:, CHANS:]
+
+
+def bands(values, left, right, cot, cot_left, cot_right):
+    def ends(array, dim, size):
+        shape = tuple(size if i == dim else n for i, n in enumerate(array.shape))
+        last = array.shape[dim] // size - 1
+
+        def spec(place):
+            index = tuple(place if i == dim else 0 for i in range(len(shape)))
+            return pl.BlockSpec(shape, lambda _: index)
+
+        return [spec(0), spec(last)]
+
+    kinds = (
+        (values, 1, 2 * GROUP), (left, 1, 2 * STRIP), (right, 1, 2 * STRIP),
+        (cot, 0, 4), (cot_left, 0, 2), (cot_right, 0, 2),
+    )
+    band = jax.ShapeDtypeStruct((BAND, CHANS), BF16)
+    full = pl.BlockSpec((BAND, CHANS), lambda _: (0, 0))
+    return pl.pallas_call(
+        bands_kernel,
+        grid=(1,),
+        in_specs=[spec for kind in kinds for spec in ends(*kind)],
+        out_specs=[full, full],
+        out_shape=[band, band],
+        name="bands",
+    )(*[kind[0] for kind in kinds for _ in (0, 1)])
 
 
 def at(row):
@@ -546,39 +603,19 @@
     return lax.ppermute(after, axis, up), lax.ppermute(before, axis, down)
 
 
-def on_device(points, row_len, w_embed, kernel1, gain1, point1, kernel2, gain2, point2, cotangent):
+def whole_step(points, row_len, w_embed, kernel1, gain1, point1, kernel2, gain2, point2, cotangent):
     lon_total = COLS * lax.axis_size("lon")
     rows_total = ROWS * lax.axis_size("lat")
+    values, west, east = regrid(jnp.swapaxes(points, 0, 1), row_len, lon_total)
+    left, right = shifted(west, east, "lon", True)
     cot_left, cot_right = shifted(
         cotangent[:, :4].reshape(ROWS // 2, 8, CHANS),
         cotangent[:, COLS - 4 :].reshape(ROWS // 2, 8, CHANS),
         "lon",
         True,
     )
-    values, west, east = regrid(jnp.swapaxes(points, 0, 1), row_len, lon_total)
-    left, right = shifted(west, east, "lon", True)
-
-    def band(rows, pairs, lanes, edge):
-        sides = [c[pairs].reshape(4, 4, CHANS) for c in (cot_left, cot_right)]
-        given = jnp.concatenate([sides[0], cotangent[rows], sides[1]], 1).reshape(-1, CHANS)
-        field = jnp.concatenate([left[:, edge], values[:, lanes], right[:, edge]], 1)
-        pieces = [field[:, :CHANS], field[:, CHANS:]]
-        pieces = [
-            jnp.pad(x, ((0, 80 - VARS), (0, CHANS - x.shape[1]))) for x in pieces
-        ]
-        return jnp.concatenate([given, *pieces], 0)
-
-    above, below = shifted(
-        band(slice(0, 4), slice(0, 2), slice(0, GROUP), slice(0, STRIP)),
-        band(
-            slice(ROWS - 4, ROWS),
-            slice(ROWS // 2 - 2, ROWS // 2),
-            slice(GROUP * (ROWS // 8 - 1), GROUP * (ROWS // 8)),
-            slice(STRIP * (ROWS // 8 - 1), STRIP * (ROWS // 8)),
-        ),
-        "lat",
-        False,
-    )
+    before, after = bands(values, left, right, cotangent, cot_left, cot_right)
+    above, below = shifted(before, after, "lat", False)
     fields = (values, left, right, above, below, cotangent, cot_left, cot_right)
     weights = (
         w_embed, kernel1, gain1.reshape(1, CHANS), point1,
@@ -603,5 +640,5 @@
     )
     out_specs = (P("lat", "lon", None), P(), P(), P(), P(), P(), P(), P())
     return jax.shard_map(
-        on_device, mesh=mesh, in_specs=in_specs, out_specs=out_specs, check_vma=False
-    )
+        whole_step, mesh=mesh, in_specs=in_specs, out_specs=out_specs, check_vma=False
+    )

time: 123 us -> 125 us (1.016)
  waiting for transfers between devices: 6.25 us -> 8.2 us
    ppermute x6, waiting for transfers between devices: 6.25 us -> 8.2 us  [shifted(): return (lax.ppermute(after, axis, up), lax.ppermute(before, axis, down))]
    slice x7 -> x1, local copies, waits for them, and re-layouts: 3 us -> 1.14 us  [whole_step(): cotangent[:, :4].reshape(ROWS // 2, 8, CHANS)]
    pallas_call x1 -> x2, Pallas kernels: 6.09 us -> 7.33 us  [the longest x1 5.53 us: regrid(): pl.pallas_call(functools.partial(regrid_kernel, lon_total=lon_total), in_...]
  transfers between devices with their start and end apart: 6 -> 6, of which waited for: 3 -> 3; matrix products, arithmetic and copies ran while one was open for 2% -> 0% of each run, Pallas kernels for 5% -> 4%
where the time goes in v5:
time: 125 us; the launch traced here: 124 us
  Pallas kernels  52.1 us (42%)
  blocking collectives  38.3 us (31%)
  starting transfers between devices  22.3 us (18%)
  waiting for transfers between devices  8.2 us (7%)
  local copies, waits for them, and re-layouts  2.65 us (2%)
    pallas_call x1, Pallas kernels, blocks(): pl.pallas_call(functools.partial(blocks_kernel, lat_devices=lat_devices),...  42.9 us
    ppermute x6, starting transfers between devices, shifted(): return (lax.ppermute(after, axis, up), lax.ppermute(before, axis, down))  22.3 us
    all_to_all x1, blocking collectives, summed(): parts = lax.all_to_all(packed, AXES, 0, 0, tiled=True)  20.4 us
    all_to_all x1, blocking collectives, summed(): lax.all_to_all(jnp.tile(mine, (devices, 1, 1, 1)), AXES, 0, 0, tiled=True)  17.9 us
    ppermute x6, waiting for transfers between devices, shifted(): return (lax.ppermute(after, axis, up), lax.ppermute(before, axis, down))  8.2 us
    pallas_call x1, Pallas kernels, regrid(): pl.pallas_call(functools.partial(regrid_kernel, lon_total=lon_total), in_...  5.53 us
  transfers between devices with their start and end apart: 6, of which 3 were waited for; matrix products, arithmetic and copies ran while one was open for 0% of the time, Pallas kernels for 4%

profile of v5, /device:TPU:1, one launch (start us, length us, event | category | flops | bytes accessed | tf_op | source)
XLA Modules:
  0.0 124.4 jit_solution(6652393669616943452)
XLA Ops:
  0.6 1.1 fusion
  1.8 2.1 %collective-permute-start.2 = (bf16[32,8,256]{2,1,0:T(8,128)(2,1)S(1)}, bf16[32,8,256]{2,1,0:T(8,128)(2,1)S(1)}, u32[]{:S(2)}, u32[]{:S(2)}) collective-permute-start(bf16[32,8,256]{2,1,0:T(8,128)(2,1)S(1)} %reshape.52), channel_id=1, source_target_pairs={{0,4},{4,8},{8,12},{12,16},{16,20},{20,24},{24,28},{28,32},{32,36}... | collective-permute-start | bytes 393224 | tf_op jit(solution)/shard_map/ppermute | solution.py:603
  4.0 6.0 %collective-permute-start.3 = (bf16[32,8,256]{2,1,0:T(8,128)(2,1)S(1)}, bf16[32,8,256]{2,1,0:T(8,128)(2,1)S(1)}, u32[]{:S(2)}, u32[]{:S(2)}) collective-permute-start(bf16[32,8,256]{2,1,0:T(8,128)(2,1)S(1)} %reshape.53), channel_id=1, source_target_pairs={{4,0},{8,4},{12,8},{16,12},{20,16},{24,20},{28,24},{32,28},{36,32}... | collective-permute-start | bytes 393224 | tf_op jit(solution)/shard_map/ppermute | solution.py:603
  10.0 5.5 %regrid.1 = (bf16[69,1536]{1,0:T(8,128)(2,1)}, bf16[69,512]{1,0:T(8,128)(2,1)}, bf16[69,512]{1,0:T(8,128)(2,1)}) custom-call(s32[64]{0:T(128)} %row_len.1, s32[1]{0:T(128)} %bitcast.1.sector, bf16[69,8,8,163]{3,2,1,0:T(8,128)(2,1)} %bitcast.9), custom_call_target="tpu_custom_call" | custom-call | tf_op jit(solution)/shard_map/regrid/pallas_call | solution.py:87
  15.5 0.1 collective-permute-start
  15.6 5.7 %collective-permute-start.1 = (bf16[69,512]{1,0:T(8,128)(2,1)}, bf16[69,512]{1,0:T(8,128)(2,1)S(1)}, u32[]{:S(2)}, u32[]{:S(2)}) collective-permute-start(bf16[69,512]{1,0:T(8,128)(2,1)} %get-tuple-element.24), channel_id=1, source_target_pairs={{4,0},{8,4},{12,8},{16,12},{20,16},{24,20},{28,24},{32,28},{36,32}... | collective-permute-start | bytes 211976 | tf_op jit(solution)/shard_map/ppermute | solution.py:603
  21.3 1.9 %collective-permute-done.refs_2_.refs_3_.left = bf16[69,512]{1,0:T(8,128)(2,1)S(1)} collective-permute-done((bf16[69,512]{1,0:T(8,128)(2,1)}, bf16[69,512]{1,0:T(8,128)(2,1)S(1)}, u32[]{:S(2)}, u32[]{:S(2)}) %collective-permute-start) | collective-permute-done | bytes 70688 | tf_op jit(solution)/shard_map/ppermute | solution.py:603
  23.2 0.0 copy-start.2
  23.2 0.0 collective-permute-done.1.refs_4_.refs_5_.right
  23.2 0.0 copy-start.3
  23.2 0.0 collective-permute-done.2.refs_8_.refs_9_.cot_left
  23.2 0.0 copy-start
  23.2 0.0 collective-permute-done.3.refs_10_.refs_11_.cot_right
  23.2 0.0 copy-start.1
  23.2 0.6 copy-done.2
  23.8 0.0 copy-done.3
  23.9 0.1 copy-done
  23.9 0.0 copy-done.1
  23.9 1.8 %bands.1 = (bf16[288,256]{1,0:T(8,128)(2,1)}, bf16[288,256]{1,0:T(8,128)(2,1)}) custom-call(bf16[69,1536]{1,0:T(8,128)(2,1)} %get-tuple-element.22.refs_0_.refs_1_.regridded, bf16[69,1536]{1,0:T(8,128)(2,1)} %get-tuple-element.22.refs_0_.refs_1_.regridded, bf16[69,512]{1,0:T(8,128)(2,1)} %copy-done.2, bf16[69,512]{1,0:T(8,128)(2,1)} %copy-done.2, ...), custom_call_target="tpu_custom_call" | custom-call | tf_op jit(solution)/shard_map/bands/pallas_call | solution.py:140
  25.7 6.5 %collective-permute-start.4 = (bf16[288,256]{1,0:T(8,128)(2,1)}, bf16[288,256]{1,0:T(8,128)(2,1)S(1)}, u32[]{:S(2)}, u32[]{:S(2)}) collective-permute-start(bf16[288,256]{1,0:T(8,128)(2,1)} %get-tuple-element.25), channel_id=1, source_target_pairs={{0,1},{1,2},{2,3},{4,5},{5,6},{6,7},{8,9},{9,10},{10,11},{12,13},{... | collective-permute-start | bytes 442376 | tf_op jit(solution)/shard_map/ppermute | solution.py:603
  32.2 1.9 %collective-permute-start.5 = (bf16[288,256]{1,0:T(8,128)(2,1)}, bf16[288,256]{1,0:T(8,128)(2,1)S(1)}, u32[]{:S(2)}, u32[]{:S(2)}) collective-permute-start(bf16[288,256]{1,0:T(8,128)(2,1)} %get-tuple-element.26), channel_id=1, source_target_pairs={{1,0},{2,1},{3,2},{5,4},{6,5},{7,6},{9,8},{10,9},{11,10},{13,12},{... | collective-permute-start | bytes 442376 | tf_op jit(solution)/shard_map/ppermute | solution.py:603
  34.2 0.5 collective-permute-done.4.above
  34.6 0.0 copy-start.4
  34.6 5.8 %collective-permute-done.5.below = bf16[288,256]{1,0:T(8,128)(2,1)S(1)} collective-permute-done((bf16[288,256]{1,0:T(8,128)(2,1)}, bf16[288,256]{1,0:T(8,128)(2,1)S(1)}, u32[]{:S(2)}, u32[]{:S(2)}) %collective-permute-start.5) | collective-permute-done | bytes 147488 | tf_op jit(solution)/shard_map/ppermute | solution.py:603
  40.4 0.0 copy-start.5
  40.4 0.0 copy-done.4
  40.4 0.7 copy-done.5
  41.1 42.9 %both_blocks.1 = (bf16[64,24,256]{2,1,0:T(8,128)(2,1)}, bf16[128,2,8,128]{3,2,1,0:T(8,128)(2,1)}) custom-call(s32[1]{0:T(128)} %bitcast.lat, bf16[69,1536]{1,0:T(8,128)(2,1)} %get-tuple-element.22.refs_0_.refs_1_.regridded, bf16[69,512]{1,0:T(8,128)(2,1)} %copy-done.2, bf16[69,512]{1,0:T(8,128)(2,1)} %copy-done.3, bf16[288,256]{1,0:T(8,128)(2,1)} %copy-done.4, ...), custom_call_target="tpu_custom_call" | custom-call | tf_op jit(solution)/shard_map/both_blocks/pallas_call | solution.py:549
  84.0 20.4 %all_to_all.10 = bf16[128,2,8,128]{3,2,1,0:T(8,128)(2,1)S(1)} all-to-all(bf16[128,2,8,128]{3,2,1,0:T(8,128)(2,1)} %get-tuple-element.28), channel_id=1, replica_groups=mesh['lon'=32,'lat'=4] {'lon','lat'}, dimensions={0} | all-to-all | bytes 1048576 | tf_op jit(solution)/shard_map/all_to_all | solution.py:587
  104.3 0.1 reduce_sum.12
  104.5 0.1 tile.2
  104.6 17.9 %all_to_all.11.packed = bf16[128,2,8,128]{3,2,1,0:T(8,128)(2,1)} all-to-all(bf16[128,2,8,128]{3,2,1,0:T(8,128)(2,1)S(1)} %tile.2), channel_id=1, replica_groups=mesh['lon'=32,'lat'=4] {'lon','lat'}, dimensions={0} | all-to-all | bytes 1048576 | tf_op jit(solution)/shard_map/all_to_all | solution.py:589
  122.5 1.9 %unpack.1 = (f32[69,256]{1,0:T(8,128)}, f32[25,256]{1,0:T(8,128)}, f32[25,256]{1,0:T(8,128)}, f32[256,256]{1,0:T(8,128)}, f32[256,256]{1,0:T(8,128)}, /*index=5*/f32[1,256]{1,0:T(1,128)}, f32[1,256]{1,0:T(1,128)}) custom-call(bf16[128,2,8,128]{3,2,1,0:T(8,128)(2,1)} %all_to_all.11.packed), custom_call_target="tpu_custom_call" | custom-call | tf_op jit(solution)/shard_map/unpack/pallas_call | solution.py:591
  (2 shorter events, 0.1 us)
Async XLA Ops:
  1.8 21.4 %collective-permute-start.2 = (bf16[32,8,256]{2,1,0:T(8,128)(2,1)S(1)}, bf16[32,8,256]{2,1,0:T(8,128)(2,1)S(1)}, u32[]{:S(2)}, u32[]{:S(2)}) collective-permute-start(bf16[32,8,256]{2,1,0:T(8,128)(2,1)S(1)} %reshape.52), channel_id=1, source_target_pairs={{0,4},{4,8},{8,12},{12,16},{16,20},{20,24},{24,28},{28,32},{32,36}... | collective-permute-start | bytes 393224 | tf_op jit(solution)/shard_map/ppermute | solution.py:603
  4.0 19.3 %collective-permute-start.3 = (bf16[32,8,256]{2,1,0:T(8,128)(2,1)S(1)}, bf16[32,8,256]{2,1,0:T(8,128)(2,1)S(1)}, u32[]{:S(2)}, u32[]{:S(2)}) collective-permute-start(bf16[32,8,256]{2,1,0:T(8,128)(2,1)S(1)} %reshape.53), channel_id=1, source_target_pairs={{4,0},{8,4},{12,8},{16,12},{20,16},{24,20},{28,24},{32,28},{36,32}... | collective-permute-start | bytes 393224 | tf_op jit(solution)/shard_map/ppermute | solution.py:603
  15.5 7.7 %collective-permute-start = (bf16[69,512]{1,0:T(8,128)(2,1)}, bf16[69,512]{1,0:T(8,128)(2,1)S(1)}, u32[]{:S(2)}, u32[]{:S(2)}) collective-permute-start(bf16[69,512]{1,0:T(8,128)(2,1)} %get-tuple-element.23), channel_id=1, source_target_pairs={{0,4},{4,8},{8,12},{12,16},{16,20},{20,24},{24,28},{28,32},{32,36}... | collective-permute-start | bytes 211976 | tf_op jit(solution)/shard_map/ppermute | solution.py:603
  15.6 7.6 %collective-permute-start.1 = (bf16[69,512]{1,0:T(8,128)(2,1)}, bf16[69,512]{1,0:T(8,128)(2,1)S(1)}, u32[]{:S(2)}, u32[]{:S(2)}) collective-permute-start(bf16[69,512]{1,0:T(8,128)(2,1)} %get-tuple-element.24), channel_id=1, source_target_pairs={{4,0},{8,4},{12,8},{16,12},{20,16},{24,20},{28,24},{32,28},{36,32}... | collective-permute-start | bytes 211976 | tf_op jit(solution)/shard_map/ppermute | solution.py:603
  23.2 0.6 copy-start.2
  23.2 0.7 copy-start.3
  23.2 0.7 copy-start
  23.2 0.7 copy-start.1
  25.7 8.9 %collective-permute-start.4 = (bf16[288,256]{1,0:T(8,128)(2,1)}, bf16[288,256]{1,0:T(8,128)(2,1)S(1)}, u32[]{:S(2)}, u32[]{:S(2)}) collective-permute-start(bf16[288,256]{1,0:T(8,128)(2,1)} %get-tuple-element.25), channel_id=1, source_target_pairs={{0,1},{1,2},{2,3},{4,5},{5,6},{6,7},{8,9},{9,10},{10,11},{12,13},{... | collective-permute-start | bytes 442376 | tf_op jit(solution)/shard_map/ppermute | solution.py:603
  32.2 8.2 %collective-permute-start.5 = (bf16[288,256]{1,0:T(8,128)(2,1)}, bf16[288,256]{1,0:T(8,128)(2,1)S(1)}, u32[]{:S(2)}, u32[]{:S(2)}) collective-permute-start(bf16[288,256]{1,0:T(8,128)(2,1)} %get-tuple-element.26), channel_id=1, source_target_pairs={{1,0},{2,1},{3,2},{5,4},{6,5},{7,6},{9,8},{10,9},{11,10},{13,12},{... | collective-permute-start | bytes 442376 | tf_op jit(solution)/shard_map/ppermute | solution.py:603
  34.6 5.8 %copy-start.4 = (bf16[288,256]{1,0:T(8,128)(2,1)}, bf16[288,256]{1,0:T(8,128)(2,1)S(1)}, u32[]{:S(2)}) copy-start(bf16[288,256]{1,0:T(8,128)(2,1)S(1)} %collective-permute-done.4.above) | copy-start | bytes 442372
  40.4 0.7 copy-start.5

commit v6 on v4

--- a/solution.py
+++ b/solution.py
@@ -28,7 +28,8 @@
 STRIP = 8 * HALO
 
 
-def regrid_kernel(row_len, sector, points, values, west, east, *, lon_total):
+def regrid_kernel(row_len, sector, points, *refs, lon_total, skipped):
+    values, west, east = refs[-3:]
     first = (sector[0] * COLS).astype(F32)
     whole = lon_total // 4
     lane = lax.broadcasted_iota(jnp.int32, (8, GROUP), 1)
@@ -42,7 +43,7 @@
     mark = lax.broadcasted_iota(jnp.int32, (points.shape[3], GROUP), 0).astype(F32)
     found = []
     for k in range(points.shape[1]):
-        group = pl.program_id(0) * points.shape[1] + k
+        group = (pl.program_id(0) + skipped) * points.shape[1] + k
         count = jnp.zeros((8, GROUP), F32)
         for q in range(8):
             count = jnp.where(row == q, row_len[8 * group + q].astype(F32), count)
@@ -63,30 +64,36 @@
     east[...] = jnp.concatenate([f[:, GROUP - STRIP :] for f in found], 1).astype(BF16)
 
 
-def regrid(points, row_len, lon_total):
+def regrid(points, row_len, lon_total, part, earlier):
     nvars, nrows, slots = points.shape
     groups = 2
-    steps = nrows // (8 * groups)
+    steps = nrows // (16 * groups)
+    skipped = steps * part
     strips = jax.ShapeDtypeStruct((nvars, nrows * HALO), BF16)
     full = jax.ShapeDtypeStruct((nvars, nrows * COLS), BF16)
     return pl.pallas_call(
-        functools.partial(regrid_kernel, lon_total=lon_total),
+        functools.partial(regrid_kernel, lon_total=lon_total, skipped=skipped),
         grid_spec=pltpu.PrefetchScalarGridSpec(
             num_scalar_prefetch=2,
             grid=(steps,),
-            in_specs=[pl.BlockSpec((nvars, groups, 8, slots), lambda i, *_: (0, i, 0, 0))],
+            in_specs=[
+                pl.BlockSpec((nvars, groups, 8, slots), lambda i, *_: (0, i + skipped, 0, 0))
+            ]
+            + [pl.BlockSpec(memory_space=pl.ANY)] * len(earlier),
             out_specs=[
-                pl.BlockSpec((nvars, groups * GROUP), lambda i, *_: (0, i)),
-                pl.BlockSpec((nvars, groups * STRIP), lambda i, *_: (0, i)),
-                pl.BlockSpec((nvars, groups * STRIP), lambda i, *_: (0, i)),
+                pl.BlockSpec((nvars, groups * GROUP), lambda i, *_: (0, i + skipped)),
+                pl.BlockSpec((nvars, groups * STRIP), lambda i, *_: (0, i + skipped)),
+                pl.BlockSpec((nvars, groups * STRIP), lambda i, *_: (0, i + skipped)),
             ],
         ),
         out_shape=[full, strips, strips],
+        input_output_aliases={3 + i: i for i in range(len(earlier))},
         name="regrid",
     )(
         row_len,
         jnp.reshape(lax.axis_index("lon"), (1,)).astype(jnp.int32),
         points.reshape(nvars, nrows // 8, 8, slots),
+        *earlier,
     )
 
 
@@ -546,16 +553,19 @@
     return lax.ppermute(after, axis, up), lax.ppermute(before, axis, down)
 
 
-def on_device(points, row_len, w_embed, kernel1, gain1, point1, kernel2, gain2, point2, cotangent):
+def whole_step(points, row_len, w_embed, kernel1, gain1, point1, kernel2, gain2, point2, cotangent):
     lon_total = COLS * lax.axis_size("lon")
     rows_total = ROWS * lax.axis_size("lat")
-    cot_left, cot_right = shifted(
-        cotangent[:, :4].reshape(ROWS // 2, 8, CHANS),
-        cotangent[:, COLS - 4 :].reshape(ROWS // 2, 8, CHANS),
-        "lon",
-        True,
-    )
-    values, west, east = regrid(jnp.swapaxes(points, 0, 1), row_len, lon_total)
+    devices = lax.axis_size("lon")
+    up = [(i, (i + 1) % devices) for i in range(devices)]
+    columns = [
+        x.reshape(ROWS // 2, 8, CHANS) for x in (cotangent[:, COLS - 4 :], cotangent[:, :4])
+    ]
+    swapped = jnp.swapaxes(points, 0, 1)
+    cot_left = lax.ppermute(columns[0], "lon", up)
+    early = regrid(swapped, row_len, lon_total, 0, ())
+    cot_right = lax.ppermute(columns[1], "lon", [(j, i) for i, j in up])
+    values, west, east = regrid(swapped, row_len, lon_total, 1, early)
     left, right = shifted(west, east, "lon", True)
 
     def band(rows, pairs, lanes, edge):
@@ -603,5 +613,5 @@
     )
     out_specs = (P("lat", "lon", None), P(), P(), P(), P(), P(), P(), P())
     return jax.shard_map(
-        on_device, mesh=mesh, in_specs=in_specs, out_specs=out_specs, check_vma=False
-    )
+        whole_step, mesh=mesh, in_specs=in_specs, out_specs=out_specs, check_vma=False
+    )

time: 123 us -> 125 us (1.016)
  Pallas kernels: 50.9 us -> 53 us
    ppermute x6 -> x4, starting transfers between devices: 22.9 us -> 14.8 us  [shifted(): return (lax.ppermute(after, axis, up), lax.ppermute(before, axis, down))]
    ppermute x0 -> x2, starting transfers between devices: none -> 8.1 us  [the longest x1 8.02 us: whole_step(): cot_right = lax.ppermute(columns[1], 'lon', [(j, i) for i, j in up])]
    pallas_call x1 -> x2, Pallas kernels: 6.09 us -> 8.16 us  [regrid(): pl.pallas_call(functools.partial(regrid_kernel, lon_total=lon_total, skip...]
    ppermute x6 -> x4, waiting for transfers between devices: 6.25 us -> 6.25 us  [shifted(): return (lax.ppermute(after, axis, up), lax.ppermute(before, axis, down))]
  transfers between devices with their start and end apart: 6 -> 6, of which waited for: 3 -> 3; matrix products, arithmetic and copies ran while one was open for 2% -> 2% of each run, Pallas kernels for 5% -> 7%
where the time goes in v6:
time: 125 us
  Pallas kernels  53 us (42%)
  blocking collectives  37.7 us (30%)
  starting transfers between devices  22.9 us (18%)
  waiting for transfers between devices  6.25 us (5%)
  local copies, waits for them, and re-layouts  3.84 us (3%)
    pallas_call x1, Pallas kernels, blocks(): pl.pallas_call(functools.partial(blocks_kernel, lat_devices=lat_devices),...  42.9 us
    all_to_all x1, blocking collectives, summed(): parts = lax.all_to_all(packed, AXES, 0, 0, tiled=True)  19.7 us
    all_to_all x1, blocking collectives, summed(): lax.all_to_all(jnp.tile(mine, (devices, 1, 1, 1)), AXES, 0, 0, tiled=True)  17.9 us
    ppermute x4, starting transfers between devices, shifted(): return (lax.ppermute(after, axis, up), lax.ppermute(before, axis, down))  14.8 us
    pallas_call x2, Pallas kernels, regrid(): pl.pallas_call(functools.partial(regrid_kernel, lon_total=lon_total, skip...  8.16 us
    ppermute x1, starting transfers between devices, whole_step(): cot_right = lax.ppermute(columns[1], 'lon', [(j, i) for i, j in up])  8.02 us
    ppermute x4, waiting for transfers between devices, shifted(): return (lax.ppermute(after, axis, up), lax.ppermute(before, axis, down))  6.25 us
  transfers between devices with their start and end apart: 6, of which 3 were waited for; matrix products, arithmetic and copies ran while one was open for 2% of the time, Pallas kernels for 7%

profile of v6, /device:TPU:1, one launch (start us, length us, event | category | flops | bytes accessed | tf_op | source)
XLA Modules:
  0.0 124.8 jit_solution(8121657770309890875)
XLA Ops:
  0.6 1.1 fusion.11
  1.8 8.0 %collective-permute-start.3 = (bf16[32,8,256]{2,1,0:T(8,128)(2,1)S(1)}, bf16[32,8,256]{2,1,0:T(8,128)(2,1)S(1)}, u32[]{:S(2)}, u32[]{:S(2)}) collective-permute-start(bf16[32,8,256]{2,1,0:T(8,128)(2,1)S(1)} %reshape.74), channel_id=1, source_target_pairs={{4,0},{8,4},{12,8},{16,12},{20,16},{24,20},{28,24},{32,28},{36,32}... | collective-permute-start | bytes 393224 | tf_op jit(solution)/shard_map/ppermute | solution.py:567
  9.9 0.1 collective-permute-start.2
  10.0 4.1 %regrid.2 = (bf16[69,1536]{1,0:T(8,128)(2,1)}, bf16[69,512]{1,0:T(8,128)(2,1)}, bf16[69,512]{1,0:T(8,128)(2,1)}) custom-call(s32[64]{0:T(128)} %row_len.3, s32[1]{0:T(128)} %bitcast.1.sector, bf16[69,8,8,163]{3,2,1,0:T(8,128)(2,1)} %bitcast.11), custom_call_target="tpu_custom_call" | custom-call | tf_op jit(solution)/shard_map/regrid/pallas_call | solution.py:74
  14.0 4.1 %regrid.3 = (bf16[69,1536]{1,0:T(8,128)(2,1)}, bf16[69,512]{1,0:T(8,128)(2,1)}, bf16[69,512]{1,0:T(8,128)(2,1)}) custom-call(s32[64]{0:T(128)} %row_len.3, s32[1]{0:T(128)} %bitcast.1.sector, bf16[69,8,8,163]{3,2,1,0:T(8,128)(2,1)} %bitcast.12, ...), custom_call_target="tpu_custom_call", output_to_operand_aliasing={{0}: (3, {}), {1}: (4, {}), {2}: (5, {})} | custom-call | tf_op jit(solution)/shard_map/regrid/pallas_call | solution.py:74
  18.1 0.0 collective-permute-start
  18.1 5.7 %collective-permute-start.1 = (bf16[69,512]{1,0:T(8,128)(2,1)}, bf16[69,512]{1,0:T(8,128)(2,1)S(1)}, u32[]{:S(2)}, u32[]{:S(2)}) collective-permute-start(bf16[69,512]{1,0:T(8,128)(2,1)} %get-tuple-element.28), channel_id=1, source_target_pairs={{4,0},{8,4},{12,8},{16,12},{20,16},{24,20},{28,24},{32,28},{36,32}... | collective-permute-start | bytes 211976 | tf_op jit(solution)/shard_map/ppermute | solution.py:553
  23.9 0.8 fusion.10
  24.7 0.9 fusion.12
  25.5 0.2 collective-permute-done.left
  25.8 0.0 copy-start.2
  25.8 0.1 fusion.15
  25.8 0.0 collective-permute-done.1.right
  25.8 0.0 copy-start.3
  25.9 0.1 fusion.16
  25.9 0.1 fusion.9
  26.0 0.1 fusion.8
  26.1 0.0 collective-permute-done.3.cot_right
  26.1 0.0 copy-start
  26.2 0.0 collective-permute-done.2.cot_left
  26.2 0.0 copy-start.1
  26.2 0.1 pad_maximum_fusion
  26.3 7.1 %collective-permute-start.4 = (bf16[288,256]{1,0:T(8,128)(2,1)S(1)}, bf16[288,256]{1,0:T(8,128)(2,1)S(1)}, u32[]{:S(2)}, u32[]{:S(2)}) collective-permute-start(bf16[288,256]{1,0:T(8,128)(2,1)S(1)} %fusion.2), channel_id=1, source_target_pairs={{0,1},{1,2},{2,3},{4,5},{5,6},{6,7},{8,9},{9,10},{10,11},{12,13},{... | collective-permute-start | bytes 442376 | tf_op jit(solution)/shard_map/ppermute | solution.py:553
  33.4 1.9 %collective-permute-start.5 = (bf16[288,256]{1,0:T(8,128)(2,1)S(1)}, bf16[288,256]{1,0:T(8,128)(2,1)S(1)}, u32[]{:S(2)}, u32[]{:S(2)}) collective-permute-start(bf16[288,256]{1,0:T(8,128)(2,1)S(1)} %fusion.3), channel_id=1, source_target_pairs={{1,0},{2,1},{3,2},{5,4},{6,5},{7,6},{9,8},{10,9},{11,10},{13,12},{... | collective-permute-start | bytes 442376 | tf_op jit(solution)/shard_map/ppermute | solution.py:553
  35.4 0.1 collective-permute-done.4.above
  35.5 0.0 copy-start.4
  35.5 5.9 %collective-permute-done.5.below = bf16[288,256]{1,0:T(8,128)(2,1)S(1)} collective-permute-done((bf16[288,256]{1,0:T(8,128)(2,1)S(1)}, bf16[288,256]{1,0:T(8,128)(2,1)S(1)}, u32[]{:S(2)}, u32[]{:S(2)}) %collective-permute-start.5) | collective-permute-done | bytes 147488 | tf_op jit(solution)/shard_map/ppermute | solution.py:553
  41.4 0.0 copy-start.5
  41.4 0.0 copy-done.2
  41.4 0.0 copy-done.3
  41.4 0.0 copy-done
  41.4 0.0 copy-done.1
  41.4 0.0 copy-done.4
  41.4 0.6 copy-done.5
  42.1 42.9 %both_blocks.1 = (bf16[64,24,256]{2,1,0:T(8,128)(2,1)}, bf16[128,2,8,128]{3,2,1,0:T(8,128)(2,1)}) custom-call(s32[1]{0:T(128)} %bitcast.lat, bf16[69,1536]{1,0:T(8,128)(2,1)} %get-tuple-element.26.regridded, bf16[69,512]{1,0:T(8,128)(2,1)} %copy-done.2, bf16[69,512]{1,0:T(8,128)(2,1)} %copy-done.3, bf16[288,256]{1,0:T(8,128)(2,1)} %copy-done.4, ...), custom_call_target="tpu_custom_call" | custom-call | tf_op jit(solution)/shard_map/both_blocks/pallas_call | solution.py:499
  85.0 19.7 %all_to_all.10 = bf16[128,2,8,128]{3,2,1,0:T(8,128)(2,1)S(1)} all-to-all(bf16[128,2,8,128]{3,2,1,0:T(8,128)(2,1)} %get-tuple-element.30), channel_id=1, replica_groups=mesh['lon'=32,'lat'=4] {'lon','lat'}, dimensions={0} | all-to-all | bytes 1048576 | tf_op jit(solution)/shard_map/all_to_all | solution.py:537
  104.7 0.1 reduce_sum.12
  104.9 0.1 tile.2
  104.9 17.9 %all_to_all.11.packed = bf16[128,2,8,128]{3,2,1,0:T(8,128)(2,1)} all-to-all(bf16[128,2,8,128]{3,2,1,0:T(8,128)(2,1)S(1)} %tile.2), channel_id=1, replica_groups=mesh['lon'=32,'lat'=4] {'lon','lat'}, dimensions={0} | all-to-all | bytes 1048576 | tf_op jit(solution)/shard_map/all_to_all | solution.py:539
  122.9 1.9 %unpack.1 = (f32[69,256]{1,0:T(8,128)}, f32[25,256]{1,0:T(8,128)}, f32[25,256]{1,0:T(8,128)}, f32[256,256]{1,0:T(8,128)}, f32[256,256]{1,0:T(8,128)}, /*index=5*/f32[1,256]{1,0:T(1,128)}, f32[1,256]{1,0:T(1,128)}) custom-call(bf16[128,2,8,128]{3,2,1,0:T(8,128)(2,1)} %all_to_all.11.packed), custom_call_target="tpu_custom_call" | custom-call | tf_op jit(solution)/shard_map/unpack/pallas_call | solution.py:541
  (10 shorter events, 0.2 us)
Async XLA Ops:
  1.8 24.3 %collective-permute-start.3 = (bf16[32,8,256]{2,1,0:T(8,128)(2,1)S(1)}, bf16[32,8,256]{2,1,0:T(8,128)(2,1)S(1)}, u32[]{:S(2)}, u32[]{:S(2)}) collective-permute-start(bf16[32,8,256]{2,1,0:T(8,128)(2,1)S(1)} %reshape.74), channel_id=1, source_target_pairs={{4,0},{8,4},{12,8},{16,12},{20,16},{24,20},{28,24},{32,28},{36,32}... | collective-permute-start | bytes 393224 | tf_op jit(solution)/shard_map/ppermute | solution.py:567
  9.9 16.3 %collective-permute-start.2 = (bf16[32,8,256]{2,1,0:T(8,128)(2,1)S(1)}, bf16[32,8,256]{2,1,0:T(8,128)(2,1)S(1)}, u32[]{:S(2)}, u32[]{:S(2)}) collective-permute-start(bf16[32,8,256]{2,1,0:T(8,128)(2,1)S(1)} %reshape.72), channel_id=1, source_target_pairs={{0,4},{4,8},{8,12},{12,16},{16,20},{20,24},{24,28},{28,32},{32,36}... | collective-permute-start | bytes 393224 | tf_op jit(solution)/shard_map/ppermute | solution.py:565
  18.1 7.6 %collective-permute-start = (bf16[69,512]{1,0:T(8,128)(2,1)}, bf16[69,512]{1,0:T(8,128)(2,1)S(1)}, u32[]{:S(2)}, u32[]{:S(2)}) collective-permute-start(bf16[69,512]{1,0:T(8,128)(2,1)} %get-tuple-element.27), channel_id=1, source_target_pairs={{0,4},{4,8},{8,12},{12,16},{16,20},{20,24},{24,28},{28,32},{32,36}... | collective-permute-start | bytes 211976 | tf_op jit(solution)/shard_map/ppermute | solution.py:553
  18.1 7.7 %collective-permute-start.1 = (bf16[69,512]{1,0:T(8,128)(2,1)}, bf16[69,512]{1,0:T(8,128)(2,1)S(1)}, u32[]{:S(2)}, u32[]{:S(2)}) collective-permute-start(bf16[69,512]{1,0:T(8,128)(2,1)} %get-tuple-element.28), channel_id=1, source_target_pairs={{4,0},{8,4},{12,8},{16,12},{20,16},{24,20},{28,24},{32,28},{36,32}... | collective-permute-start | bytes 211976 | tf_op jit(solution)/shard_map/ppermute | solution.py:553
  25.8 15.7 %copy-start.2 = (bf16[69,512]{1,0:T(8,128)(2,1)}, bf16[69,512]{1,0:T(8,128)(2,1)S(1)}, u32[]{:S(2)}) copy-start(bf16[69,512]{1,0:T(8,128)(2,1)S(1)} %collective-permute-done.left) | copy-start | bytes 211972
  25.8 15.6 %copy-start.3 = (bf16[69,512]{1,0:T(8,128)(2,1)}, bf16[69,512]{1,0:T(8,128)(2,1)S(1)}, u32[]{:S(2)}) copy-start(bf16[69,512]{1,0:T(8,128)(2,1)S(1)} %collective-permute-done.1.right) | copy-start | bytes 211972
  26.1 15.3 %copy-start = (bf16[32,8,256]{2,1,0:T(8,128)(2,1)}, bf16[32,8,256]{2,1,0:T(8,128)(2,1)S(1)}, u32[]{:S(2)}) copy-start(bf16[32,8,256]{2,1,0:T(8,128)(2,1)S(1)} %collective-permute-done.3.cot_right) | copy-start | bytes 393220
  26.2 15.3 %copy-start.1 = (bf16[32,8,256]{2,1,0:T(8,128)(2,1)}, bf16[32,8,256]{2,1,0:T(8,128)(2,1)S(1)}, u32[]{:S(2)}) copy-start(bf16[32,8,256]{2,1,0:T(8,128)(2,1)S(1)} %collective-permute-done.2.cot_left) | copy-start | bytes 393220
  26.3 9.2 %collective-permute-start.4 = (bf16[288,256]{1,0:T(8,128)(2,1)S(1)}, bf16[288,256]{1,0:T(8,128)(2,1)S(1)}, u32[]{:S(2)}, u32[]{:S(2)}) collective-permute-start(bf16[288,256]{1,0:T(8,128)(2,1)S(1)} %fusion.2), channel_id=1, source_target_pairs={{0,1},{1,2},{2,3},{4,5},{5,6},{6,7},{8,9},{9,10},{10,11},{12,13},{... | collective-permute-start | bytes 442376 | tf_op jit(solution)/shard_map/ppermute | solution.py:553
  33.4 8.0 %collective-permute-start.5 = (bf16[288,256]{1,0:T(8,128)(2,1)S(1)}, bf16[288,256]{1,0:T(8,128)(2,1)S(1)}, u32[]{:S(2)}, u32[]{:S(2)}) collective-permute-start(bf16[288,256]{1,0:T(8,128)(2,1)S(1)} %fusion.3), channel_id=1, source_target_pairs={{1,0},{2,1},{3,2},{5,4},{6,5},{7,6},{9,8},{10,9},{11,10},{13,12},{... | collective-permute-start | bytes 442376 | tf_op jit(solution)/shard_map/ppermute | solution.py:553
  35.5 5.9 %copy-start.4 = (bf16[288,256]{1,0:T(8,128)(2,1)}, bf16[288,256]{1,0:T(8,128)(2,1)S(1)}, u32[]{:S(2)}) copy-start(bf16[288,256]{1,0:T(8,128)(2,1)S(1)} %collective-permute-done.4.above) | copy-start | bytes 442372
  41.4 0.7 copy-start.5
